TPU v7x, 256 devices: a whole 4x4x8 slice. The times are simulated.
256 devices in a mesh: lat: 4 (over y), lon: 64 (over x, z, core).
Axes of the slice: x: 4, y: 4, z: 8, core: 2. Of those that a mesh axis runs over, the one named last changes fastest.
Arguments:
- grid_feat: bfloat16 [64, 2048, 1024], P('lat', 'lon'), may hold values from -40 to 40
- mesh_feat: bfloat16 [32, 1024, 1024], P('lat', 'lon'), may hold values from -40 to 40
- edges: int32 [12, 64, 2048], P(None, 'lat', 'lon'), may hold values from 0 to 32767, as said below
- edge_mask: int32 [12, 64, 2048], P(None, 'lat', 'lon'), may hold values from 0 to 1, as said below
- w_query: bfloat16 [1024, 1024], replicated, may hold values from -0.1875 to 0.1875
- w_key: bfloat16 [1024, 1024], replicated, may hold values from -0.1875 to 0.1875
- w_value: bfloat16 [1024, 1024], replicated, may hold values from -0.1875 to 0.1875
- w_out: bfloat16 [1024, 1024], replicated, may hold values from -0.1875 to 0.1875
- cotangent: bfloat16 [64, 2048, 1024], P('lat', 'lon'), may hold values from -6 to 6
Outputs:
- layer_out: bfloat16 [64, 2048, 1024], P('lat', 'lon')
- grid_grad: bfloat16 [64, 2048, 1024], P('lat', 'lon')
- mesh_grad: bfloat16 [32, 1024, 1024], P('lat', 'lon')
Inputs may be any that keep to these rules, and one draw needn't show every extreme that they name: edges[e,i,j] = r * 1024 + c names a mesh node with 0 <= r < 32, |r - i // 2| <= 4, and c within 4 of j // 2 around the circle of 1024 columns; the 12 slots of a grid point name distinct nodes, masked slots included. `edge_mask`: each grid point has 3 to 12 live slots, and they come first.
All inputs are finite; a program needn't handle non-finite values.
Results may differ from a plain program's by a relative error of at most 0.01.
The roundings to bfloat16 on the way count: a program that leaves them out, or rounds other values in their place, can miss the bound.
Values may be sent and summed in bfloat16 or wider, within the bound.
No kernel may reach another device: no remote copies, remote signals or barrier semaphores. Data moves between devices by JAX's collectives and lax.ppermute only.
A program may use at most 128 MiB of HBM per device.

v0:
```python
import math

import jax
import jax.numpy as jnp
from jax import lax
from jax.sharding import PartitionSpec as P

HEAD_COUNT = 16
EDGE_SLOTS = 12
HALO_REACH = 4


NEG_FILL = -1e30


def padded_2(block, sides, width, periodic):
    for axis, dim in sides:
        count = lax.axis_size(axis)
        forward = [(i, i + 1) for i in range(count - 1)]
        if periodic:
            forward.append((count - 1, 0))
        backward = [(target, source) for source, target in forward]
        low = lax.ppermute(
            lax.slice_in_dim(block, block.shape[dim] - width, None, axis=dim), axis, forward
        )
        high = lax.ppermute(lax.slice_in_dim(block, 0, width, axis=dim), axis, backward)
        block = jnp.concatenate([low, block, high], axis=dim)
    return block


def fetch_tile(tile):
    return padded_2(tile, (("lat", 0), ("lon", 1)), HALO_REACH, True)


def send_rims_back(padded):
    cols_inner = padded.shape[1] - 2 * HALO_REACH
    rows_inner = padded.shape[0] - 2 * HALO_REACH
    lon_rims = jnp.concatenate([padded[:, :HALO_REACH], padded[:, -HALO_REACH:]], axis=1)
    lon_back = padded_2(lon_rims, (("lon", 1),), HALO_REACH, True)
    middle = padded[:, HALO_REACH : HALO_REACH + cols_inner]
    middle = middle + jnp.pad(
        lon_back[:, :HALO_REACH], ((0, 0), (0, cols_inner - HALO_REACH), (0, 0))
    )
    middle = middle + jnp.pad(
        lon_back[:, 3 * HALO_REACH :], ((0, 0), (cols_inner - HALO_REACH, 0), (0, 0))
    )
    lat_rims = jnp.concatenate([middle[:HALO_REACH], middle[-HALO_REACH:]], axis=0)
    lat_back = padded_2(lat_rims.astype(jnp.bfloat16), (("lat", 0),), HALO_REACH, False).astype(
        lat_rims.dtype
    )
    owned = middle[HALO_REACH : HALO_REACH + rows_inner]
    owned = owned + jnp.pad(lat_back[:HALO_REACH], ((0, rows_inner - HALO_REACH), (0, 0), (0, 0)))
    owned = owned + jnp.pad(
        lat_back[3 * HALO_REACH :], ((rows_inner - HALO_REACH, 0), (0, 0), (0, 0))
    )
    return owned


def local(grid_feat, mesh_feat, edges, edge_mask, w_query, w_key, w_value, w_out, cotangent):
    grid_rows, grid_cols, width = grid_feat.shape
    mesh_rows, mesh_cols = (mesh_feat.shape[0], mesh_feat.shape[1])
    points = grid_rows * grid_cols
    head_size = width // HEAD_COUNT
    score_scale = 1.0 / math.sqrt(head_size)
    padded_rows = mesh_rows + 2 * HALO_REACH
    padded_cols = mesh_cols + 2 * HALO_REACH
    padded_count = padded_rows * padded_cols
    lon_total = mesh_cols * lax.axis_size("lon")
    w_pair = jnp.concatenate([w_key, w_value], axis=1)
    own_pair = jnp.dot(
        mesh_feat.reshape(mesh_rows * mesh_cols, width), w_pair, preferred_element_type=jnp.float32
    ).astype(jnp.bfloat16)
    padded_pair = fetch_tile(own_pair.reshape(mesh_rows, mesh_cols, 2 * width)).reshape(
        padded_count, 2 * width
    )
    key_rows = padded_pair[:, :width].reshape(padded_count, HEAD_COUNT, head_size)
    value_rows = padded_pair[:, width:].reshape(padded_count, HEAD_COUNT, head_size)
    lat_start = lax.axis_index("lat") * mesh_rows
    lon_start = lax.axis_index("lon") * mesh_cols
    targets = edges.reshape(EDGE_SLOTS, points)
    live = edge_mask.reshape(EDGE_SLOTS, points)
    target_lat = targets // lon_total - lat_start + HALO_REACH
    target_lon = jnp.mod(targets % lon_total - lon_start + HALO_REACH, lon_total)
    local_slot = target_lat * padded_cols + target_lon
    candidates = lax.broadcasted_iota(jnp.int32, (1, 1, padded_count), 2)
    linked = jnp.sum(
        jnp.where((local_slot[:, :, None] == candidates) & (live[:, :, None] > 0), 1, 0), axis=0
    )
    allowed = linked > 0
    grid_flat = grid_feat.reshape(points, width)
    queries = jnp.dot(grid_flat, w_query, preferred_element_type=jnp.float32).astype(jnp.bfloat16)
    query_heads = queries.reshape(points, HEAD_COUNT, head_size)
    scores = (
        jnp.einsum("rhd,phd->hrp", query_heads, key_rows, preferred_element_type=jnp.float32)
        * score_scale
    )
    scores = jnp.where(allowed[None], scores, NEG_FILL)
    row_max = jnp.max(scores, axis=2, keepdims=True)
    exp_scores = jnp.exp(scores - row_max)
    prob_full = exp_scores / jnp.sum(exp_scores, axis=2, keepdims=True)
    probs_half = prob_full.astype(jnp.bfloat16)
    attended = jnp.einsum(
        "hrp,phd->rhd", probs_half, value_rows, preferred_element_type=jnp.float32
    )
    attended = attended.astype(jnp.bfloat16).reshape(points, width)
    layer_out = (
        grid_flat.astype(jnp.float32) + jnp.dot(attended, w_out, preferred_element_type=jnp.float32)
    ).astype(jnp.bfloat16)
    cot_rows = cotangent.reshape(points, width)
    d_attended = jnp.dot(cot_rows, w_out.T, preferred_element_type=jnp.float32).astype(jnp.bfloat16)
    d_heads = d_attended.reshape(points, HEAD_COUNT, head_size)
    d_probs = jnp.einsum("rhd,phd->hrp", d_heads, value_rows, preferred_element_type=jnp.float32)
    centred = jnp.sum(prob_full * d_probs, axis=2, keepdims=True)
    d_scores = (prob_full * (d_probs - centred) * score_scale).astype(jnp.bfloat16)
    d_query = jnp.einsum("hrp,phd->rhd", d_scores, key_rows, preferred_element_type=jnp.float32)
    d_query = d_query.astype(jnp.bfloat16).reshape(points, width)
    grid_grad = (
        cot_rows.astype(jnp.float32)
        + jnp.dot(d_query, w_query.T, preferred_element_type=jnp.float32)
    ).astype(jnp.bfloat16)
    d_keys = jnp.einsum(
        "hrp,rhd->phd", d_scores, query_heads, preferred_element_type=jnp.float32
    ).reshape(padded_count, width)
    d_values = jnp.einsum(
        "hrp,rhd->phd", probs_half, d_heads, preferred_element_type=jnp.float32
    ).reshape(padded_count, width)
    d_pair = jnp.concatenate([d_keys, d_values], axis=1)
    owned = send_rims_back(d_pair.reshape(padded_rows, padded_cols, 2 * width)).reshape(
        mesh_rows * mesh_cols, 2 * width
    )
    owned_half = owned.astype(jnp.bfloat16)
    mesh_grad = jnp.dot(owned_half, w_pair.T, preferred_element_type=jnp.float32).astype(
        jnp.bfloat16
    )
    return (
        layer_out.reshape(grid_rows, grid_cols, width),
        grid_grad.reshape(grid_rows, grid_cols, width),
        mesh_grad.reshape(mesh_rows, mesh_cols, width),
    )


def solution(mesh):
    placed = (
        P("lat", "lon", None),
        P("lat", "lon", None),
        P(None, "lat", "lon"),
        P(None, "lat", "lon"),
        P(),
        P(),
        P(),
        P(),
        P("lat", "lon", None),
    )
    return jax.shard_map(
        local,
        mesh=mesh,
        in_specs=placed,
        out_specs=(P("lat", "lon", None), P("lat", "lon", None), P("lat", "lon", None)),
        check_vma=False,
    )
```

profile of v0, /device:TPU:8, one launch (start us, length us, event | category | flops | bytes accessed | tf_op | source)
XLA Modules:
  0.0 156.9 jit_solution(14484346672989023384)
XLA Ops:
  0.6 0.0 copy-start
  0.6 0.0 copy-start.5
  0.7 0.0 copy-start.7
  0.7 1.9 %constant_dynamic-update-slice_fusion.1 = bf16[1024,2048]{1,0:T(8,128)(2,1)S(1)} fusion(bf16[1024,1024]{1,0:T(8,128)(2,1)} %param.14), kind=kLoop, calls=%fused_computation.65 | loop fusion | bytes 4194304
  2.6 0.4 copy-done.5
  3.0 0.2 constant_dynamic-update-slice_fusion
  3.3 0.0 copy-start.1
  3.3 2.0 %copy-done.1 = bf16[1024,2048]{1,0:T(8,128)(2,1)} copy-done((bf16[1024,2048]{1,0:T(8,128)(2,1)}, bf16[1024,2048]{1,0:T(8,128)(2,1)S(1)}, u32[]{:S(2)}) %copy-start.1) | copy-done | bytes 4194328
  5.2 0.0 copy-done.7
  5.2 0.7 convolution_convert_fusion
  6.0 0.8 fusion.58
  6.8 2.2 %collective-permute-start.1 = (bf16[4,16,2048]{2,1,0:T(8,128)(2,1)}, bf16[4,16,2048]{2,1,0:T(8,128)(2,1)S(1)}, u32[]{:S(2)}, u32[]{:S(2)}) collective-permute-start(bf16[4,16,2048]{2,1,0:T(8,128)(2,1)} %bitcast.5), channel_id=1, source_target_pairs={{64,0},{128,64},{192,128},{0,192},{65,1},{129,65},{193,129},{1,193... | collective-permute-start | bytes 786440 | tf_op jit(solution)/shard_map/ppermute | solution.py:26
  9.0 0.0 collective-permute-start
  9.0 0.1 reshape.147
  9.1 0.1 gt.23
  9.2 0.1 fusion.41
  9.3 2.6 %select_reduce_fusion = s32[512,384]{1,0:T(8,128)S(1)} fusion(s32[12,512]{1,0:T(8,128)S(1)} %fusion.41, pred[12,512]{1,0:T(8,128)(4,1)S(1)} %gt.23), kind=kLoop, calls=%fused_computation.8 | loop fusion | flops 9240576 | bytes 817152 | tf_op jit(solution)/shard_map/reduce_sum | solution.py:86
  11.9 0.1 broadcast_compare_fusion
  12.0 1.0 copy.33
  12.9 4.1 %convolution_convert_fusion.2 = bf16[512,1024]{1,0:T(8,128)(2,1)} fusion(bf16[512,1024]{1,0:T(8,128)(2,1)} %bitcast.64, bf16[1024,1024]{1,0:T(8,128)(2,1)} %param.13), kind=kOutput, calls=%fused_computation.31 | convolution fusion | flops 1074266112 | bytes 4194304 | tf_op jit(solution)/shard_map/dot_general | solution.py:91
  17.1 2.3 %copy.34 = bf16[512,1024]{0,1:T(8,128)(2,1)} copy(bf16[512,1024]{1,0:T(8,128)(2,1)} %convolution_convert_fusion.2) | data formatting | bytes 2097152 | tf_op jit(solution)/shard_map/convert_element_type | solution.py:91
  19.4 0.0 collective-permute-done.1
  19.4 0.0 collective-permute-done
  19.4 1.1 pad_maximum_fusion.3
  20.4 6.8 %collective-permute-start.3 = (bf16[16,4,2048]{2,1,0:T(4,128)(2,1)}, bf16[16,4,2048]{2,1,0:T(4,128)(2,1)S(1)}, u32[]{:S(2)}, u32[]{:S(2)}) collective-permute-start(bf16[16,4,2048]{2,1,0:T(4,128)(2,1)} %get-tuple-element.12), channel_id=1, source_target_pairs={{1,0},{2,1},{3,2},{4,3},{5,4},{6,5},{7,6},{8,7},{9,8},{10,9},{11,1... | collective-permute-start | bytes 786440 | tf_op jit(solution)/shard_map/ppermute | solution.py:26
  27.2 0.0 collective-permute-start.2
  27.2 3.5 %convolution_convert_fusion.1 = bf16[512,1024]{1,0:T(8,128)(2,1)} fusion(bf16[512,1024]{1,0:T(8,128)(2,1)} %bitcast.66, bf16[1024,1024]{1,0:T(8,128)(2,1)S(1)} %copy-done), kind=kOutput, calls=%fused_computation.30 | convolution fusion | flops 1074266112 | bytes 4194304 | tf_op jit(solution)/shard_map/dot_general | solution.py:110
  30.7 2.3 %copy.37 = bf16[512,1024]{0,1:T(8,128)(2,1)} copy(bf16[512,1024]{1,0:T(8,128)(2,1)} %convolution_convert_fusion.1) | data formatting | bytes 2097152 | tf_op jit(solution)/shard_map/convert_element_type | solution.py:110
  33.0 0.0 collective-permute-done.3
  33.0 3.7 %collective-permute-done.2 = bf16[16,4,2048]{2,1,0:T(4,128)(2,1)} collective-permute-done((bf16[16,4,2048]{2,1,0:T(4,128)(2,1)}, bf16[16,4,2048]{2,1,0:T(4,128)(2,1)}, u32[]{:S(2)}, u32[]{:S(2)}) %collective-permute-start.2) | collective-permute-done | bytes 262176 | tf_op jit(solution)/shard_map/ppermute | solution.py:23
  36.7 1.7 %pad_maximum_fusion = bf16[16,24,2048]{2,1,0:T(8,128)(2,1)S(1)} fusion(bf16[16,4,2048]{2,1,0:T(4,128)(2,1)S(1)} %collective-permute-done.3, bf16[4,16,2048]{2,1,0:T(8,128)(2,1)S(1)} %collective-permute-done.1, bf16[8,16,2048]{2,1,0:T(8,128)(2,1)S(1)} %bitcast.51, bf16[4,16,2048]{2,1,0:T(8,128)(2,1)S(1)} %collective-permute-done, ...), kind=kLoop, calls=%fused_computation.26 | loop fusion | flops 7864320 | bytes 3145728 | tf_op jit(solution)/shard_map/concatenate | solution.py:27
  38.4 1.3 fusion.56
  39.7 2.4 %copy.47 = bf16[384,1024]{0,1:T(8,128)(2,1)} copy(bf16[384,1024]{1,0:T(8,128)(2,1)} %get-tuple-element.8) | data formatting | bytes 1572864
  42.1 2.3 %copy.48 = bf16[384,1024]{0,1:T(8,128)(2,1)} copy(bf16[384,1024]{1,0:T(8,128)(2,1)} %get-tuple-element.7) | data formatting | bytes 1572864
  44.4 7.5 %fusion.60 = f32[16,512,384]{1,2,0:T(8,128)} fusion(bf16[512,16,64]{0,2,1:T(8,128)(2,1)S(1)} %bitcast.53, bf16[384,16,64]{0,2,1:T(8,128)(2,1)} %bitcast.55), kind=kOutput, calls=%fused_computation.80 | convolution fusion | flops 402653184 | bytes 14417920 | tf_op jit(solution)/shard_map/rhd,phd->hrp/dot_general | solution.py:112
  51.9 10.6 %fusion.59 = (f32[16,512]{1,0:T(8,128)S(1)}, f32[16,512,384]{1,2,0:T(8,128)}) fusion(pred[512,384]{0,1:T(8,128)(4,1)S(1)} %copy-done.8, bf16[512,16,64]{0,2,1:T(8,128)(2,1)} %bitcast.58, bf16[384,16,64]{0,2,1:T(8,128)(2,1)} %bitcast.60), kind=kOutput, calls=%fused_computation.79 | convolution fusion | flops 415236480 | bytes 14647296 | tf_op jit(solution)/shard_map/sub | solution.py:99
  62.6 7.2 %fusion.21 = bf16[16,64,512]{2,1,0:T(8,128)(2,1)} fusion(bf16[384,16,64]{0,2,1:T(8,128)(2,1)} %bitcast.56, f32[16,512,384]{1,2,0:T(8,128)} %get-tuple-element.16, f32[16,512]{1,0:T(8,128)S(1)} %get-tuple-element.15), kind=kOutput, calls=%fused_computation.27 | convolution fusion | flops 409468928 | bytes 14450688 | tf_op jit(solution)/shard_map/hrp,phd->rhd/dot_general | solution.py:102
  69.7 1.6 %copy-done.15 = f32[16,512,384]{1,2,0:T(8,128)S(1)} copy-done((f32[16,512,384]{1,2,0:T(8,128)S(1)}, f32[16,512,384]{1,2,0:T(8,128)}, u32[]{:S(2)}) %copy-start.15) | copy-done | bytes 12582936
  71.3 3.2 %fusion.24 = f32[384,16,64]{0,2,1:T(8,128)} fusion(bf16[512,16,64]{0,2,1:T(8,128)(2,1)S(1)} %bitcast.54, f32[16,512,384]{1,2,0:T(8,128)S(1)} %copy-done.15, f32[16,512]{1,0:T(8,128)S(1)} %get-tuple-element.15), kind=kOutput, calls=%fused_computation.28 | convolution fusion | flops 408944640 | bytes 15237120 | tf_op jit(solution)/shard_map/hrp,rhd->phd/dot_general | solution.py:124
  74.6 18.8 %fusion.30 = f32[384,16,64]{0,2,1:T(8,128)} fusion(bf16[512,16,64]{0,2,1:T(8,128)(2,1)} %bitcast.59, f32[16,512,384]{1,2,0:T(8,128)} %fusion.60, f32[16,512,384]{1,2,0:T(8,128)} %get-tuple-element.16, f32[16,512]{1,0:T(8,128)S(1)} %get-tuple-element.15), kind=kOutput, calls=%fused_computation.32 | convolution fusion | flops 424681856 | bytes 27820032 | tf_op jit(solution)/shard_map/hrp,rhd->phd/dot_general | solution.py:121
  93.4 3.3 %copy.40 = f32[384,16,64]{2,1,0:T(8,128)} copy(f32[384,16,64]{0,2,1:T(8,128)} %fusion.30) | data formatting | bytes 3145728 | tf_op jit(solution)/shard_map/hrp,rhd->phd/transpose | solution.py:121
  96.7 3.7 %concatenate.26 = f32[16,24,1024]{2,1,0:T(8,128)} reshape(f32[384,16,64]{2,1,0:T(8,128)} %copy.40) | data formatting | bytes 3145728 | tf_op jit(solution)/shard_map/concatenate | solution.py:127
  100.4 2.8 %constant_dynamic-update-slice_fusion.3 = f32[16,24,2048]{2,1,0:T(8,128)} fusion(f32[16,24,1024]{2,1,0:T(8,128)} %concatenate.26), kind=kLoop, calls=%fused_computation.67 | loop fusion | bytes 3145728
  103.2 3.3 %copy.42 = f32[384,16,64]{2,1,0:T(8,128)} copy(f32[384,16,64]{0,2,1:T(8,128)} %fusion.24) | data formatting | bytes 3145728 | tf_op jit(solution)/shard_map/hrp,rhd->phd/transpose | solution.py:124
  106.6 3.8 %concatenate.27 = f32[16,24,1024]{2,1,0:T(8,128)} reshape(f32[384,16,64]{2,1,0:T(8,128)} %copy.42) | data formatting | bytes 3145728 | tf_op jit(solution)/shard_map/concatenate | solution.py:127
  110.4 2.8 %constant_dynamic-update-slice_fusion.2 = f32[16,24,2048]{2,1,0:T(8,128)} fusion(f32[16,24,2048]{2,1,0:T(8,128)} %constant_dynamic-update-slice_fusion.3, f32[16,24,1024]{2,1,0:T(8,128)} %concatenate.27), kind=kLoop, calls=%fused_computation.66 | loop fusion | bytes 3145728 | tf_op jit(solution)/shard_map/concatenate | solution.py:127
  113.2 2.7 %fusion.55 = (f32[16,4,2048]{2,1,0:T(4,128)}, f32[16,4,2048]{2,1,0:T(4,128)}) fusion(f32[16,24,2048]{2,1,0:T(8,128)} %constant_dynamic-update-slice_fusion.2), kind=kLoop, calls=%fused_computation.75 | loop fusion | bytes 2097152 | tf_op jit(solution)/shard_map/slice | solution.py:38
  115.9 1.4 collective-permute-start.5
  117.3 0.0 collective-permute-start.4
  117.3 18.5 %fusion.27 = bf16[16,64,512]{2,1,0:T(8,128)(2,1)} fusion(bf16[384,16,64]{0,2,1:T(8,128)(2,1)S(1)} %bitcast.61, f32[16,512,384]{1,2,0:T(8,128)} %fusion.60, f32[16,512,384]{1,2,0:T(8,128)} %get-tuple-element.16, f32[16,512]{1,0:T(8,128)S(1)} %get-tuple-element.15), kind=kOutput, calls=%fused_computation.29 | convolution fusion | flops 425206144 | bytes 27033600 | tf_op jit(solution)/shard_map/hrp,phd->rhd/dot_general | solution.py:115
  135.8 3.9 %add_convert_fusion.1 = bf16[512,1024]{1,0:T(8,128)(2,1)} fusion(bf16[512,1024]{1,0:T(8,128)(2,1)} %bitcast.65, bf16[512,1024]{0,1:T(8,128)(2,1)} %bitcast.69, bf16[1024,1024]{1,0:T(8,128)(2,1)S(1)} %copy-done), kind=kOutput, calls=%fused_computation.25 | convolution fusion | flops 1075314688 | bytes 5242880 | tf_op jit(solution)/shard_map/dot_general | solution.py:107
  139.7 0.0 collective-permute-done.5
  139.7 0.0 collective-permute-done.4
  139.7 0.0 copy-done.3
  139.7 1.8 %fusion.53 = (bf16[16,16,2048]{2,1,0:T(8,128)(2,1)S(1)}, f32[16,16,2048]{2,1,0:T(8,128)S(1)}) fusion(f32[16,4,2048]{2,1,0:T(4,128)S(1)} %collective-permute-done.5, f32[16,4,2048]{2,1,0:T(4,128)} %collective-permute-done.4, f32[16,24,2048]{2,1,0:T(8,128)S(1)} %copy-done.3), kind=kLoop, calls=%fused_computation.74 | loop fusion | flops 1572864 | bytes 6291456 | tf_op jit(solution)/shard_map/convert.2
  141.6 3.6 %collective-permute-start.7 = (bf16[4,16,2048]{2,1,0:T(8,128)(2,1)S(1)}, bf16[4,16,2048]{2,1,0:T(8,128)(2,1)S(1)}, u32[]{:S(2)}, u32[]{:S(2)}) collective-permute-start(bf16[4,16,2048]{2,1,0:T(8,128)(2,1)S(1)} %get-tuple-element.10), channel_id=1, source_target_pairs={{64,0},{128,64},{192,128},{65,1},{129,65},{193,129},{66,2},{130,66... | collective-permute-start | bytes 786440 | tf_op jit(solution)/shard_map/ppermute | solution.py:26
  145.2 2.2 %collective-permute-start.6 = (bf16[4,16,2048]{2,1,0:T(8,128)(2,1)S(1)}, bf16[4,16,2048]{2,1,0:T(8,128)(2,1)S(1)}, u32[]{:S(2)}, u32[]{:S(2)}) collective-permute-start(bf16[4,16,2048]{2,1,0:T(8,128)(2,1)S(1)} %get-tuple-element.9), channel_id=1, source_target_pairs={{0,64},{64,128},{128,192},{1,65},{65,129},{129,193},{2,66},{66,130... | collective-permute-start | bytes 786440 | tf_op jit(solution)/shard_map/ppermute | solution.py:23
  147.5 2.3 %add_convert_fusion = bf16[512,1024]{1,0:T(8,128)(2,1)} fusion(bf16[512,1024]{1,0:T(8,128)(2,1)S(1)} %bitcast.67, bf16[512,1024]{0,1:T(8,128)(2,1)S(1)} %bitcast.70, bf16[1024,1024]{1,0:T(8,128)(2,1)S(1)} %copy-done.12), kind=kOutput, calls=%fused_computation.24 | convolution fusion | flops 1075314688 | bytes 5242880 | tf_op jit(solution)/shard_map/dot_general | solution.py:119
  149.8 1.0 collective-permute-done.7
  150.8 3.4 %collective-permute-done.6 = bf16[4,16,2048]{2,1,0:T(8,128)(2,1)S(1)} collective-permute-done((bf16[4,16,2048]{2,1,0:T(8,128)(2,1)S(1)}, bf16[4,16,2048]{2,1,0:T(8,128)(2,1)S(1)}, u32[]{:S(2)}, u32[]{:S(2)}) %collective-permute-start.6) | collective-permute-done | bytes 262176 | tf_op jit(solution)/shard_map/ppermute | solution.py:23
  154.2 0.2 maximum_convert_fusion
  154.4 0.2 fusion.37
  154.6 0.0 copy-done.2
  154.7 2.2 %convolution_convert_fusion.3 = bf16[128,1024]{1,0:T(8,128)(2,1)} fusion(bf16[128,2048]{1,0:T(8,128)(2,1)S(1)} %bitcast.57, bf16[1024,2048]{1,0:T(8,128)(2,1)S(1)} %copy-done.2), kind=kOutput, calls=%fused_computation.34 | convolution fusion | flops 537001984 | bytes 4980736 | tf_op jit(solution)/shard_map/dot_general | solution.py:132
  (25 shorter events, 0.1 us)
Async XLA Ops:
  0.6 26.6 %copy-start = (bf16[1024,1024]{1,0:T(8,128)(2,1)S(1)}, bf16[1024,1024]{1,0:T(8,128)(2,1)}, u32[]{:S(2)}) copy-start(bf16[1024,1024]{1,0:T(8,128)(2,1)} %param.16) | copy-start | bytes 6291460
  0.6 2.4 %copy-start.5 = (bf16[1024,1024]{1,0:T(8,128)(2,1)S(1)}, bf16[1024,1024]{1,0:T(8,128)(2,1)}, u32[]{:S(2)}) copy-start(bf16[1024,1024]{1,0:T(8,128)(2,1)} %param.15) | copy-start | bytes 6291460
  0.7 4.6 %copy-start.7 = (bf16[8,16,1024]{2,1,0:T(8,128)(2,1)S(1)}, bf16[8,16,1024]{2,1,0:T(8,128)(2,1)}, u32[]{:S(2)}) copy-start(bf16[8,16,1024]{2,1,0:T(8,128)(2,1)} %param.10) | copy-start | bytes 786436
  3.0 5.9 %copy-start.9 = (s32[12,16,32]{2,1,0:T(8,128)S(1)}, s32[12,16,32]{2,1,0:T(8,128)}, u32[]{:S(2)}) copy-start(s32[12,16,32]{2,1,0:T(8,128)} %param.11) | copy-start | bytes 73732
  3.0 6.0 %copy-start.10 = (s32[12,16,32]{2,1,0:T(8,128)S(1)}, s32[12,16,32]{2,1,0:T(8,128)}, u32[]{:S(2)}) copy-start(s32[12,16,32]{2,1,0:T(8,128)} %param.12) | copy-start | bytes 73732
  3.3 2.0 %copy-start.1 = (bf16[1024,2048]{1,0:T(8,128)(2,1)}, bf16[1024,2048]{1,0:T(8,128)(2,1)S(1)}, u32[]{:S(2)}) copy-start(bf16[1024,2048]{1,0:T(8,128)(2,1)S(1)} %constant_dynamic-update-slice_fusion) | copy-start | bytes 12582916
  6.8 12.6 %collective-permute-start.1 = (bf16[4,16,2048]{2,1,0:T(8,128)(2,1)}, bf16[4,16,2048]{2,1,0:T(8,128)(2,1)S(1)}, u32[]{:S(2)}, u32[]{:S(2)}) collective-permute-start(bf16[4,16,2048]{2,1,0:T(8,128)(2,1)} %bitcast.5), channel_id=1, source_target_pairs={{64,0},{128,64},{192,128},{0,192},{65,1},{129,65},{193,129},{1,193... | collective-permute-start | bytes 786440 | tf_op jit(solution)/shard_map/ppermute | solution.py:26
  9.0 10.4 %collective-permute-start = (bf16[4,16,2048]{2,1,0:T(8,128)(2,1)}, bf16[4,16,2048]{2,1,0:T(8,128)(2,1)S(1)}, u32[]{:S(2)}, u32[]{:S(2)}) collective-permute-start(bf16[4,16,2048]{2,1,0:T(8,128)(2,1)} %bitcast.3), channel_id=1, source_target_pairs={{0,64},{64,128},{128,192},{192,0},{1,65},{65,129},{129,193},{193,1... | collective-permute-start | bytes 786440 | tf_op jit(solution)/shard_map/ppermute | solution.py:23
  20.4 12.6 %collective-permute-start.3 = (bf16[16,4,2048]{2,1,0:T(4,128)(2,1)}, bf16[16,4,2048]{2,1,0:T(4,128)(2,1)S(1)}, u32[]{:S(2)}, u32[]{:S(2)}) collective-permute-start(bf16[16,4,2048]{2,1,0:T(4,128)(2,1)} %get-tuple-element.12), channel_id=1, source_target_pairs={{1,0},{2,1},{3,2},{4,3},{5,4},{6,5},{7,6},{8,7},{9,8},{10,9},{11,1... | collective-permute-start | bytes 786440 | tf_op jit(solution)/shard_map/ppermute | solution.py:26
  27.2 9.4 %collective-permute-start.2 = (bf16[16,4,2048]{2,1,0:T(4,128)(2,1)}, bf16[16,4,2048]{2,1,0:T(4,128)(2,1)}, u32[]{:S(2)}, u32[]{:S(2)}) collective-permute-start(bf16[16,4,2048]{2,1,0:T(4,128)(2,1)} %get-tuple-element.11), channel_id=1, source_target_pairs={{0,1},{1,2},{2,3},{3,4},{4,5},{5,6},{6,7},{7,8},{8,9},{9,10},{10,1... | collective-permute-start | bytes 786440 | tf_op jit(solution)/shard_map/ppermute | solution.py:23
  38.4 6.0 %copy-start.4 = (bf16[512,1024]{0,1:T(8,128)(2,1)S(1)}, bf16[512,1024]{0,1:T(8,128)(2,1)}, u32[]{:S(2)}) copy-start(bf16[512,1024]{0,1:T(8,128)(2,1)} %copy.37) | copy-start | bytes 3145732
  44.4 7.5 %copy-start.8 = (pred[512,384]{0,1:T(8,128)(4,1)S(1)}, pred[512,384]{0,1:T(8,128)(4,1)}, u32[]{:S(2)}) copy-start(pred[512,384]{0,1:T(8,128)(4,1)} %copy.33) | copy-start | bytes 589828
  62.6 8.8 %copy-start.15 = (f32[16,512,384]{1,2,0:T(8,128)S(1)}, f32[16,512,384]{1,2,0:T(8,128)}, u32[]{:S(2)}) copy-start(f32[16,512,384]{1,2,0:T(8,128)} %get-tuple-element.16) | copy-start | bytes 37748740
  106.6 10.7 %copy-start.6 = (bf16[384,1024]{0,1:T(8,128)(2,1)S(1)}, bf16[384,1024]{0,1:T(8,128)(2,1)}, u32[]{:S(2)}) copy-start(bf16[384,1024]{0,1:T(8,128)(2,1)} %copy.48) | copy-start | bytes 2359300
  115.9 23.8 %collective-permute-start.5 = (f32[16,4,2048]{2,1,0:T(4,128)}, f32[16,4,2048]{2,1,0:T(4,128)S(1)}, u32[]{:S(2)}, u32[]{:S(2)}) collective-permute-start(f32[16,4,2048]{2,1,0:T(4,128)} %get-tuple-element.6), channel_id=1, source_target_pairs={{1,0},{2,1},{3,2},{4,3},{5,4},{6,5},{7,6},{8,7},{9,8},{10,9},{11,1... | collective-permute-start | bytes 1572872 | tf_op jit(solution)/shard_map/ppermute | solution.py:26
  117.3 22.4 %collective-permute-start.4 = (f32[16,4,2048]{2,1,0:T(4,128)}, f32[16,4,2048]{2,1,0:T(4,128)}, u32[]{:S(2)}, u32[]{:S(2)}) collective-permute-start(f32[16,4,2048]{2,1,0:T(4,128)} %get-tuple-element.5), channel_id=1, source_target_pairs={{0,1},{1,2},{2,3},{3,4},{4,5},{5,6},{6,7},{7,8},{8,9},{9,10},{10,1... | collective-permute-start | bytes 1572872 | tf_op jit(solution)/shard_map/ppermute | solution.py:23
  135.8 4.0 %copy-start.3 = (f32[16,24,2048]{2,1,0:T(8,128)S(1)}, f32[16,24,2048]{2,1,0:T(8,128)}, u32[]{:S(2)}) copy-start(f32[16,24,2048]{2,1,0:T(8,128)} %constant_dynamic-update-slice_fusion.2) | copy-start | bytes 9437188
  139.7 7.7 %copy-start.12 = (bf16[1024,1024]{1,0:T(8,128)(2,1)S(1)}, bf16[1024,1024]{1,0:T(8,128)(2,1)}, u32[]{:S(2)}) copy-start(bf16[1024,1024]{1,0:T(8,128)(2,1)} %param.13) | copy-start | bytes 6291460
  139.7 7.8 %copy-start.13 = (bf16[16,32,1024]{2,1,0:T(8,128)(2,1)S(1)}, bf16[16,32,1024]{2,1,0:T(8,128)(2,1)}, u32[]{:S(2)}) copy-start(bf16[16,32,1024]{2,1,0:T(8,128)(2,1)} %param.17) | copy-start | bytes 3145732
  139.7 7.8 %copy-start.14 = (bf16[16,64,512]{2,1,0:T(8,128)(2,1)S(1)}, bf16[16,64,512]{2,1,0:T(8,128)(2,1)}, u32[]{:S(2)}) copy-start(bf16[16,64,512]{2,1,0:T(8,128)(2,1)} %fusion.27) | copy-start | bytes 3145732
  141.6 9.2 %collective-permute-start.7 = (bf16[4,16,2048]{2,1,0:T(8,128)(2,1)S(1)}, bf16[4,16,2048]{2,1,0:T(8,128)(2,1)S(1)}, u32[]{:S(2)}, u32[]{:S(2)}) collective-permute-start(bf16[4,16,2048]{2,1,0:T(8,128)(2,1)S(1)} %get-tuple-element.10), channel_id=1, source_target_pairs={{64,0},{128,64},{192,128},{65,1},{129,65},{193,129},{66,2},{130,66... | collective-permute-start | bytes 786440 | tf_op jit(solution)/shard_map/ppermute | solution.py:26
  145.2 8.9 %collective-permute-start.6 = (bf16[4,16,2048]{2,1,0:T(8,128)(2,1)S(1)}, bf16[4,16,2048]{2,1,0:T(8,128)(2,1)S(1)}, u32[]{:S(2)}, u32[]{:S(2)}) collective-permute-start(bf16[4,16,2048]{2,1,0:T(8,128)(2,1)S(1)} %get-tuple-element.9), channel_id=1, source_target_pairs={{0,64},{64,128},{128,192},{1,65},{65,129},{129,193},{2,66},{66,130... | collective-permute-start | bytes 786440 | tf_op jit(solution)/shard_map/ppermute | solution.py:23
  149.8 4.6 %copy-start.11 = (pred[8]{0:T(512)(128)(4,1)S(1)}, pred[8]{0:T(512)(128)(4,1)}, u32[]{:S(2)}) copy-start(pred[8]{0:T(512)(128)(4,1)} %constant.64.clone.1) | copy-start | bytes 28
  149.8 4.9 %copy-start.2 = (bf16[1024,2048]{1,0:T(8,128)(2,1)S(1)}, bf16[1024,2048]{1,0:T(8,128)(2,1)}, u32[]{:S(2)}) copy-start(bf16[1024,2048]{1,0:T(8,128)(2,1)} %copy-done.1) | copy-start | bytes 12582916
where the time goes:
time: 158 us; the launch traced here: 157 us
  matrix products  82.6 us (52%)
  local copies, waits for them, and re-layouts  41.3 us (26%)
  starting transfers between devices  16.2 us (10%)
  waiting for transfers between devices  8.08 us (5%)
  other arithmetic  7.8 us (5%)
    dot_general x1, matrix products, local(): jnp.einsum('hrp,rhd->phd', d_scores, query_heads, preferred_element_type=...  18.8 us
    dot_general x1, matrix products, local(): jnp.einsum('hrp,phd->rhd', d_scores, key_rows, preferred_element_type=jnp...  18.5 us
    ppermute x4, starting transfers between devices, padded_2(): lax.ppermute(lax.slice_in_dim(block, 0, width, axis=dim), axis, backward)  14 us
    unnamed x36, local copies, waits for them, and re-layouts  13.5 us
    sub x1, matrix products, local(): exp_scores = jnp.exp(scores - row_max)  10.6 us
    concatenate x3, local copies, waits for them, and re-layouts, local(): d_pair = jnp.concatenate([d_keys, d_values], axis=1)  10.3 us
    dot_general x1, matrix products, local(): jnp.einsum('rhd,phd->hrp', d_heads, value_rows, preferred_element_type=jn...  7.53 us
    dot_general x1, matrix products, local(): jnp.einsum('hrp,phd->rhd', probs_half, value_rows, preferred_element_type...  7.17 us
  transfers between devices with their start and end apart: 8, of which 3 were waited for; matrix products, arithmetic and copies ran while one was open for 26% of the time, Pallas kernels for 0%

commit v1 on v0

v1 whole, which is shorter than its diff:
```python
import functools

import jax
import jax.numpy as jnp
from jax import lax
from jax.experimental import pallas as pl
from jax.experimental.pallas import tpu as pltpu
from jax.sharding import PartitionSpec as P

HEADS = 16
HEAD = 64
SLOTS = 12
REACH = 4
NEG_FILL = -1e30
SCALE = 0.125
GROUP = 4
WIDE = GROUP * HEAD

BF = jnp.bfloat16
F32 = jnp.float32
NT = (((1,), (1,)), ((), ()))
NN = (((1,), (0,)), ((), ()))
TN = (((0,), (0,)), ((), ()))


def mm(a, b, dims):
    return lax.dot_general(a, b, dims, preferred_element_type=F32)


TILES = 4
POINTS = 128
RUNS = 4
RUN = 48
NODES = RUNS * RUN
ALL_NODES = 384


def project_kernel(x_ref, c_ref, wq_ref, wo_ref, q_ref, da_ref):
    for t in range(TILES):
        tr, tc = t // 2, t % 2
        rows = pl.ds(t * POINTS, POINTS)
        x = x_ref[tr, :, tc].reshape(POINTS, x_ref.shape[-1])
        q = mm(x, wq_ref[...], NN).astype(BF)
        q_ref[rows, :] = q * SCALE
        c = c_ref[tr, :, tc].reshape(POINTS, c_ref.shape[-1])
        d = mm(c, wo_ref[...], NT).astype(BF)
        da_ref[rows, :] = d * SCALE


def project(x5, c5, w_query, w_out):
    width = x5.shape[-1]
    points = TILES * POINTS
    cols = 256
    whole5 = pl.BlockSpec(x5.shape, lambda j: (0, 0, 0, 0, 0))
    out = pl.BlockSpec((points, cols), lambda j: (0, j))
    return pl.pallas_call(
        project_kernel,
        grid=(width // cols,),
        in_specs=[
            whole5,
            whole5,
            pl.BlockSpec((width, cols), lambda j: (0, j)),
            pl.BlockSpec((cols, width), lambda j: (j, 0)),
        ],
        out_specs=[out, out],
        out_shape=[jax.ShapeDtypeStruct((points, width), BF)] * 2,
        cost_estimate=pl.CostEstimate(
            flops=4 * points * width * width, bytes_accessed=8 << 20, transcendentals=0
        ),
        name="project",
    )(x5, c5, w_query, w_out)


def attend_kernel(
    mesh_ref, wk_ref, wv_ref, q_ref, da_ref, slot_ref, att_ref, dq_ref, part_ref,
    k_scr, v_scr, dk_scr, dv_scr, bias_scr, pw_scr, sw_scr, pt_scr, st_scr,
):
    k_scr[...] = mm(mesh_ref[...], wk_ref[...], NN).astype(BF)
    v_scr[...] = mm(mesh_ref[...], wv_ref[...], NN).astype(BF)
    dk_scr[...] = jnp.zeros_like(dk_scr)
    dv_scr[...] = jnp.zeros_like(dv_scr)
    head_of_lane = lax.broadcasted_iota(jnp.int32, (1, WIDE), 1) // HEAD
    node = lax.broadcasted_iota(jnp.int32, (NODES, POINTS), 0)

    def tile(t, carry):
        tr, tc = t // 2, t % 2
        base = pl.multiple_of(tc * 128 + tr * 16, 16)
        runs = [pl.ds(pl.multiple_of(base + k * 64, 16), RUN) for k in range(RUNS)]
        rows = pl.ds(pl.multiple_of(t * POINTS, POINTS), POINTS)
        slots = slot_ref[t]
        hit = node == slots[0:1]
        for e in range(1, SLOTS):
            hit = hit | (node == slots[e : e + 1])
        bias_scr[...] = jnp.where(hit, 0.0, NEG_FILL)

        def take(ref, lanes):
            return jnp.concatenate([ref[r, lanes] for r in runs], axis=0)

        def spread(block):
            return jnp.concatenate(
                [jnp.where(head_of_lane == h, block, jnp.zeros_like(block)) for h in range(GROUP)],
                axis=0,
            )

        for g in range(HEADS // GROUP):
            lanes = pl.ds(g * WIDE, WIDE)
            keys = take(k_scr, lanes)
            values = take(v_scr, lanes)
            queries = spread(q_ref[rows, lanes])
            grads = spread(da_ref[rows, lanes])
            scores = mm(keys, queries, NT)
            d_probs = mm(values, grads, NT)
            for h in range(GROUP):
                at = slice(h * POINTS, (h + 1) * POINTS)
                s = scores[:, at] + bias_scr[...]
                e = jnp.exp(s - jnp.max(s, axis=0, keepdims=True))
                p = e * (1.0 / jnp.sum(e, axis=0, keepdims=True))
                half = p.astype(BF)
                dp = d_probs[:, at]
                centred = jnp.sum(p * dp, axis=0, keepdims=True)
                ds = (p * (dp - centred)).astype(BF)
                pw_scr[:, at] = half
                sw_scr[:, at] = ds
                tall = slice(h * NODES, (h + 1) * NODES)
                pt_scr[tall, :] = half
                st_scr[tall, :] = ds
            att_ref[rows, lanes] = mm(pt_scr[...], spread(values), TN).astype(BF)
            dq_ref[rows, lanes] = mm(st_scr[...], spread(keys), TN).astype(BF)
            dk = mm(sw_scr[...], queries, NN)
            dv = mm(pw_scr[...], grads, NN)
            for k in range(RUNS):
                part = slice(k * RUN, (k + 1) * RUN)
                dk_scr[runs[k], lanes] += dk[part]
                dv_scr[runs[k], lanes] += dv[part]
        return carry

    lax.fori_loop(0, TILES, tile, 0)
    part_ref[...] = (
        mm((dk_scr[...] * (1.0 / SCALE)).astype(BF), wk_ref[...], NT)
        + mm((dv_scr[...] * (1.0 / SCALE)).astype(BF), wv_ref[...], NT)
    ).astype(part_ref.dtype)


def attend(nodes, w_key, w_value, q, da, slots):
    width = q.shape[1]
    points = q.shape[0]
    return pl.pallas_call(
        attend_kernel,
        in_specs=[pl.BlockSpec(memory_space=pltpu.VMEM)] * 6,
        out_specs=[pl.BlockSpec(memory_space=pltpu.VMEM)] * 3,
        out_shape=[
            jax.ShapeDtypeStruct((points, width), BF),
            jax.ShapeDtypeStruct((points, width), BF),
            jax.ShapeDtypeStruct((ALL_NODES, width), F32),
        ],
        scratch_shapes=[
            pltpu.VMEM((ALL_NODES, width), BF),
            pltpu.VMEM((ALL_NODES, width), BF),
            pltpu.VMEM((ALL_NODES, width), F32),
            pltpu.VMEM((ALL_NODES, width), F32),
            pltpu.VMEM((NODES, POINTS), F32),
            pltpu.VMEM((NODES, GROUP * POINTS), BF),
            pltpu.VMEM((NODES, GROUP * POINTS), BF),
            pltpu.VMEM((GROUP * NODES, POINTS), BF),
            pltpu.VMEM((GROUP * NODES, POINTS), BF),
        ],
        cost_estimate=pl.CostEstimate(
            flops=12 * 10**9, bytes_accessed=10 << 20, transcendentals=2 * 10**6
        ),
        name="attend",
    )(nodes, w_key, w_value, q, da, slots)


def outputs_kernel(x_ref, c_ref, att_ref, dq_ref, wo_ref, wq_ref, out_ref, grad_ref):
    for t in range(TILES):
        tr, tc = t // 2, t % 2
        rows = pl.ds(t * POINTS, POINTS)
        shape = (8, 16, out_ref.shape[-1])
        a = mm(att_ref[rows, :], wo_ref[...], NN).reshape(shape)
        out_ref[tr, :, tc] = (x_ref[tr, :, tc].astype(F32) + a).astype(BF)
        b = mm(dq_ref[rows, :], wq_ref[...], NT).reshape(shape)
        grad_ref[tr, :, tc] = (c_ref[tr, :, tc].astype(F32) + b).astype(BF)


def outputs(x5, c5, att, dq, w_out, w_query):
    width = x5.shape[-1]
    points = TILES * POINTS
    cols = 256
    whole = pl.BlockSpec((points, width), lambda j: (0, 0))
    block5 = pl.BlockSpec(x5.shape[:-1] + (cols,), lambda j: (0, 0, 0, 0, j))
    return pl.pallas_call(
        outputs_kernel,
        grid=(width // cols,),
        in_specs=[
            block5,
            block5,
            whole,
            whole,
            pl.BlockSpec((width, cols), lambda j: (0, j)),
            pl.BlockSpec((cols, width), lambda j: (j, 0)),
        ],
        out_specs=[block5, block5],
        out_shape=[jax.ShapeDtypeStruct(x5.shape, BF)] * 2,
        cost_estimate=pl.CostEstimate(
            flops=4 * points * width * width, bytes_accessed=10 << 20, transcendentals=0
        ),
        name="outputs",
    )(x5, c5, att, dq, w_out, w_query)


def shift(piece, d_lat, d_lon):
    lats, lons = lax.axis_size("lat"), lax.axis_size("lon")
    pairs = [
        (a * lons + o, (a + d_lat) * lons + (o + d_lon) % lons)
        for a in range(lats)
        for o in range(lons)
        if 0 <= a + d_lat < lats
    ]
    return lax.ppermute(piece, ("lat", "lon"), pairs)


def local(grid_feat, mesh_feat, edges, edge_mask, w_query, w_key, w_value, w_out, cotangent):
    width = grid_feat.shape[-1]
    mesh_rows, mesh_cols = mesh_feat.shape[:2]
    lon_total = mesh_cols * lax.axis_size("lon")
    x5 = grid_feat.reshape(2, 8, 2, 16, width)
    c5 = cotangent.reshape(2, 8, 2, 16, width)

    own = mesh_feat.reshape(2, 4, 4, 4, width).transpose(2, 0, 1, 3, 4).reshape(4, 2, 16, width)
    from_low = shift(own[:, 1], 1, 0)
    from_high = shift(own[:, 0], -1, 0)
    from_left = shift(own[3], 0, 1)
    from_right = shift(own[0], 0, -1)
    low_left = shift(own[3, 1], 1, 1)
    low_right = shift(own[0, 1], 1, -1)
    high_left = shift(own[3, 0], -1, 1)
    high_right = shift(own[0, 0], -1, -1)

    q, da = project(x5, c5, w_query, w_out)

    lat_start = lax.axis_index("lat") * mesh_rows
    lon_start = lax.axis_index("lon") * mesh_cols
    row = edges // lon_total - lat_start + REACH
    col = jnp.mod(edges % lon_total - lon_start + REACH, lon_total)
    tile_row = lax.broadcasted_iota(jnp.int32, edges.shape, 1) // 8
    tile_col = lax.broadcasted_iota(jnp.int32, edges.shape, 2) // 16
    slot = (
        (col // 4 - 2 * tile_col) * RUN
        + (row // 4 - tile_row) * 16
        + (row % 4) * 4
        + col % 4
    )
    slot = jnp.where(edge_mask > 0, slot, -1)
    slot = slot.reshape(SLOTS, 2, 8, 2, 16).transpose(1, 3, 0, 2, 4).reshape(TILES, SLOTS, POINTS)

    middle = jnp.concatenate([from_low[:, None], own, from_high[:, None]], axis=1)
    left = jnp.concatenate([low_left[None], from_left, high_left[None]], axis=0)
    right = jnp.concatenate([low_right[None], from_right, high_right[None]], axis=0)
    nodes = jnp.concatenate([left[None], middle, right[None]], axis=0).reshape(ALL_NODES, width)

    att, dq, part = attend(nodes, w_key, w_value, q, da, slot)

    part = part.reshape(6, 4, 16, width)
    sent = part.astype(BF)
    to_low = shift(sent[1:5, 0], -1, 0)
    to_high = shift(sent[1:5, 3], 1, 0)
    to_left = shift(sent[0, 1:3], 0, -1)
    to_right = shift(sent[5, 1:3], 0, 1)
    to_low_left = shift(sent[0, 0], -1, -1)
    to_low_right = shift(sent[5, 0], -1, 1)
    to_high_left = shift(sent[0, 3], 1, -1)
    to_high_right = shift(sent[5, 3], 1, 1)

    layer_out, grid_grad = outputs(x5, c5, att, dq, w_out, w_query)

    total = part[1:5, 1:3]
    total = total.at[:, 1].add(to_low.astype(F32))
    total = total.at[:, 0].add(to_high.astype(F32))
    total = total.at[3].add(to_left.astype(F32))
    total = total.at[0].add(to_right.astype(F32))
    total = total.at[3, 1].add(to_low_left.astype(F32))
    total = total.at[0, 1].add(to_low_right.astype(F32))
    total = total.at[3, 0].add(to_high_left.astype(F32))
    total = total.at[0, 0].add(to_high_right.astype(F32))
    mesh_grad = (
        total.astype(BF)
        .reshape(4, 2, 4, 4, width)
        .transpose(1, 2, 0, 3, 4)
        .reshape(mesh_rows, mesh_cols, width)
    )
    return layer_out.reshape(grid_feat.shape), grid_grad.reshape(grid_feat.shape), mesh_grad


def solution(mesh):
    tiled = P("lat", "lon", None)
    placed = (tiled, tiled, P(None, "lat", "lon"), P(None, "lat", "lon")) + (P(),) * 4 + (tiled,)
    return jax.shard_map(
        local, mesh=mesh, in_specs=placed, out_specs=(tiled, tiled, tiled), check_vma=False
    )
```

time: 158 us -> 104 us (0.66)
  matrix products: 82.6 us -> 0 us
  local copies, waits for them, and re-layouts: 41.3 us -> 4.21 us
  Pallas kernels: 0 us -> 34.2 us
  starting transfers between devices: 16.2 us -> 49.7 us
  other arithmetic: 7.8 us -> 4.53 us
    dot_general x11 -> x0, matrix products: 72 us -> none  [the longest x1 18.8 us: local(): jnp.einsum('hrp,rhd->phd', d_scores, query_heads, preferred_element_type=...]
    pallas_call x0 -> x3, Pallas kernels: none -> 34.2 us  [the longest x1 19 us: attend(): pl.pallas_call(attend_kernel, in_specs=[pl.BlockSpec(memory_space=pltpu.V...]
    ppermute x8 -> x16, starting transfers between devices: 16.2 us -> 49.7 us  [shift(): return lax.ppermute(piece, ('lat', 'lon'), pairs)]
    unnamed x36 -> x6, local copies, waits for them, and re-layouts: 13.5 us -> 0.25 us
    sub x1 -> x0, matrix products: 10.6 us -> none  [local(): exp_scores = jnp.exp(scores - row_max)]
    concatenate x4 -> x0, local copies, waits for them, and re-layouts: 10.5 us -> none  [the longest x3 10.3 us: local(): d_pair = jnp.concatenate([d_keys, d_values], axis=1)]
    transpose x2 -> x1, local copies, waits for them, and re-layouts: 6.64 us -> 0.1 us  [local(): mesh_feat.reshape(2, 4, 4, 4, width).transpose(2, 0, 1, 3, 4)]
    slice x4 -> x2, local copies, waits for them, and re-layouts: 4.92 us -> 0.09 us  [the longest x1 0.05 us: local(): from_left = shift(own[3], 0, 1)]
  transfers between devices with their start and end apart: 8 -> 16, of which waited for: 3 -> 3; matrix products, arithmetic and copies ran while one was open for 26% -> 3% of each run, Pallas kernels for 0% -> 15%
where the time goes in v1:
time: 104 us; the launch traced here: 103 us
  starting transfers between devices  49.7 us (48%)
  Pallas kernels  34.2 us (33%)
  waiting for transfers between devices  8.98 us (9%)
  other arithmetic  4.53 us (4%)
  local copies, waits for them, and re-layouts  4.21 us (4%)
  between operations  1.1 us (1%)
    ppermute x16, starting transfers between devices, shift(): return lax.ppermute(piece, ('lat', 'lon'), pairs)  49.7 us
    pallas_call x1, Pallas kernels, attend(): pl.pallas_call(attend_kernel, in_specs=[pl.BlockSpec(memory_space=pltpu.V...  19 us
    ppermute x16, waiting for transfers between devices, shift(): return lax.ppermute(piece, ('lat', 'lon'), pairs)  8.98 us
    pallas_call x1, Pallas kernels, outputs(): pl.pallas_call(outputs_kernel, grid=(width // cols,), in_specs=[block5, b...  7.83 us
    pallas_call x1, Pallas kernels, project(): pl.pallas_call(project_kernel, grid=(width // cols,), in_specs=[whole5, w...  7.33 us
  transfers between devices with their start and end apart: 16, of which 3 were waited for; matrix products, arithmetic and copies ran while one was open for 3% of the time, Pallas kernels for 15%

profile of v1, /device:TPU:8, one launch (start us, length us, event | category | flops | bytes accessed | tf_op | source)
XLA Modules:
  0.0 102.7 jit_solution(16749905829698622618)
XLA Ops:
  0.6 1.1 %reshape.353 = bf16[2,4,4,4,1024]{4,3,2,1,0:T(4,128)(2,1)S(1)} reshape(bf16[8,16,1024]{2,1,0:T(8,128)(2,1)} %param.26) | data formatting | bytes 524288 | tf_op jit(solution)/shard_map/reshape | solution.py:229
  1.7 0.1 copy.19
  1.8 0.1 reshape.354
  1.9 2.9 %collective-permute-start = (bf16[16,1024]{1,0:T(8,128)(2,1)S(1)}, bf16[16,1024]{1,0:T(8,128)(2,1)S(1)}, u32[]{:S(2)}, u32[]{:S(2)}) collective-permute-start(bf16[16,1024]{1,0:T(8,128)(2,1)S(1)} %get-tuple-element.121), channel_id=1, source_target_pairs={{0,65},{1,66},{2,67},{3,68},{4,69},{5,70},{6,71},{7,72},{8,73},{9,... | collective-permute-start | bytes 98312 | tf_op jit(solution)/shard_map/ppermute | solution.py:219
  4.8 4.0 %collective-permute-start.2 = (bf16[16,1024]{1,0:T(8,128)(2,1)S(1)}, bf16[16,1024]{1,0:T(8,128)(2,1)S(1)}, u32[]{:S(2)}, u32[]{:S(2)}) collective-permute-start(bf16[16,1024]{1,0:T(8,128)(2,1)S(1)} %get-tuple-element.124), channel_id=1, source_target_pairs={{64,1},{65,2},{66,3},{67,4},{68,5},{69,6},{70,7},{71,8},{72,9},{73... | collective-permute-start | bytes 98312 | tf_op jit(solution)/shard_map/ppermute | solution.py:219
  8.9 0.1 collective-permute-start.1
  9.0 8.0 %collective-permute-start.5 = (bf16[16,1024]{1,0:T(8,128)(2,1)S(1)}, bf16[16,1024]{1,0:T(8,128)(2,1)S(1)}, u32[]{:S(2)}, u32[]{:S(2)}) collective-permute-start(bf16[16,1024]{1,0:T(8,128)(2,1)S(1)} %get-tuple-element.122), channel_id=1, source_target_pairs={{0,127},{1,64},{2,65},{3,66},{4,67},{5,68},{6,69},{7,70},{8,71},{9... | collective-permute-start | bytes 98312 | tf_op jit(solution)/shard_map/ppermute | solution.py:219
  17.0 3.0 %collective-permute-start.7 = (bf16[16,1024]{1,0:T(8,128)(2,1)S(1)}, bf16[16,1024]{1,0:T(8,128)(2,1)S(1)}, u32[]{:S(2)}, u32[]{:S(2)}) collective-permute-start(bf16[16,1024]{1,0:T(8,128)(2,1)S(1)} %get-tuple-element.123), channel_id=1, source_target_pairs={{64,63},{65,0},{66,1},{67,2},{68,3},{69,4},{70,5},{71,6},{72,7},{7... | collective-permute-start | bytes 98312 | tf_op jit(solution)/shard_map/ppermute | solution.py:219
  20.1 0.0 copy-start.1
  20.1 0.0 copy-start.2
  20.1 7.3 %project.1 = (bf16[512,1024]{1,0:T(8,128)(2,1)}, bf16[512,1024]{1,0:T(8,128)(2,1)}) custom-call(bf16[2,8,2,16,1024]{4,3,2,1,0:T(8,128)(2,1)} %bitcast.101, bf16[2,8,2,16,1024]{4,3,2,1,0:T(8,128)(2,1)} %bitcast.103, bf16[1024,1024]{1,0:T(8,128)(2,1)} %wq_ref.3, bf16[1024,1024]{1,0:T(8,128)(2,1)} %wo_ref.3), custom_call_target="tpu_custom_call" | custom-call | flops 2147483648 | bytes 8388608 | tf_op jit(solution)/shard_map/project/pallas_call | solution.py:56
  27.4 0.0 copy-done.1
  27.4 0.0 copy-done.2
  27.4 0.3 fusion.12
  27.8 0.6 fusion.33
  28.5 0.2 reshape.356
  28.7 0.1 reshape.357
  28.8 0.6 copy.23.slot_ref
  29.4 0.0 collective-permute-done
  29.4 1.7 %collective-permute-start.6 = (bf16[2,16,1024]{2,1,0:T(8,128)(2,1)S(1)}, bf16[2,16,1024]{2,1,0:T(8,128)(2,1)S(1)}, u32[]{:S(2)}, u32[]{:S(2)}) collective-permute-start(bf16[2,16,1024]{2,1,0:T(8,128)(2,1)S(1)} %squeeze.54), channel_id=1, source_target_pairs={{0,63},{1,0},{2,1},{3,2},{4,3},{5,4},{6,5},{7,6},{8,7},{9,8},{10,9... | collective-permute-start | bytes 196616 | tf_op jit(solution)/shard_map/ppermute | solution.py:219
  31.2 0.0 collective-permute-done.2
  31.2 1.9 %collective-permute-start.4 = (bf16[4,16,1024]{2,1,0:T(8,128)(2,1)S(1)}, bf16[4,16,1024]{2,1,0:T(8,128)(2,1)S(1)}, u32[]{:S(2)}, u32[]{:S(2)}) collective-permute-start(bf16[4,16,1024]{2,1,0:T(8,128)(2,1)S(1)} %get-tuple-element.128), channel_id=1, source_target_pairs={{64,0},{65,1},{66,2},{67,3},{68,4},{69,5},{70,6},{71,7},{72,8},{73... | collective-permute-start | bytes 393224 | tf_op jit(solution)/shard_map/ppermute | solution.py:219
  33.1 0.0 collective-permute-done.1
  33.1 3.9 %collective-permute-start.3 = (bf16[4,16,1024]{2,1,0:T(8,128)(2,1)S(1)}, bf16[4,16,1024]{2,1,0:T(8,128)(2,1)S(1)}, u32[]{:S(2)}, u32[]{:S(2)}) collective-permute-start(bf16[4,16,1024]{2,1,0:T(8,128)(2,1)S(1)} %get-tuple-element.127), channel_id=1, source_target_pairs={{0,64},{1,65},{2,66},{3,67},{4,68},{5,69},{6,70},{7,71},{8,72},{9,... | collective-permute-start | bytes 393224 | tf_op jit(solution)/shard_map/ppermute | solution.py:219
  37.0 0.0 collective-permute-done.5
  37.1 0.0 collective-permute-done.7
  37.1 0.0 collective-permute-done.6
  37.1 0.9 collective-permute-done.4
  38.0 1.9 %collective-permute-done.3 = bf16[4,16,1024]{2,1,0:T(8,128)(2,1)S(1)} collective-permute-done((bf16[4,16,1024]{2,1,0:T(8,128)(2,1)S(1)}, bf16[4,16,1024]{2,1,0:T(8,128)(2,1)S(1)}, u32[]{:S(2)}, u32[]{:S(2)}) %collective-permute-start.3) | collective-permute-done | bytes 131104 | tf_op jit(solution)/shard_map/ppermute | solution.py:219
  39.9 1.0 pad_maximum_fusion
  41.0 19.0 %attend.1 = (bf16[512,1024]{1,0:T(8,128)(2,1)}, bf16[512,1024]{1,0:T(8,128)(2,1)}, f32[384,1024]{1,0:T(8,128)}) custom-call(bf16[384,1024]{1,0:T(8,128)(2,1)} %bitcast.105, bf16[1024,1024]{1,0:T(8,128)(2,1)} %wk_ref.1, bf16[1024,1024]{1,0:T(8,128)(2,1)} %wv_ref.1, bf16[512,1024]{1,0:T(8,128)(2,1)} %get-tuple-element.106.q_ref, ...), custom_call_target="tpu_custom_call" | custom-call | flops 12000000000 | bytes 10485760 | tf_op jit(solution)/shard_map/attend/pallas_call | solution.py:147
  60.0 0.0 copy-start
  60.0 1.6 %convert_element_type.4 = bf16[6,4,16,1024]{3,2,1,0:T(8,128)(2,1)S(1)} convert(f32[6,4,16,1024]{3,2,1,0:T(8,128)} %bitcast.95) | non-fusion elementwise | flops 393216 | bytes 2359296 | tf_op jit(solution)/shard_map/convert_element_type | solution.py:264
  61.6 0.2 copy-done
  62.0 1.9 %collective-permute-start.8 = (bf16[4,16,1024]{2,1,0:T(8,128)(2,1)S(1)}, bf16[4,16,1024]{2,1,0:T(8,128)(2,1)S(1)}, u32[]{:S(2)}, u32[]{:S(2)}) collective-permute-start(bf16[4,16,1024]{2,1,0:T(8,128)(2,1)S(1)} %get-tuple-element.120), channel_id=1, source_target_pairs={{64,0},{65,1},{66,2},{67,3},{68,4},{69,5},{70,6},{71,7},{72,8},{73... | collective-permute-start | bytes 393224 | tf_op jit(solution)/shard_map/ppermute | solution.py:219
  63.9 3.9 %collective-permute-start.9 = (bf16[4,16,1024]{2,1,0:T(8,128)(2,1)S(1)}, bf16[4,16,1024]{2,1,0:T(8,128)(2,1)S(1)}, u32[]{:S(2)}, u32[]{:S(2)}) collective-permute-start(bf16[4,16,1024]{2,1,0:T(8,128)(2,1)S(1)} %get-tuple-element.119), channel_id=1, source_target_pairs={{0,64},{1,65},{2,66},{3,67},{4,68},{5,69},{6,70},{7,71},{8,72},{9,... | collective-permute-start | bytes 393224 | tf_op jit(solution)/shard_map/ppermute | solution.py:219
  67.8 0.1 collective-permute-start.10
  67.9 0.5 collective-permute-start.11
  68.4 6.0 %collective-permute-start.12 = (bf16[16,1024]{1,0:T(8,128)(2,1)S(1)}, bf16[16,1024]{1,0:T(8,128)(2,1)S(1)}, u32[]{:S(2)}, u32[]{:S(2)}) collective-permute-start(bf16[16,1024]{1,0:T(8,128)(2,1)S(1)} %get-tuple-element.116), channel_id=1, source_target_pairs={{64,63},{65,0},{66,1},{67,2},{68,3},{69,4},{70,5},{71,6},{72,7},{7... | collective-permute-start | bytes 98312 | tf_op jit(solution)/shard_map/ppermute | solution.py:219
  74.4 7.8 %outputs.1 = (bf16[2,8,2,16,1024]{4,3,2,1,0:T(8,128)(2,1)}, bf16[2,8,2,16,1024]{4,3,2,1,0:T(8,128)(2,1)}) custom-call(bf16[2,8,2,16,1024]{4,3,2,1,0:T(8,128)(2,1)} %bitcast.102, bf16[2,8,2,16,1024]{4,3,2,1,0:T(8,128)(2,1)} %bitcast.104, bf16[512,1024]{1,0:T(8,128)(2,1)} %get-tuple-element.108.att_ref, bf16[512,1024]{1,0:T(8,128)(2,1)} %get-tuple-element.109.dq_ref, ...), custom_call_target="tpu_custom_call" | custom-call | flops 2147483648 | bytes 10485760 | tf_op jit(solution)/shard_map/outputs/pallas_call | solution.py:191
  82.2 0.0 collective-permute-done.8
  82.2 1.9 %collective-permute-start.13 = (bf16[16,1024]{1,0:T(8,128)(2,1)S(1)}, bf16[16,1024]{1,0:T(8,128)(2,1)S(1)}, u32[]{:S(2)}, u32[]{:S(2)}) collective-permute-start(bf16[16,1024]{1,0:T(8,128)(2,1)S(1)} %get-tuple-element.115), channel_id=1, source_target_pairs={{64,1},{65,2},{66,3},{67,4},{68,5},{69,6},{70,7},{71,8},{72,9},{73... | collective-permute-start | bytes 98312 | tf_op jit(solution)/shard_map/ppermute | solution.py:219
  84.2 0.0 collective-permute-done.9
  84.2 7.9 %collective-permute-start.14 = (bf16[16,1024]{1,0:T(8,128)(2,1)S(1)}, bf16[16,1024]{1,0:T(8,128)(2,1)S(1)}, u32[]{:S(2)}, u32[]{:S(2)}) collective-permute-start(bf16[16,1024]{1,0:T(8,128)(2,1)S(1)} %get-tuple-element.114), channel_id=1, source_target_pairs={{0,127},{1,64},{2,65},{3,66},{4,67},{5,68},{6,69},{7,70},{8,71},{9... | collective-permute-start | bytes 98312 | tf_op jit(solution)/shard_map/ppermute | solution.py:219
  92.1 0.1 fusion
  92.1 0.0 collective-permute-done.10
  92.2 1.9 %collective-permute-start.15 = (bf16[16,1024]{1,0:T(8,128)(2,1)S(1)}, bf16[16,1024]{1,0:T(8,128)(2,1)S(1)}, u32[]{:S(2)}, u32[]{:S(2)}) collective-permute-start(bf16[16,1024]{1,0:T(8,128)(2,1)S(1)} %get-tuple-element.113), channel_id=1, source_target_pairs={{0,65},{1,66},{2,67},{3,68},{4,69},{5,70},{6,71},{7,72},{8,73},{9,... | collective-permute-start | bytes 98312 | tf_op jit(solution)/shard_map/ppermute | solution.py:219
  94.1 0.0 collective-permute-done.11
  94.2 0.0 collective-permute-done.12
  94.2 0.0 collective-permute-done.13
  94.2 1.3 %fusion.31 = f32[4,2,16,1024]{3,2,1,0:T(8,128)S(1)} fusion(f32[4,2,16,1024]{3,2,1,0:T(8,128)S(1)} %fusion.30, s32[]{:T(128)} %bitcast.32, s32[]{:T(128)} %bitcast.33, bf16[16,1024]{1,0:T(8,128)(2,1)S(1)} %collective-permute-done.13), kind=kLoop, calls=%fused_computation.71 | loop fusion | flops 32768 | bytes 163848 | tf_op jit(solution)/shard_map/scatter-add | solution.py:282
  95.5 0.0 collective-permute-done.14
  95.5 6.1 %collective-permute-done.15 = bf16[16,1024]{1,0:T(8,128)(2,1)S(1)} collective-permute-done((bf16[16,1024]{1,0:T(8,128)(2,1)S(1)}, bf16[16,1024]{1,0:T(8,128)(2,1)S(1)}, u32[]{:S(2)}, u32[]{:S(2)}) %collective-permute-start.15) | collective-permute-done | bytes 32800 | tf_op jit(solution)/shard_map/ppermute | solution.py:219
  101.7 0.1 reshape.371
  101.8 0.1 copy.33
  101.9 0.8 reshape.372
  (24 shorter events, 0.4 us)
Async XLA Ops:
  1.9 27.5 %collective-permute-start = (bf16[16,1024]{1,0:T(8,128)(2,1)S(1)}, bf16[16,1024]{1,0:T(8,128)(2,1)S(1)}, u32[]{:S(2)}, u32[]{:S(2)}) collective-permute-start(bf16[16,1024]{1,0:T(8,128)(2,1)S(1)} %get-tuple-element.121), channel_id=1, source_target_pairs={{0,65},{1,66},{2,67},{3,68},{4,69},{5,70},{6,71},{7,72},{8,73},{9,... | collective-permute-start | bytes 98312 | tf_op jit(solution)/shard_map/ppermute | solution.py:219
  4.8 26.3 %collective-permute-start.2 = (bf16[16,1024]{1,0:T(8,128)(2,1)S(1)}, bf16[16,1024]{1,0:T(8,128)(2,1)S(1)}, u32[]{:S(2)}, u32[]{:S(2)}) collective-permute-start(bf16[16,1024]{1,0:T(8,128)(2,1)S(1)} %get-tuple-element.124), channel_id=1, source_target_pairs={{64,1},{65,2},{66,3},{67,4},{68,5},{69,6},{70,7},{71,8},{72,9},{73... | collective-permute-start | bytes 98312 | tf_op jit(solution)/shard_map/ppermute | solution.py:219
  8.9 24.2 %collective-permute-start.1 = (bf16[2,16,1024]{2,1,0:T(8,128)(2,1)S(1)}, bf16[2,16,1024]{2,1,0:T(8,128)(2,1)S(1)}, u32[]{:S(2)}, u32[]{:S(2)}) collective-permute-start(bf16[2,16,1024]{2,1,0:T(8,128)(2,1)S(1)} %squeeze.49), channel_id=1, source_target_pairs={{0,1},{1,2},{2,3},{3,4},{4,5},{5,6},{6,7},{7,8},{8,9},{9,10},{10,1... | collective-permute-start | bytes 196616 | tf_op jit(solution)/shard_map/ppermute | solution.py:219
  9.0 28.1 %collective-permute-start.5 = (bf16[16,1024]{1,0:T(8,128)(2,1)S(1)}, bf16[16,1024]{1,0:T(8,128)(2,1)S(1)}, u32[]{:S(2)}, u32[]{:S(2)}) collective-permute-start(bf16[16,1024]{1,0:T(8,128)(2,1)S(1)} %get-tuple-element.122), channel_id=1, source_target_pairs={{0,127},{1,64},{2,65},{3,66},{4,67},{5,68},{6,69},{7,70},{8,71},{9... | collective-permute-start | bytes 98312 | tf_op jit(solution)/shard_map/ppermute | solution.py:219
  17.0 20.1 %collective-permute-start.7 = (bf16[16,1024]{1,0:T(8,128)(2,1)S(1)}, bf16[16,1024]{1,0:T(8,128)(2,1)S(1)}, u32[]{:S(2)}, u32[]{:S(2)}) collective-permute-start(bf16[16,1024]{1,0:T(8,128)(2,1)S(1)} %get-tuple-element.123), channel_id=1, source_target_pairs={{64,63},{65,0},{66,1},{67,2},{68,3},{69,4},{70,5},{71,6},{72,7},{7... | collective-permute-start | bytes 98312 | tf_op jit(solution)/shard_map/ppermute | solution.py:219
  20.1 7.4 %copy-start.1 = (s32[12,16,32]{2,1,0:T(8,128)S(1)}, s32[12,16,32]{2,1,0:T(8,128)}, u32[]{:S(2)}) copy-start(s32[12,16,32]{2,1,0:T(8,128)} %param.27) | copy-start | bytes 73732
  20.1 7.3 %copy-start.2 = (s32[12,16,32]{2,1,0:T(8,128)S(1)}, s32[12,16,32]{2,1,0:T(8,128)}, u32[]{:S(2)}) copy-start(s32[12,16,32]{2,1,0:T(8,128)} %param.28) | copy-start | bytes 73732
  29.4 7.7 %collective-permute-start.6 = (bf16[2,16,1024]{2,1,0:T(8,128)(2,1)S(1)}, bf16[2,16,1024]{2,1,0:T(8,128)(2,1)S(1)}, u32[]{:S(2)}, u32[]{:S(2)}) collective-permute-start(bf16[2,16,1024]{2,1,0:T(8,128)(2,1)S(1)} %squeeze.54), channel_id=1, source_target_pairs={{0,63},{1,0},{2,1},{3,2},{4,3},{5,4},{6,5},{7,6},{8,7},{9,8},{10,9... | collective-permute-start | bytes 196616 | tf_op jit(solution)/shard_map/ppermute | solution.py:219
  31.2 6.9 %collective-permute-start.4 = (bf16[4,16,1024]{2,1,0:T(8,128)(2,1)S(1)}, bf16[4,16,1024]{2,1,0:T(8,128)(2,1)S(1)}, u32[]{:S(2)}, u32[]{:S(2)}) collective-permute-start(bf16[4,16,1024]{2,1,0:T(8,128)(2,1)S(1)} %get-tuple-element.128), channel_id=1, source_target_pairs={{64,0},{65,1},{66,2},{67,3},{68,4},{69,5},{70,6},{71,7},{72,8},{73... | collective-permute-start | bytes 393224 | tf_op jit(solution)/shard_map/ppermute | solution.py:219
  33.1 6.9 %collective-permute-start.3 = (bf16[4,16,1024]{2,1,0:T(8,128)(2,1)S(1)}, bf16[4,16,1024]{2,1,0:T(8,128)(2,1)S(1)}, u32[]{:S(2)}, u32[]{:S(2)}) collective-permute-start(bf16[4,16,1024]{2,1,0:T(8,128)(2,1)S(1)} %get-tuple-element.127), channel_id=1, source_target_pairs={{0,64},{1,65},{2,66},{3,67},{4,68},{5,69},{6,70},{7,71},{8,72},{9,... | collective-permute-start | bytes 393224 | tf_op jit(solution)/shard_map/ppermute | solution.py:219
  60.0 1.9 %copy-start = (f32[384,1024]{1,0:T(8,128)S(1)}, f32[384,1024]{1,0:T(8,128)}, u32[]{:S(2)}) copy-start(f32[384,1024]{1,0:T(8,128)} %get-tuple-element.112) | copy-start | bytes 4718596
  62.0 20.3 %collective-permute-start.8 = (bf16[4,16,1024]{2,1,0:T(8,128)(2,1)S(1)}, bf16[4,16,1024]{2,1,0:T(8,128)(2,1)S(1)}, u32[]{:S(2)}, u32[]{:S(2)}) collective-permute-start(bf16[4,16,1024]{2,1,0:T(8,128)(2,1)S(1)} %get-tuple-element.120), channel_id=1, source_target_pairs={{64,0},{65,1},{66,2},{67,3},{68,4},{69,5},{70,6},{71,7},{72,8},{73... | collective-permute-start | bytes 393224 | tf_op jit(solution)/shard_map/ppermute | solution.py:219
  63.9 20.3 %collective-permute-start.9 = (bf16[4,16,1024]{2,1,0:T(8,128)(2,1)S(1)}, bf16[4,16,1024]{2,1,0:T(8,128)(2,1)S(1)}, u32[]{:S(2)}, u32[]{:S(2)}) collective-permute-start(bf16[4,16,1024]{2,1,0:T(8,128)(2,1)S(1)} %get-tuple-element.119), channel_id=1, source_target_pairs={{0,64},{1,65},{2,66},{3,67},{4,68},{5,69},{6,70},{7,71},{8,72},{9,... | collective-permute-start | bytes 393224 | tf_op jit(solution)/shard_map/ppermute | solution.py:219
  67.8 24.3 %collective-permute-start.10 = (bf16[2,16,1024]{2,1,0:T(8,128)(2,1)S(1)}, bf16[2,16,1024]{2,1,0:T(8,128)(2,1)S(1)}, u32[]{:S(2)}, u32[]{:S(2)}) collective-permute-start(bf16[2,16,1024]{2,1,0:T(8,128)(2,1)S(1)} %get-tuple-element.118), channel_id=1, source_target_pairs={{0,63},{1,0},{2,1},{3,2},{4,3},{5,4},{6,5},{7,6},{8,7},{9,8},{10,9... | collective-permute-start | bytes 196616 | tf_op jit(solution)/shard_map/ppermute | solution.py:219
  67.9 26.2 %collective-permute-start.11 = (bf16[2,16,1024]{2,1,0:T(8,128)(2,1)S(1)}, bf16[2,16,1024]{2,1,0:T(8,128)(2,1)S(1)}, u32[]{:S(2)}, u32[]{:S(2)}) collective-permute-start(bf16[2,16,1024]{2,1,0:T(8,128)(2,1)S(1)} %get-tuple-element.117), channel_id=1, source_target_pairs={{0,1},{1,2},{2,3},{3,4},{4,5},{5,6},{6,7},{7,8},{8,9},{9,10},{10,1... | collective-permute-start | bytes 196616 | tf_op jit(solution)/shard_map/ppermute | solution.py:219
  68.4 25.8 %collective-permute-start.12 = (bf16[16,1024]{1,0:T(8,128)(2,1)S(1)}, bf16[16,1024]{1,0:T(8,128)(2,1)S(1)}, u32[]{:S(2)}, u32[]{:S(2)}) collective-permute-start(bf16[16,1024]{1,0:T(8,128)(2,1)S(1)} %get-tuple-element.116), channel_id=1, source_target_pairs={{64,63},{65,0},{66,1},{67,2},{68,3},{69,4},{70,5},{71,6},{72,7},{7... | collective-permute-start | bytes 98312 | tf_op jit(solution)/shard_map/ppermute | solution.py:219
  82.2 12.0 %collective-permute-start.13 = (bf16[16,1024]{1,0:T(8,128)(2,1)S(1)}, bf16[16,1024]{1,0:T(8,128)(2,1)S(1)}, u32[]{:S(2)}, u32[]{:S(2)}) collective-permute-start(bf16[16,1024]{1,0:T(8,128)(2,1)S(1)} %get-tuple-element.115), channel_id=1, source_target_pairs={{64,1},{65,2},{66,3},{67,4},{68,5},{69,6},{70,7},{71,8},{72,9},{73... | collective-permute-start | bytes 98312 | tf_op jit(solution)/shard_map/ppermute | solution.py:219
  84.2 11.3 %collective-permute-start.14 = (bf16[16,1024]{1,0:T(8,128)(2,1)S(1)}, bf16[16,1024]{1,0:T(8,128)(2,1)S(1)}, u32[]{:S(2)}, u32[]{:S(2)}) collective-permute-start(bf16[16,1024]{1,0:T(8,128)(2,1)S(1)} %get-tuple-element.114), channel_id=1, source_target_pairs={{0,127},{1,64},{2,65},{3,66},{4,67},{5,68},{6,69},{7,70},{8,71},{9... | collective-permute-start | bytes 98312 | tf_op jit(solution)/shard_map/ppermute | solution.py:219
  92.2 9.5 %collective-permute-start.15 = (bf16[16,1024]{1,0:T(8,128)(2,1)S(1)}, bf16[16,1024]{1,0:T(8,128)(2,1)S(1)}, u32[]{:S(2)}, u32[]{:S(2)}) collective-permute-start(bf16[16,1024]{1,0:T(8,128)(2,1)S(1)} %get-tuple-element.113), channel_id=1, source_target_pairs={{0,65},{1,66},{2,67},{3,68},{4,69},{5,70},{6,71},{7,72},{8,73},{9,... | collective-permute-start | bytes 98312 | tf_op jit(solution)/shard_map/ppermute | solution.py:219

commit v2 on v0

v2 whole, which is shorter than its diff:
```python
import jax
import jax.numpy as jnp
from jax import lax
from jax.experimental import pallas as pl
from jax.experimental.pallas import tpu as pltpu
from jax.sharding import PartitionSpec as P

HEADS = 16
HEAD = 64
SLOTS = 12
REACH = 4
NEG_FILL = -1e30
SCALE = 0.125
GROUP = 4
WIDE = GROUP * HEAD

TILES = 4
POINTS = 128
BLOCK = 64
NODES = 3 * BLOCK
MIDDLE = 4 * BLOCK

BF = jnp.bfloat16
F32 = jnp.float32
NT = (((1,), (1,)), ((), ()))
NN = (((1,), (0,)), ((), ()))
TN = (((0,), (0,)), ((), ()))
IN_VMEM = pl.BlockSpec(memory_space=pltpu.VMEM)


def mm(a, b, dims):
    return lax.dot_general(a, b, dims, preferred_element_type=F32)


def call(kernel, name, inputs, outs, flops, scratch=(), limit=16 << 20):
    moved = sum(a.size * a.dtype.itemsize for a in inputs)
    return pl.pallas_call(
        kernel,
        in_specs=[IN_VMEM] * len(inputs),
        out_specs=[IN_VMEM] * len(outs),
        out_shape=[jax.ShapeDtypeStruct(s, d) for s, d in outs],
        scratch_shapes=list(scratch),
        compiler_params=pltpu.CompilerParams(vmem_limit_bytes=limit),
        cost_estimate=pl.CostEstimate(flops=flops, bytes_accessed=moved, transcendentals=0),
        name=name,
    )(*inputs)


def to_tiles(rows):
    cut = rows.reshape(16, TILES, 8, rows.shape[-1])
    return [cut[:, t].reshape(POINTS, rows.shape[-1]) for t in range(TILES)]


def from_tiles(tiles):
    n = tiles[0].shape[-1]
    cut = [t.reshape(16, 1, 8, n) for t in tiles]
    return jnp.concatenate(cut, axis=1).reshape(TILES * POINTS, n)


def node_of(index):
    row, col = index // 16, index % 16
    return (col // 4) * BLOCK + row * 4 + col % 4


def project_kernel(x_ref, c_ref, wq_ref, wo_ref, edges_ref, mask_ref, q_ref, da_ref, bias_ref):
    lat_start = lax.axis_index("lat") * 8
    lon_start = lax.axis_index("lon") * 16
    edges = edges_ref[...]
    row = (edges >> 10) - lat_start + REACH
    col = (edges - lon_start + REACH) & 1023
    tile_of = lax.broadcasted_iota(jnp.int32, edges.shape, 2) >> 3
    slot = ((col >> 2) - tile_of) * BLOCK + row * 4 + (col & 3)
    slot = jnp.where(mask_ref[...] > 0, slot, -1).astype(F32).astype(BF)
    slot = slot.reshape(SLOTS * 16, 32)
    src = lax.broadcasted_iota(jnp.int32, (32, TILES * POINTS), 0)
    dst = lax.broadcasted_iota(jnp.int32, (32, TILES * POINTS), 1)
    pick = jnp.where(src == (dst >> 7) * 8 + (dst & 7), 1.0, 0.0).astype(BF)
    wide = mm(slot, pick, NN).reshape(SLOTS, 16, TILES * POINTS)
    r_of_lane = (lax.broadcasted_iota(jnp.int32, wide.shape, 2) >> 3) & 15
    own_row = lax.broadcasted_iota(jnp.int32, wide.shape, 1) == r_of_lane
    slots = jnp.sum(jnp.where(own_row, wide, 0.0), axis=1)
    node = lax.broadcasted_iota(jnp.int32, (NODES, POINTS), 0).astype(F32)
    for t in range(TILES):
        at = slice(t * POINTS, (t + 1) * POINTS)
        hit = node == slots[0:1, at]
        for e in range(1, SLOTS):
            hit = hit | (node == slots[e : e + 1, at])
        bias_ref[t] = jnp.where(hit, 0.0, NEG_FILL)
    width = q_ref.shape[-1]
    for j in range(0, width, 256):
        lanes = slice(j, j + 256)
        q = to_tiles(mm(x_ref[...], wq_ref[:, lanes], NN))
        d = to_tiles(mm(c_ref[...], wo_ref[lanes, :], NT))
        for t in range(TILES):
            q_ref[t, :, lanes] = q[t].astype(BF) * SCALE
            da_ref[t, :, lanes] = d[t].astype(BF) * SCALE


def assemble_kernel(low_ref, own_ref, high_ref, mid_ref):
    rows = jnp.concatenate([low_ref[...], own_ref[...], high_ref[...]], axis=0)
    dst = lax.broadcasted_iota(jnp.int32, (MIDDLE, MIDDLE), 0)
    src = lax.broadcasted_iota(jnp.int32, (MIDDLE, MIDDLE), 1)
    pick = jnp.where(dst == node_of(src), 1.0, 0.0).astype(BF)
    for j in range(0, mid_ref.shape[-1], 256):
        lanes = slice(j, j + 256)
        mid_ref[:, lanes] = mm(pick, rows[:, lanes], NN).astype(BF)


def pair_kernel(mid_ref, wk_ref, wv_ref, k_ref, v_ref):
    for j in range(0, mid_ref.shape[-1], 256):
        lanes = slice(j, j + 256)
        k_ref[:, lanes] = mm(mid_ref[...], wk_ref[:, lanes], NN).astype(BF)
        v_ref[:, lanes] = mm(mid_ref[...], wv_ref[:, lanes], NN).astype(BF)


def spread(block):
    head = lax.broadcasted_iota(jnp.int32, (1, WIDE), 1) // HEAD
    zero = jnp.zeros_like(block)
    return jnp.concatenate([jnp.where(head == h, block, zero) for h in range(GROUP)], axis=0)


def attend_group(keys, values, q4, d4, bias_ref, t, scratch):
    pw, sw, pt, st = scratch
    queries, grads = spread(q4), spread(d4)
    scores = mm(keys, queries, NT)
    d_probs = mm(values, grads, NT)
    for h in range(GROUP):
        at = slice(h * POINTS, (h + 1) * POINTS)
        s = scores[:, at] + bias_ref[t]
        e = jnp.exp(s - jnp.max(s, axis=0, keepdims=True))
        p = e * (1.0 / jnp.sum(e, axis=0, keepdims=True))
        half = p.astype(BF)
        dp = d_probs[:, at]
        centred = jnp.sum(p * dp, axis=0, keepdims=True)
        ds = (p * (dp - centred)).astype(BF)
        pw[:, at] = half
        sw[:, at] = ds
        tall = slice(h * NODES, (h + 1) * NODES)
        pt[tall, :] = half
        st[tall, :] = ds
    att = mm(pt[...], spread(values), TN).astype(BF)
    dq = mm(st[...], spread(keys), TN).astype(BF)
    dk = mm(sw[...], queries, NN)
    dv = mm(pw[...], grads, NN)
    return att, dq, dk, dv


ATTEND_SCRATCH = (
    pltpu.VMEM((NODES, GROUP * POINTS), BF),
    pltpu.VMEM((NODES, GROUP * POINTS), BF),
    pltpu.VMEM((GROUP * NODES, POINTS), BF),
    pltpu.VMEM((GROUP * NODES, POINTS), BF),
)


def edges_kernel(
    left_ref, right_ref, k_ref, v_ref, wk_ref, wv_ref, q_ref, da_ref, bias_ref,
    att_ref, dq_ref, dk_ref, dv_ref, low_ref, high_ref,
    kl, vl, dkl, dvl, *scratch,
):
    rim = jnp.concatenate([left_ref[...], right_ref[...]], axis=0)
    for j in range(0, rim.shape[-1], 256):
        lanes = slice(j, j + 256)
        kl[:, lanes] = mm(rim, wk_ref[:, lanes], NN).astype(BF)
        vl[:, lanes] = mm(rim, wv_ref[:, lanes], NN).astype(BF)

    def group(g, carry):
        lanes = pl.ds(pl.multiple_of(g * WIDE, WIDE), WIDE)
        left = (slice(0, BLOCK), slice(0, 2 * BLOCK))
        right = (slice(BLOCK, 2 * BLOCK), slice(2 * BLOCK, 4 * BLOCK))
        for i, t, (rim_at, mid_at) in ((0, 0, left), (1, 3, right)):
            order = (lambda r, m: [r, m]) if i == 0 else (lambda r, m: [m, r])
            keys = jnp.concatenate(order(kl[rim_at, lanes], k_ref[mid_at, lanes]), axis=0)
            values = jnp.concatenate(order(vl[rim_at, lanes], v_ref[mid_at, lanes]), axis=0)
            att, dq, dk, dv = attend_group(
                keys, values, q_ref[t, :, lanes], da_ref[t, :, lanes], bias_ref, t, scratch
            )
            att_ref[i, :, lanes] = att
            dq_ref[i, :, lanes] = dq
            r, m = (
                (slice(0, BLOCK), slice(BLOCK, NODES))
                if i == 0
                else (slice(2 * BLOCK, NODES), slice(0, 2 * BLOCK))
            )
            dkl[rim_at, lanes] = (dk[r] * (1.0 / SCALE)).astype(BF)
            dvl[rim_at, lanes] = (dv[r] * (1.0 / SCALE)).astype(BF)
            dk_ref[mid_at, lanes] = dk[m]
            dv_ref[mid_at, lanes] = dv[m]
        return carry

    lax.fori_loop(0, HEADS // GROUP, group, 0)
    for j in range(0, rim.shape[-1], 256):
        lanes = slice(j, j + 256)
        part = mm(dkl[...], wk_ref[lanes, :], NT) + mm(dvl[...], wv_ref[lanes, :], NT)
        low_ref[:, lanes] = part[:BLOCK].astype(BF)
        high_ref[:, lanes] = part[BLOCK:].astype(BF)


def middle_kernel(
    k_ref, v_ref, wk_ref, wv_ref, q_ref, da_ref, bias_ref, dk_ref, dv_ref,
    att_ref, dq_ref, part_ref,
    dks, dvs, *scratch,
):
    def group(g, carry):
        lanes = pl.ds(pl.multiple_of(g * WIDE, WIDE), WIDE)
        dks[:, lanes] = dk_ref[:, lanes]
        dvs[:, lanes] = dv_ref[:, lanes]
        for i, t in ((0, 1), (1, 2)):
            at = slice(i * BLOCK, i * BLOCK + NODES)
            att, dq, dk, dv = attend_group(
                k_ref[at, lanes], v_ref[at, lanes], q_ref[t, :, lanes], da_ref[t, :, lanes],
                bias_ref, t, scratch,
            )
            att_ref[i, :, lanes] = att
            dq_ref[i, :, lanes] = dq
            dks[at, lanes] += dk
            dvs[at, lanes] += dv
        return carry

    lax.fori_loop(0, HEADS // GROUP, group, 0)
    dst = lax.broadcasted_iota(jnp.int32, (MIDDLE, MIDDLE), 0)
    src = lax.broadcasted_iota(jnp.int32, (MIDDLE, MIDDLE), 1)
    pick = jnp.where(src == node_of(dst), 1.0, 0.0).astype(BF)
    dk = mm(pick, (dks[...] * (1.0 / SCALE)).astype(BF), NN).astype(BF)
    dv = mm(pick, (dvs[...] * (1.0 / SCALE)).astype(BF), NN).astype(BF)
    for j in range(0, part_ref.shape[-1], 256):
        lanes = slice(j, j + 256)
        part_ref[:, lanes] = mm(dk, wk_ref[lanes, :], NT) + mm(dv, wv_ref[lanes, :], NT)


def merge_kernel(part_ref, left_ref, right_ref, low_ref, own_ref, high_ref):
    dst = lax.broadcasted_iota(jnp.int32, (MIDDLE, 2 * BLOCK), 0)
    src = lax.broadcasted_iota(jnp.int32, (MIDDLE, 2 * BLOCK), 1)
    place = node_of(dst)
    place = jnp.where(place >= 3 * BLOCK, place - 2 * BLOCK, jnp.where(place < BLOCK, place, -1))
    pick = jnp.where(place == src, 1.0, 0.0).astype(BF)
    rims = jnp.concatenate([left_ref[...], right_ref[...]], axis=0)
    for j in range(0, part_ref.shape[-1], 256):
        lanes = slice(j, j + 256)
        total = part_ref[:, lanes] + mm(pick, rims[:, lanes], NN)
        low_ref[:, lanes] = total[:BLOCK].astype(BF)
        own_ref[:, lanes] = total[BLOCK : 3 * BLOCK]
        high_ref[:, lanes] = total[3 * BLOCK :].astype(BF)


def outputs_kernel(x_ref, c_ref, ae_ref, am_ref, de_ref, dm_ref, wo_ref, wq_ref, out_ref, grad_ref):
    width = out_ref.shape[-1]
    att = jnp.concatenate([ae_ref[0], am_ref[0], am_ref[1], ae_ref[1]], axis=0)
    dq = jnp.concatenate([de_ref[0], dm_ref[0], dm_ref[1], de_ref[1]], axis=0)

    def ordered(rows):
        return from_tiles([rows[t * POINTS : (t + 1) * POINTS] for t in range(TILES)])

    for j in range(0, width, 256):
        lanes = slice(j, j + 256)
        a = ordered(mm(att, wo_ref[:, lanes], NN))
        out_ref[:, lanes] = (x_ref[:, lanes].astype(F32) + a).astype(BF)
        b = ordered(mm(dq, wq_ref[lanes, :], NT))
        grad_ref[:, lanes] = (c_ref[:, lanes].astype(F32) + b).astype(BF)


def finish_kernel(own_ref, low_ref, high_ref, out_ref):
    out_ref[:BLOCK] = (own_ref[:BLOCK] + low_ref[...].astype(F32)).astype(BF)
    out_ref[BLOCK:] = (own_ref[BLOCK:] + high_ref[...].astype(F32)).astype(BF)


def swap(low, high, axis, ring):
    count = lax.axis_size(axis)
    odd = lax.axis_index(axis) % 2 == 1
    even_pairs = [(i, i + 1) for i in range(0, count, 2)]
    odd_pairs = [(i, i + 1) for i in range(1, count - 1, 2)]
    if ring:
        odd_pairs.append((count - 1, 0))

    def both(pairs):
        return pairs + [(b, a) for a, b in pairs]

    a = lax.ppermute(jnp.where(odd, low, high), axis, both(even_pairs))
    b = lax.ppermute(jnp.where(odd, high, low), axis, both(odd_pairs))
    return jnp.where(odd, a, b), jnp.where(odd, b, a)


def local(grid_feat, mesh_feat, edges, edge_mask, w_query, w_key, w_value, w_out, cotangent):
    width = grid_feat.shape[-1]
    points = TILES * POINTS
    x = grid_feat.reshape(points, width)
    c = cotangent.reshape(points, width)
    own = mesh_feat.reshape(2 * BLOCK, width)
    product = 2 * width * width

    low, high = swap(own[:BLOCK], own[BLOCK:], "lat", False)
    q, da, bias = call(
        project_kernel, "project", (x, c, w_query, w_out, edges, edge_mask),
        [((TILES, POINTS, width), BF)] * 2 + [((TILES, NODES, POINTS), F32)],
        2 * points * product,
    )
    (mid,) = call(assemble_kernel, "assemble", (low, own, high), [((MIDDLE, width), BF)], 10**8)
    left, right = swap(mid[:BLOCK], mid[3 * BLOCK :], "lon", True)
    k, v = call(
        pair_kernel, "pair", (mid, w_key, w_value), [((MIDDLE, width), BF)] * 2,
        2 * MIDDLE * product,
    )
    half = ((2, POINTS, width), BF)
    att_e, dq_e, dk, dv, to_left, to_right = call(
        edges_kernel, "attend_edges", (left, right, k, v, w_key, w_value, q, da, bias),
        [half, half] + [((MIDDLE, width), F32)] * 2 + [((BLOCK, width), BF)] * 2,
        6 * 10**9,
        (pltpu.VMEM((2 * BLOCK, width), BF),) * 4 + ATTEND_SCRATCH,
    )
    left, right = swap(to_left, to_right, "lon", True)
    att_m, dq_m, part = call(
        middle_kernel, "attend_middle", (k, v, w_key, w_value, q, da, bias, dk, dv),
        [half, half, ((MIDDLE, width), F32)],
        6 * 10**9,
        (pltpu.VMEM((MIDDLE, width), F32),) * 2 + ATTEND_SCRATCH,
    )
    to_low, kept, to_high = call(
        merge_kernel, "merge", (part, left, right),
        [((BLOCK, width), BF), ((2 * BLOCK, width), F32), ((BLOCK, width), BF)],
        10**8,
    )
    low, high = swap(to_low, to_high, "lat", False)
    layer_out, grid_grad = call(
        outputs_kernel, "outputs", (x, c, att_e, att_m, dq_e, dq_m, w_out, w_query),
        [((points, width), BF)] * 2,
        2 * points * product,
    )
    (mesh_grad,) = call(finish_kernel, "finish", (kept, low, high), [((2 * BLOCK, width), BF)], 10**6)
    return (
        layer_out.reshape(grid_feat.shape),
        grid_grad.reshape(grid_feat.shape),
        mesh_grad.reshape(mesh_feat.shape),
    )


def solution(mesh):
    tiled = P("lat", "lon", None)
    placed = (tiled, tiled, P(None, "lat", "lon"), P(None, "lat", "lon")) + (P(),) * 4 + (tiled,)
    return jax.shard_map(
        local, mesh=mesh, in_specs=placed, out_specs=(tiled, tiled, tiled), check_vma=False
    )
```

time: 158 us -> 55.7 us (0.35)
  matrix products: 82.6 us -> 0 us
  local copies, waits for them, and re-layouts: 41.3 us -> 6.79 us
  Pallas kernels: 0 us -> 24.9 us
  other arithmetic: 7.8 us -> 1.3 us
  waiting for transfers between devices: 8.08 us -> 4.25 us
    dot_general x11 -> x0, matrix products: 72 us -> none  [the longest x1 18.8 us: local(): jnp.einsum('hrp,rhd->phd', d_scores, query_heads, preferred_element_type=...]
    pallas_call x0 -> x8, Pallas kernels: none -> 24.9 us  [call(): pl.pallas_call(kernel, in_specs=[IN_VMEM] * len(inputs), out_specs=[IN_VM...]
    sub x1 -> x0, matrix products: 10.6 us -> none  [local(): exp_scores = jnp.exp(scores - row_max)]
    concatenate x4 -> x0, local copies, waits for them, and re-layouts: 10.5 us -> none  [the longest x3 10.3 us: local(): d_pair = jnp.concatenate([d_keys, d_values], axis=1)]
    unnamed x36 -> x24, local copies, waits for them, and re-layouts: 13.5 us -> 6.79 us
    transpose x2 -> x0, local copies, waits for them, and re-layouts: 6.64 us -> none  [the longest x1 3.34 us: local(): jnp.einsum('hrp,rhd->phd', probs_half, d_heads, preferred_element_type=jn...]
    slice x4 -> x0, local copies, waits for them, and re-layouts: 4.92 us -> none  [the longest x1 2.75 us: send_rims_back(): padded[:, -HALO_REACH:]]
    convert_element_type x2 -> x0, local copies, waits for them, and re-layouts: 4.55 us -> none  [the longest x1 2.28 us: local(): jnp.dot(cot_rows, w_out.T, preferred_element_type=jnp.float32)]
  transfers between devices with their start and end apart: 8 -> 8, of which waited for: 3 -> 2; matrix products, arithmetic and copies ran while one was open for 26% -> 0% of each run, Pallas kernels for 0% -> 28%
where the time goes in v2:
time: 55.7 us; the launch traced here: 55.3 us
  Pallas kernels  24.9 us (45%)
  starting transfers between devices  17.1 us (31%)
  local copies, waits for them, and re-layouts  6.79 us (12%)
  waiting for transfers between devices  4.25 us (8%)
  other arithmetic  1.3 us (2%)
  between operations  0.9 us (2%)
    pallas_call x8, Pallas kernels, call(): pl.pallas_call(kernel, in_specs=[IN_VMEM] * len(inputs), out_specs=[IN_VM...  24.9 us
    ppermute x4, starting transfers between devices, swap(): b = lax.ppermute(jnp.where(odd, high, low), axis, both(odd_pairs))  14.6 us
    unnamed x24, local copies, waits for them, and re-layouts  6.79 us
    ppermute x4, waiting for transfers between devices, swap(): b = lax.ppermute(jnp.where(odd, high, low), axis, both(odd_pairs))  3.78 us
    ppermute x4, starting transfers between devices, swap(): a = lax.ppermute(jnp.where(odd, low, high), axis, both(even_pairs))  2.52 us
    select_n x4, other arithmetic, swap(): b = lax.ppermute(jnp.where(odd, high, low), axis, both(odd_pairs))  1.21 us
  transfers between devices with their start and end apart: 8, of which 2 were waited for; matrix products, arithmetic and copies ran while one was open for 0% of the time, Pallas kernels for 28%

profile of v2, /device:TPU:8, one launch (start us, length us, event | category | flops | bytes accessed | tf_op | source)
XLA Modules:
  0.0 55.3 jit_solution(2036417697867753290)
XLA Ops:
  0.6 0.0 copy-start.2
  0.7 1.1 %broadcast_select_fusion = (bf16[4,16,1024]{2,1,0:T(8,128)(2,1)S(1)}, bf16[4,16,1024]{2,1,0:T(8,128)(2,1)S(1)}) fusion(pred[]{:T(512)S(6)} %eq.14, bf16[8,16,1024]{2,1,0:T(8,128)(2,1)} %param.10), kind=kLoop, calls=%fused_computation | loop fusion | flops 131072 | bytes 524289 | tf_op jit(solution)/shard_map/jit(_where)/select_n | solution.py:279
  1.8 2.2 %collective-permute-start = (bf16[64,1024]{1,0:T(8,128)(2,1)S(1)}, bf16[64,1024]{1,0:T(8,128)(2,1)S(1)}, u32[]{:S(2)}, u32[]{:S(2)}) collective-permute-start(bf16[64,1024]{1,0:T(8,128)(2,1)S(1)} %bitcast.15), channel_id=1, source_target_pairs={{0,64},{128,192},{64,0},{192,128},{1,65},{129,193},{65,1},{193,129... | collective-permute-start | bytes 393224 | tf_op jit(solution)/shard_map/ppermute | solution.py:278
  4.0 2.6 %collective-permute-start.1 = (bf16[64,1024]{1,0:T(8,128)(2,1)S(1)}, bf16[64,1024]{1,0:T(8,128)(2,1)S(1)}, u32[]{:S(2)}, u32[]{:S(2)}) collective-permute-start(bf16[64,1024]{1,0:T(8,128)(2,1)S(1)} %bitcast.14), channel_id=1, source_target_pairs={{64,128},{128,64},{65,129},{129,65},{66,130},{130,66},{67,131},{13... | collective-permute-start | bytes 393224 | tf_op jit(solution)/shard_map/ppermute | solution.py:279
  6.7 0.5 collective-permute-done
  7.1 3.8 %collective-permute-done.1 = bf16[64,1024]{1,0:T(8,128)(2,1)S(1)} collective-permute-done((bf16[64,1024]{1,0:T(8,128)(2,1)S(1)}, bf16[64,1024]{1,0:T(8,128)(2,1)S(1)}, u32[]{:S(2)}, u32[]{:S(2)}) %collective-permute-start.1) | collective-permute-done | bytes 131104 | tf_op jit(solution)/shard_map/ppermute | solution.py:279
  10.9 0.0 copy-start.5
  10.9 0.9 %copy-done.5 = bf16[8,16,1024]{2,1,0:T(8,128)(2,1)S(1)} copy-done((bf16[8,16,1024]{2,1,0:T(8,128)(2,1)S(1)}, bf16[8,16,1024]{2,1,0:T(8,128)(2,1)}, u32[]{:S(2)}) %copy-start.5) | copy-done | bytes 262168
  11.9 0.3 assemble.1.mid_ref
  12.2 0.1 collective-permute-start.2
  12.3 7.1 %collective-permute-start.3 = (bf16[64,1024]{1,0:T(8,128)(2,1)S(1)}, bf16[64,1024]{1,0:T(8,128)(2,1)S(1)}, u32[]{:S(2)}, u32[]{:S(2)}) collective-permute-start(bf16[64,1024]{1,0:T(8,128)(2,1)S(1)} %get-tuple-element.41), channel_id=1, source_target_pairs={{1,2},{3,4},{5,6},{7,8},{9,10},{11,12},{13,14},{15,16},{17,18},{19... | collective-permute-start | bytes 393224 | tf_op jit(solution)/shard_map/ppermute | solution.py:279
  19.4 0.0 copy-done.2
  19.4 0.0 copy-start.3
  19.4 1.6 %copy-done.3 = bf16[1024,1024]{1,0:T(8,128)(2,1)S(1)} copy-done((bf16[1024,1024]{1,0:T(8,128)(2,1)S(1)}, bf16[1024,1024]{1,0:T(8,128)(2,1)}, u32[]{:S(2)}) %copy-start.3) | copy-done | bytes 2097176
  21.0 0.0 copy-start.6
  21.0 1.2 %copy-done.6 = bf16[16,32,1024]{2,1,0:T(8,128)(2,1)S(1)} copy-done((bf16[16,32,1024]{2,1,0:T(8,128)(2,1)S(1)}, bf16[16,32,1024]{2,1,0:T(8,128)(2,1)}, u32[]{:S(2)}) %copy-start.6) | copy-done | bytes 1048600
  22.2 0.0 copy-start.8
  22.2 1.2 %copy-done.8 = bf16[16,32,1024]{2,1,0:T(8,128)(2,1)S(1)} copy-done((bf16[16,32,1024]{2,1,0:T(8,128)(2,1)S(1)}, bf16[16,32,1024]{2,1,0:T(8,128)(2,1)}, u32[]{:S(2)}) %copy-start.8) | copy-done | bytes 1048600
  23.5 0.0 copy-start.10
  23.5 0.9 %copy-done.10 = s32[12,16,32]{2,1,0:T(8,128)S(1)} copy-done((s32[12,16,32]{2,1,0:T(8,128)S(1)}, s32[12,16,32]{2,1,0:T(8,128)}, u32[]{:S(2)}) %copy-start.10) | copy-done | bytes 24600
  24.4 0.0 copy-start.11
  24.4 0.9 %copy-done.11 = s32[12,16,32]{2,1,0:T(8,128)S(1)} copy-done((s32[12,16,32]{2,1,0:T(8,128)S(1)}, s32[12,16,32]{2,1,0:T(8,128)}, u32[]{:S(2)}) %copy-start.11) | copy-done | bytes 24600
  25.2 0.0 copy-start
  25.2 0.0 copy-start.1
  25.2 3.0 %project.1 = (bf16[4,128,1024]{2,1,0:T(8,128)(2,1)S(1)}, bf16[4,128,1024]{2,1,0:T(8,128)(2,1)S(1)}, f32[4,192,128]{2,1,0:T(8,128)S(1)}) custom-call(bf16[512,1024]{1,0:T(8,128)(2,1)S(1)} %bitcast.9, bf16[512,1024]{1,0:T(8,128)(2,1)S(1)} %bitcast.11, bf16[1024,1024]{1,0:T(8,128)(2,1)S(1)} %copy-done.2, bf16[1024,1024]{1,0:T(8,128)(2,1)S(1)} %copy-done.3, ...), custom_call_target="tpu_custom_call" | custom-call | flops 2147483648 | bytes 6340608 | tf_op jit(solution)/shard_map/project/pallas_call | solution.py:37
  28.2 0.0 copy-done
  28.2 0.0 copy-done.1
  28.3 1.3 %pair.1 = (bf16[256,1024]{1,0:T(8,128)(2,1)S(1)}, bf16[256,1024]{1,0:T(8,128)(2,1)S(1)}) custom-call(bf16[256,1024]{1,0:T(8,128)(2,1)S(1)} %assemble.1.mid_ref, bf16[1024,1024]{1,0:T(8,128)(2,1)S(1)} %copy-done, bf16[1024,1024]{1,0:T(8,128)(2,1)S(1)} %copy-done.1), custom_call_target="tpu_custom_call" | custom-call | flops 1073741824 | bytes 4718592 | tf_op jit(solution)/shard_map/pair/pallas_call | solution.py:37
  29.5 0.0 collective-permute-done.2
  29.5 0.0 collective-permute-done.3
  29.6 8.1 %attend_edges.1 = (bf16[2,128,1024]{2,1,0:T(8,128)(2,1)S(1)}, bf16[2,128,1024]{2,1,0:T(8,128)(2,1)S(1)}, f32[256,1024]{1,0:T(8,128)S(1)}, f32[256,1024]{1,0:T(8,...) custom-call(bf16[64,1024]{1,0:T(8,128)(2,1)S(1)} %get-tuple-element.52.left_ref, ...), custom_call_target="tpu_custom_call" | custom-call | flops 6000000000 | bytes 7995392 | tf_op jit(solution)/shard_map/attend_edges/pallas_call | solution.py:37
  37.8 0.1 collective-permute-start.4
  37.9 1.1 %collective-permute-start.5 = (bf16[64,1024]{1,0:T(8,128)(2,1)S(1)}, bf16[64,1024]{1,0:T(8,128)(2,1)S(1)}, u32[]{:S(2)}, u32[]{:S(2)}) collective-permute-start(bf16[64,1024]{1,0:T(8,128)(2,1)S(1)} %get-tuple-element.49), channel_id=1, source_target_pairs={{1,2},{3,4},{5,6},{7,8},{9,10},{11,12},{13,14},{15,16},{17,18},{19... | collective-permute-start | bytes 393224 | tf_op jit(solution)/shard_map/ppermute | solution.py:279
  39.0 0.0 copy-start.7
  39.0 0.0 copy-start.9
  39.0 7.6 %attend_middle.1 = (bf16[2,128,1024]{2,1,0:T(8,128)(2,1)S(1)}, bf16[2,128,1024]{2,1,0:T(8,128)(2,1)S(1)}, f32[256,1024]{1,0:T(8,128)S(1)}) custom-call(bf16[256,1024]{1,0:T(8,128)(2,1)S(1)} %get-tuple-element.22.k_ref, bf16[256,1024]{1,0:T(8,128)(2,1)S(1)} %get-tuple-element.23.v_ref, bf16[1024,1024]{1,0:T(8,128)(2,1)S(1)} %copy-done, ...), custom_call_target="tpu_custom_call" | custom-call | flops 6000000000 | bytes 9830400 | tf_op jit(solution)/shard_map/attend_middle/pallas_call | solution.py:37
  46.5 0.0 copy-start.4
  46.5 0.0 collective-permute-done.4
  46.6 0.0 collective-permute-done.5
  46.6 0.3 merge.1
  46.9 0.1 collective-permute-start.6
  47.0 3.8 %collective-permute-start.7 = (bf16[64,1024]{1,0:T(8,128)(2,1)S(1)}, bf16[64,1024]{1,0:T(8,128)(2,1)S(1)}, u32[]{:S(2)}, u32[]{:S(2)}) collective-permute-start(bf16[64,1024]{1,0:T(8,128)(2,1)S(1)} %get-tuple-element.45), channel_id=1, source_target_pairs={{64,128},{128,64},{65,129},{129,65},{66,130},{130,66},{67,131},{13... | collective-permute-start | bytes 393224 | tf_op jit(solution)/shard_map/ppermute | solution.py:279
  50.8 0.0 copy-done.7
  50.8 0.0 copy-done.9
  50.9 0.0 copy-done.4
  50.9 3.6 %outputs.1 = (bf16[512,1024]{1,0:T(8,128)(2,1)}, bf16[512,1024]{1,0:T(8,128)(2,1)}) custom-call(bf16[512,1024]{1,0:T(8,128)(2,1)S(1)} %bitcast.10, bf16[512,1024]{1,0:T(8,128)(2,1)S(1)} %bitcast.12, bf16[2,128,1024]{2,1,0:T(8,128)(2,1)S(1)} %get-tuple-element.27.ae_ref, bf16[2,128,1024]{2,1,0:T(8,128)(2,1)S(1)} %get-tuple-element.30.am_ref, ...), custom_call_target="tpu_custom_call" | custom-call | flops 2147483648 | bytes 8388608 | tf_op jit(solution)/shard_map/outputs/pallas_call | solution.py:37
  54.5 0.0 collective-permute-done.6
  54.5 0.0 collective-permute-done.7
  54.5 0.7 %finish.1 = bf16[128,1024]{1,0:T(8,128)(2,1)} custom-call(f32[128,1024]{1,0:T(8,128)S(1)} %get-tuple-element.38.own_ref, bf16[64,1024]{1,0:T(8,128)(2,1)S(1)} %get-tuple-element.44.low_ref, bf16[64,1024]{1,0:T(8,128)(2,1)S(1)} %get-tuple-element.43.high_ref), custom_call_target="tpu_custom_call" | custom-call | flops 1000000 | bytes 786432 | tf_op jit(solution)/shard_map/finish/pallas_call | solution.py:37
  (7 shorter events, 0.2 us)
Async XLA Ops:
  0.6 18.8 %copy-start.2 = (bf16[1024,1024]{1,0:T(8,128)(2,1)S(1)}, bf16[1024,1024]{1,0:T(8,128)(2,1)}, u32[]{:S(2)}) copy-start(bf16[1024,1024]{1,0:T(8,128)(2,1)} %wq_ref.3) | copy-start | bytes 6291460
  1.8 5.3 %collective-permute-start = (bf16[64,1024]{1,0:T(8,128)(2,1)S(1)}, bf16[64,1024]{1,0:T(8,128)(2,1)S(1)}, u32[]{:S(2)}, u32[]{:S(2)}) collective-permute-start(bf16[64,1024]{1,0:T(8,128)(2,1)S(1)} %bitcast.15), channel_id=1, source_target_pairs={{0,64},{128,192},{64,0},{192,128},{1,65},{129,193},{65,1},{193,129... | collective-permute-start | bytes 393224 | tf_op jit(solution)/shard_map/ppermute | solution.py:278
  4.0 6.8 %collective-permute-start.1 = (bf16[64,1024]{1,0:T(8,128)(2,1)S(1)}, bf16[64,1024]{1,0:T(8,128)(2,1)S(1)}, u32[]{:S(2)}, u32[]{:S(2)}) collective-permute-start(bf16[64,1024]{1,0:T(8,128)(2,1)S(1)} %bitcast.14), channel_id=1, source_target_pairs={{64,128},{128,64},{65,129},{129,65},{66,130},{130,66},{67,131},{13... | collective-permute-start | bytes 393224 | tf_op jit(solution)/shard_map/ppermute | solution.py:279
  10.9 1.0 %copy-start.5 = (bf16[8,16,1024]{2,1,0:T(8,128)(2,1)S(1)}, bf16[8,16,1024]{2,1,0:T(8,128)(2,1)}, u32[]{:S(2)}) copy-start(bf16[8,16,1024]{2,1,0:T(8,128)(2,1)} %param.10) | copy-start | bytes 786436
  12.2 17.3 %collective-permute-start.2 = (bf16[64,1024]{1,0:T(8,128)(2,1)S(1)}, bf16[64,1024]{1,0:T(8,128)(2,1)S(1)}, u32[]{:S(2)}, u32[]{:S(2)}) collective-permute-start(bf16[64,1024]{1,0:T(8,128)(2,1)S(1)} %get-tuple-element.42), channel_id=1, source_target_pairs={{0,1},{2,3},{4,5},{6,7},{8,9},{10,11},{12,13},{14,15},{16,17},{18,... | collective-permute-start | bytes 393224 | tf_op jit(solution)/shard_map/ppermute | solution.py:278
  12.3 17.2 %collective-permute-start.3 = (bf16[64,1024]{1,0:T(8,128)(2,1)S(1)}, bf16[64,1024]{1,0:T(8,128)(2,1)S(1)}, u32[]{:S(2)}, u32[]{:S(2)}) collective-permute-start(bf16[64,1024]{1,0:T(8,128)(2,1)S(1)} %get-tuple-element.41), channel_id=1, source_target_pairs={{1,2},{3,4},{5,6},{7,8},{9,10},{11,12},{13,14},{15,16},{17,18},{19... | collective-permute-start | bytes 393224 | tf_op jit(solution)/shard_map/ppermute | solution.py:279
  19.4 1.6 %copy-start.3 = (bf16[1024,1024]{1,0:T(8,128)(2,1)S(1)}, bf16[1024,1024]{1,0:T(8,128)(2,1)}, u32[]{:S(2)}) copy-start(bf16[1024,1024]{1,0:T(8,128)(2,1)} %wo_ref.3) | copy-start | bytes 6291460
  21.0 1.2 %copy-start.6 = (bf16[16,32,1024]{2,1,0:T(8,128)(2,1)S(1)}, bf16[16,32,1024]{2,1,0:T(8,128)(2,1)}, u32[]{:S(2)}) copy-start(bf16[16,32,1024]{2,1,0:T(8,128)(2,1)} %param.9) | copy-start | bytes 3145732
  22.2 1.2 %copy-start.8 = (bf16[16,32,1024]{2,1,0:T(8,128)(2,1)S(1)}, bf16[16,32,1024]{2,1,0:T(8,128)(2,1)}, u32[]{:S(2)}) copy-start(bf16[16,32,1024]{2,1,0:T(8,128)(2,1)} %param.17) | copy-start | bytes 3145732
  23.5 0.9 %copy-start.10 = (s32[12,16,32]{2,1,0:T(8,128)S(1)}, s32[12,16,32]{2,1,0:T(8,128)}, u32[]{:S(2)}) copy-start(s32[12,16,32]{2,1,0:T(8,128)} %edges_ref.1) | copy-start | bytes 73732
  24.4 0.9 %copy-start.11 = (s32[12,16,32]{2,1,0:T(8,128)S(1)}, s32[12,16,32]{2,1,0:T(8,128)}, u32[]{:S(2)}) copy-start(s32[12,16,32]{2,1,0:T(8,128)} %mask_ref.1) | copy-start | bytes 73732
  25.2 3.0 %copy-start = (bf16[1024,1024]{1,0:T(8,128)(2,1)S(1)}, bf16[1024,1024]{1,0:T(8,128)(2,1)}, u32[]{:S(2)}) copy-start(bf16[1024,1024]{1,0:T(8,128)(2,1)} %wk_ref.5) | copy-start | bytes 6291460
  25.2 3.0 %copy-start.1 = (bf16[1024,1024]{1,0:T(8,128)(2,1)S(1)}, bf16[1024,1024]{1,0:T(8,128)(2,1)}, u32[]{:S(2)}) copy-start(bf16[1024,1024]{1,0:T(8,128)(2,1)} %wv_ref.5) | copy-start | bytes 6291460
  37.8 8.8 %collective-permute-start.4 = (bf16[64,1024]{1,0:T(8,128)(2,1)S(1)}, bf16[64,1024]{1,0:T(8,128)(2,1)S(1)}, u32[]{:S(2)}, u32[]{:S(2)}) collective-permute-start(bf16[64,1024]{1,0:T(8,128)(2,1)S(1)} %get-tuple-element.50), channel_id=1, source_target_pairs={{0,1},{2,3},{4,5},{6,7},{8,9},{10,11},{12,13},{14,15},{16,17},{18,... | collective-permute-start | bytes 393224 | tf_op jit(solution)/shard_map/ppermute | solution.py:278
  37.9 8.7 %collective-permute-start.5 = (bf16[64,1024]{1,0:T(8,128)(2,1)S(1)}, bf16[64,1024]{1,0:T(8,128)(2,1)S(1)}, u32[]{:S(2)}, u32[]{:S(2)}) collective-permute-start(bf16[64,1024]{1,0:T(8,128)(2,1)S(1)} %get-tuple-element.49), channel_id=1, source_target_pairs={{1,2},{3,4},{5,6},{7,8},{9,10},{11,12},{13,14},{15,16},{17,18},{19... | collective-permute-start | bytes 393224 | tf_op jit(solution)/shard_map/ppermute | solution.py:279
  39.0 11.9 %copy-start.7 = (bf16[16,32,1024]{2,1,0:T(8,128)(2,1)S(1)}, bf16[16,32,1024]{2,1,0:T(8,128)(2,1)}, u32[]{:S(2)}) copy-start(bf16[16,32,1024]{2,1,0:T(8,128)(2,1)} %param.9) | copy-start | bytes 3145732
  39.0 11.9 %copy-start.9 = (bf16[16,32,1024]{2,1,0:T(8,128)(2,1)S(1)}, bf16[16,32,1024]{2,1,0:T(8,128)(2,1)}, u32[]{:S(2)}) copy-start(bf16[16,32,1024]{2,1,0:T(8,128)(2,1)} %param.17) | copy-start | bytes 3145732
  46.5 4.3 %copy-start.4 = (bf16[1024,1024]{1,0:T(8,128)(2,1)S(1)}, bf16[1024,1024]{1,0:T(8,128)(2,1)}, u32[]{:S(2)}) copy-start(bf16[1024,1024]{1,0:T(8,128)(2,1)} %wo_ref.3) | copy-start | bytes 6291460
  46.9 7.6 %collective-permute-start.6 = (bf16[64,1024]{1,0:T(8,128)(2,1)S(1)}, bf16[64,1024]{1,0:T(8,128)(2,1)S(1)}, u32[]{:S(2)}, u32[]{:S(2)}) collective-permute-start(bf16[64,1024]{1,0:T(8,128)(2,1)S(1)} %get-tuple-element.46), channel_id=1, source_target_pairs={{0,64},{128,192},{64,0},{192,128},{1,65},{129,193},{65,1},{193,129... | collective-permute-start | bytes 393224 | tf_op jit(solution)/shard_map/ppermute | solution.py:278
  47.0 7.5 %collective-permute-start.7 = (bf16[64,1024]{1,0:T(8,128)(2,1)S(1)}, bf16[64,1024]{1,0:T(8,128)(2,1)S(1)}, u32[]{:S(2)}, u32[]{:S(2)}) collective-permute-start(bf16[64,1024]{1,0:T(8,128)(2,1)S(1)} %get-tuple-element.45), channel_id=1, source_target_pairs={{64,128},{128,64},{65,129},{129,65},{66,130},{130,66},{67,131},{13... | collective-permute-start | bytes 393224 | tf_op jit(solution)/shard_map/ppermute | solution.py:279

commit v3 on v2

v3 whole, which is shorter than its diff:
```python
import jax
import jax.numpy as jnp
from jax import lax
from jax.experimental import pallas as pl
from jax.experimental.pallas import tpu as pltpu
from jax.sharding import PartitionSpec as P


HEADS = 16
HEAD = 64
SLOTS = 12
REACH = 4
NEG_FILL = -1e30
SCALE = 0.125
GROUP = 4
WIDE = GROUP * HEAD

TILES = 4
POINTS = 128
BLOCK = 64
NODES = 3 * BLOCK
MIDDLE = 4 * BLOCK

BF = jnp.bfloat16
F32 = jnp.float32
NT = (((1,), (1,)), ((), ()))
NN = (((1,), (0,)), ((), ()))
TN = (((0,), (0,)), ((), ()))
IN_VMEM = pl.BlockSpec(memory_space=pltpu.VMEM)
IN_HBM = pl.BlockSpec(memory_space=pltpu.MemorySpace.HBM)
IN_PLACE = pl.BlockSpec(memory_space=pl.ANY)


def mm(a, b, dims):
    return lax.dot_general(a, b, dims, preferred_element_type=F32)


def call(kernel, inputs, outs, flops, scratch=(), hbm=(), loose=(), hbm_out=(), limit=16 << 20):
    moved = sum(a.size * a.dtype.itemsize for a in inputs)

    def placed(i):
        return IN_HBM if i in hbm else IN_PLACE if i in loose else IN_VMEM

    return pl.pallas_call(
        kernel,
        in_specs=[placed(i) for i in range(len(inputs))],
        out_specs=[IN_HBM if i in hbm_out else IN_VMEM for i in range(len(outs))],
        out_shape=[
            jax.ShapeDtypeStruct(s, d) if i in hbm_out else pltpu.VMEM(s, d)
            for i, (s, d) in enumerate(outs)
        ],
        scratch_shapes=list(scratch),
        compiler_params=pltpu.CompilerParams(vmem_limit_bytes=limit),
        cost_estimate=pl.CostEstimate(flops=flops, bytes_accessed=moved, transcendentals=0),
    )(
        *(
            pltpu.with_memory_space_constraint(a, pltpu.MemorySpace.HBM) if i in hbm else a
            for i, a in enumerate(inputs)
        )
    )


def to_tiles(rows):
    cut = rows.reshape(16, TILES, 8, rows.shape[-1])
    return [cut[:, t].reshape(POINTS, rows.shape[-1]) for t in range(TILES)]


def from_tiles(tiles):
    n = tiles[0].shape[-1]
    cut = [t.reshape(16, 1, 8, n) for t in tiles]
    return jnp.concatenate(cut, axis=1).reshape(TILES * POINTS, n)


def node_of(index):
    row, col = index // 16, index % 16
    return (col // 4) * BLOCK + row * 4 + col % 4


def lead_kernel(mesh_ref, a_ref, b_ref, sem):
    odd = lax.axis_index("lat") % 2
    first = pltpu.make_async_copy(mesh_ref.at[pl.ds((1 - odd) * BLOCK, BLOCK)], a_ref, sem.at[0])
    second = pltpu.make_async_copy(mesh_ref.at[pl.ds(odd * BLOCK, BLOCK)], b_ref, sem.at[1])
    first.start()
    second.start()
    first.wait()
    second.wait()


def project_q_kernel(
    x_hbm, wq_hbm, c_hbm, wo_hbm, piece_ref, q_ref, c_ref, wo_ref, pass_ref, x_scr, wq_scr, sem
):
    copies = [pltpu.make_async_copy(x_hbm, x_scr, sem.at[0])]
    width = q_ref.shape[-1]
    blocks = [slice(j, j + 256) for j in range(0, width, 256)]
    for i, lanes in enumerate(blocks):
        copies.append(
            pltpu.make_async_copy(wq_hbm.at[:, lanes], wq_scr.at[:, lanes], sem.at[1 + i])
        )
    copies.append(pltpu.make_async_copy(c_hbm, c_ref, sem.at[5]))
    copies.append(pltpu.make_async_copy(wo_hbm, wo_ref, sem.at[6]))
    for copy in copies:
        copy.start()
    pass_ref[...] = piece_ref[...]
    copies[0].wait()
    for i, lanes in enumerate(blocks):
        copies[1 + i].wait()
        q = to_tiles(mm(x_scr[...], wq_scr[:, lanes], NN))
        for t in range(TILES):
            q_ref[t, :, lanes] = q[t].astype(BF) * SCALE
    copies[5].wait()
    copies[6].wait()


def project_d_kernel(c_ref, wo_ref, edges_ref, mask_ref, da_ref, bias_ref):
    lat_start = lax.axis_index("lat") * 8
    lon_start = lax.axis_index("lon") * 16
    edges = edges_ref[...]
    row = (edges >> 10) - lat_start + REACH
    col = (edges - lon_start + REACH) & 1023
    tile_of = lax.broadcasted_iota(jnp.int32, edges.shape, 2) >> 3
    slot = ((col >> 2) - tile_of) * BLOCK + row * 4 + (col & 3)
    slot = jnp.where(mask_ref[...] > 0, slot, -1).astype(F32).astype(BF)
    slot = slot.reshape(SLOTS * 16, 32)
    src = lax.broadcasted_iota(jnp.int32, (32, TILES * POINTS), 0)
    dst = lax.broadcasted_iota(jnp.int32, (32, TILES * POINTS), 1)
    pick = jnp.where(src == (dst >> 7) * 8 + (dst & 7), 1.0, 0.0).astype(BF)
    wide = mm(slot, pick, NN).reshape(SLOTS, 16, TILES * POINTS)
    r_of_lane = (lax.broadcasted_iota(jnp.int32, wide.shape, 2) >> 3) & 15
    own_row = lax.broadcasted_iota(jnp.int32, wide.shape, 1) == r_of_lane
    slots = jnp.sum(jnp.where(own_row, wide, 0.0), axis=1)
    node = lax.broadcasted_iota(jnp.int32, (NODES, POINTS), 0).astype(F32)
    for t in range(TILES):
        at = slice(t * POINTS, (t + 1) * POINTS)
        hit = node == slots[0:1, at]
        for e in range(1, SLOTS):
            hit = hit | (node == slots[e : e + 1, at])
        bias_ref[t] = jnp.where(hit, 0.0, NEG_FILL)
    for j in range(0, da_ref.shape[-1], 256):
        lanes = slice(j, j + 256)
        d = to_tiles(mm(c_ref[...], wo_ref[lanes, :], NT))
        for t in range(TILES):
            da_ref[t, :, lanes] = d[t].astype(BF) * SCALE


def sort_pair(axis, a, b):
    odd = lax.axis_index(axis) % 2 == 1
    return jnp.where(odd, a, b), jnp.where(odd, b, a)


def assemble_kernel(got_a, got_b, own_a, own_b, after_ref, mid_ref, send_a, send_b):
    low, high = sort_pair("lat", got_a[...], got_b[...])
    own_low, own_high = sort_pair("lat", own_a[...], own_b[...])
    rows = jnp.concatenate([low, own_low, own_high, high], axis=0)
    dst = lax.broadcasted_iota(jnp.int32, (MIDDLE, MIDDLE), 0)
    src = lax.broadcasted_iota(jnp.int32, (MIDDLE, MIDDLE), 1)
    pick = jnp.where(dst == node_of(src), 1.0, 0.0).astype(BF)
    for j in range(0, mid_ref.shape[-1], 256):
        lanes = slice(j, j + 256)
        mid = mm(pick, rows[:, lanes], NN).astype(BF)
        mid_ref[:, lanes] = mid
        send_a[:, lanes], send_b[:, lanes] = sort_pair("lon", mid[:BLOCK], mid[3 * BLOCK :])


def pair_kernel(mid_ref, wk_ref, wv_ref, k_ref, v_ref):
    for j in range(0, mid_ref.shape[-1], 256):
        lanes = slice(j, j + 256)
        k_ref[:, lanes] = mm(mid_ref[...], wk_ref[:, lanes], NN).astype(BF)
        v_ref[:, lanes] = mm(mid_ref[...], wv_ref[:, lanes], NN).astype(BF)


def spread(block):
    head = lax.broadcasted_iota(jnp.int32, (1, WIDE), 1) // HEAD
    return jnp.concatenate(
        [block * jnp.where(head == h, 1.0, 0.0).astype(BF) for h in range(GROUP)], axis=0
    )


def score(keys, values, q4, d4, bufs):
    s_ref, d_ref, qs_ref, gs_ref = bufs[:4]
    queries, grads = spread(q4), spread(d4)
    qs_ref[...] = queries
    gs_ref[...] = grads
    s_ref[...] = mm(keys, queries, NT)
    d_ref[...] = mm(values, grads, NT)


def soften(bias, bufs):
    s_ref, d_ref, _, _, pw, sw, pt, st = bufs
    for h in range(GROUP):
        at = slice(h * POINTS, (h + 1) * POINTS)
        s = s_ref[:, at] + bias
        e = jnp.exp(s - jnp.max(s, axis=0, keepdims=True))
        p = e * (1.0 / jnp.sum(e, axis=0, keepdims=True))
        half = p.astype(BF)
        dp = d_ref[:, at]
        centred = jnp.sum(p * dp, axis=0, keepdims=True)
        ds = (p * (dp - centred)).astype(BF)
        pw[:, at] = half
        sw[:, at] = ds
        tall = slice(h * NODES, (h + 1) * NODES)
        pt[tall, :] = half
        st[tall, :] = ds


def gather_grads(keys, values, bufs):
    _, _, qs_ref, gs_ref, pw, sw, pt, st = bufs
    att = mm(pt[...], spread(values), TN).astype(BF)
    dq = mm(st[...], spread(keys), TN).astype(BF)
    dk = mm(sw[...], qs_ref[...], NN)
    dv = mm(pw[...], gs_ref[...], NN)
    return att, dq, dk, dv


ITEM_SCRATCH = (
    (pltpu.VMEM((NODES, GROUP * POINTS), F32),) * 2
    + (pltpu.VMEM((GROUP * POINTS, WIDE), BF),) * 2
    + (pltpu.VMEM((NODES, GROUP * POINTS), BF),) * 2
    + (pltpu.VMEM((GROUP * NODES, POINTS), BF),) * 2
)
PAIR_SCRATCH = ITEM_SCRATCH * 2


def attend_pair(tiles, load, store, q_ref, da_ref, bias_ref, scratch):
    n = len(ITEM_SCRATCH)
    bufs = (scratch[:n], scratch[n:])
    groups = HEADS // GROUP

    def lanes_of(g):
        return pl.ds(pl.multiple_of(g * WIDE, WIDE), WIDE)

    def do_score(g, i):
        lanes = lanes_of(g)
        keys, values = load(i, lanes)
        t = tiles[i]
        score(keys, values, q_ref[t, :, lanes], da_ref[t, :, lanes], bufs[i])

    def do_grads(g, i):
        lanes = lanes_of(g)
        keys, values = load(i, lanes)
        store(i, lanes, *gather_grads(keys, values, bufs[i]))

    for ref in bufs[1][2:]:
        ref[...] = jnp.zeros_like(ref)
    do_score(0, 0)

    def step(g, carry):
        do_grads(jnp.maximum(g - 1, 0), 1)
        soften(bias_ref[tiles[0]], bufs[0])
        do_score(g, 1)
        do_grads(g, 0)
        soften(bias_ref[tiles[1]], bufs[1])
        do_score(jnp.minimum(g + 1, groups - 1), 0)
        return carry

    lax.fori_loop(0, groups, step, 0)
    do_grads(groups - 1, 1)


def edges_kernel(
    got_a, got_b, k_ref, v_ref, wk_ref, wv_ref, q_ref, da_ref, bias_ref,
    att_ref, dq_ref, dk_ref, dv_ref, send_a, send_b,
    kl, vl, dkl, dvl, *scratch,
):
    rim = jnp.concatenate(sort_pair("lon", got_a[...], got_b[...]), axis=0)
    for j in range(0, rim.shape[-1], 256):
        lanes = slice(j, j + 256)
        kl[:, lanes] = mm(rim, wk_ref[:, lanes], NN).astype(BF)
        vl[:, lanes] = mm(rim, wv_ref[:, lanes], NN).astype(BF)

    def load(i, lanes):
        def one(rim, mid):
            if i == 0:
                return jnp.concatenate([rim[:BLOCK, lanes], mid[: 2 * BLOCK, lanes]], axis=0)
            return jnp.concatenate([mid[2 * BLOCK :, lanes], rim[BLOCK:, lanes]], axis=0)

        return one(kl, k_ref), one(vl, v_ref)

    def store(i, lanes, att, dq, dk, dv):
        att_ref[i, :, lanes] = att
        dq_ref[i, :, lanes] = dq
        rim_at = slice(i * BLOCK, (i + 1) * BLOCK)
        mid_at = slice(i * 2 * BLOCK, (i + 1) * 2 * BLOCK)
        r = slice(0, BLOCK) if i == 0 else slice(2 * BLOCK, NODES)
        m = slice(BLOCK, NODES) if i == 0 else slice(0, 2 * BLOCK)
        dkl[rim_at, lanes] = (dk[r] * (1.0 / SCALE)).astype(BF)
        dvl[rim_at, lanes] = (dv[r] * (1.0 / SCALE)).astype(BF)
        dk_ref[mid_at, lanes] = dk[m]
        dv_ref[mid_at, lanes] = dv[m]

    attend_pair((0, 3), load, store, q_ref, da_ref, bias_ref, scratch)
    for j in range(0, rim.shape[-1], 256):
        lanes = slice(j, j + 256)
        part = mm(dkl[...], wk_ref[lanes, :], NT) + mm(dvl[...], wv_ref[lanes, :], NT)
        send_a[:, lanes], send_b[:, lanes] = sort_pair(
            "lon", part[:BLOCK].astype(BF), part[BLOCK:].astype(BF)
        )


def middle_kernel(
    k_ref, v_ref, wk_ref, wv_ref, q_ref, da_ref, bias_ref, dk_ref, dv_ref,
    att_ref, dq_ref, part_ref, dko_ref, dvo_ref,
    dks, dvs, *scratch,
):
    dks[...] = dk_ref[...]
    dvs[...] = dv_ref[...]

    def load(i, lanes):
        at = slice(i * BLOCK, i * BLOCK + NODES)
        return k_ref[at, lanes], v_ref[at, lanes]

    def store(i, lanes, att, dq, dk, dv):
        at = slice(i * BLOCK, i * BLOCK + NODES)
        att_ref[i, :, lanes] = att
        dq_ref[i, :, lanes] = dq
        dks[at, lanes] += dk
        dvs[at, lanes] += dv

    attend_pair((1, 2), load, store, q_ref, da_ref, bias_ref, scratch)
    row = lax.broadcasted_iota(jnp.int32, (MIDDLE, MIDDLE), 0)
    src = lax.broadcasted_iota(jnp.int32, (MIDDLE, MIDDLE), 1)
    nodes = jnp.where(
        row < BLOCK, row, jnp.where(row < 2 * BLOCK, row + 2 * BLOCK, row - BLOCK)
    )
    pick = jnp.where(src == node_of(nodes), 1.0, 0.0).astype(BF)
    dk = mm(pick, (dks[...] * (1.0 / SCALE)).astype(BF), NN).astype(BF)
    dv = mm(pick, (dvs[...] * (1.0 / SCALE)).astype(BF), NN).astype(BF)
    dko_ref[...] = dk[2 * BLOCK :]
    dvo_ref[...] = dv[2 * BLOCK :]
    for j in range(0, part_ref.shape[-1], 256):
        lanes = slice(j, j + 256)
        part_ref[:, lanes] = mm(dk[: 2 * BLOCK], wk_ref[lanes, :], NT) + mm(
            dv[: 2 * BLOCK], wv_ref[lanes, :], NT
        )


def rim_pick(first, count):
    row = lax.broadcasted_iota(jnp.int32, (count, 2 * BLOCK), 0)
    src = lax.broadcasted_iota(jnp.int32, (count, 2 * BLOCK), 1)
    place = node_of(row + first)
    place = jnp.where(place >= 3 * BLOCK, place - 2 * BLOCK, jnp.where(place < BLOCK, place, -1))
    return jnp.where(place == src, 1.0, 0.0).astype(BF)


def merge_kernel(part_ref, got_a, got_b, send_a, send_b):
    pick = jnp.concatenate([rim_pick(0, BLOCK), rim_pick(3 * BLOCK, BLOCK)], axis=0)
    rims = jnp.concatenate(sort_pair("lon", got_a[...], got_b[...]), axis=0)
    for j in range(0, part_ref.shape[-1], 256):
        lanes = slice(j, j + 256)
        total = part_ref[:, lanes] + mm(pick, rims[:, lanes], NN)
        send_a[:, lanes], send_b[:, lanes] = sort_pair(
            "lat", total[:BLOCK].astype(BF), total[BLOCK:].astype(BF)
        )


def emit(res_ref, rows_e, rows_m, w_ref, dims, out_hbm, out_scr, sem):
    rows = jnp.concatenate([rows_e[0], rows_m[0], rows_m[1], rows_e[1]], axis=0)
    copies = []
    for i, j in enumerate(range(0, out_scr.shape[-1], 256)):
        lanes = slice(j, j + 256)
        w = w_ref[:, lanes] if dims is NN else w_ref[lanes, :]
        product = mm(rows, w, dims)
        tiles = [product[t * POINTS : (t + 1) * POINTS] for t in range(TILES)]
        out_scr[:, lanes] = (res_ref[:, lanes].astype(F32) + from_tiles(tiles)).astype(BF)
        copy = pltpu.make_async_copy(out_scr.at[:, lanes], out_hbm.at[:, lanes], sem.at[i])
        copy.start()
        copies.append(copy)
    return copies


def layer_out_kernel(
    x_ref, ae_ref, am_ref, wo_ref, piece_ref, out_hbm, pass_ref, out_scr, sem
):
    pass_ref[...] = piece_ref[...]
    for copy in emit(x_ref, ae_ref, am_ref, wo_ref, NN, out_hbm, out_scr, sem):
        copy.wait()


def grid_grad_kernel(
    c_ref, de_ref, dm_ref, wq_ref, dk_ref, dv_ref, wk_ref, wv_ref, got_a, got_b,
    grad_hbm, own_ref, out_scr, sem,
):
    copies = emit(c_ref, de_ref, dm_ref, wq_ref, NT, grad_hbm, out_scr, sem)
    pick = rim_pick(BLOCK, 2 * BLOCK)
    rims = jnp.concatenate(sort_pair("lon", got_a[...], got_b[...]), axis=0)
    for j in range(0, own_ref.shape[-1], 256):
        lanes = slice(j, j + 256)
        own_ref[:, lanes] = (
            mm(dk_ref[...], wk_ref[lanes, :], NT)
            + mm(dv_ref[...], wv_ref[lanes, :], NT)
            + mm(pick, rims[:, lanes], NN)
        )
    for copy in copies:
        copy.wait()


def finish_kernel(own_ref, got_a, got_b, out_hbm, out_scr, sem):
    copies = []
    for i, part in enumerate(sort_pair("lat", got_a[...], got_b[...])):
        rows = slice(i * BLOCK, (i + 1) * BLOCK)
        out_scr[rows] = (own_ref[rows] + part.astype(F32)).astype(BF)
        copies.append(pltpu.make_async_copy(out_scr.at[rows], out_hbm.at[rows], sem.at[i]))
        copies[-1].start()
    for copy in copies:
        copy.wait()


def pairs_of(axis, ring):
    count = lax.axis_size(axis)
    even = [(i, i + 1) for i in range(0, count, 2)]
    odd = [(i, i + 1) for i in range(1, count - 1, 2)]
    if ring:
        odd.append((count - 1, 0))
    return tuple(pairs + [(b, a) for a, b in pairs] for pairs in (even, odd))


def local(grid_feat, mesh_feat, edges, edge_mask, w_query, w_key, w_value, w_out, cotangent):
    width = grid_feat.shape[-1]
    points = TILES * POINTS
    x = grid_feat.reshape(points, width)
    c = cotangent.reshape(points, width)
    own = mesh_feat.reshape(2 * BLOCK, width)
    product = 2 * width * width
    lat_a, lat_b = pairs_of("lat", False)
    lon_a, lon_b = pairs_of("lon", True)
    piece = ((BLOCK, width), BF)
    tiled = ((TILES, POINTS, width), BF)
    square = ((width, width), BF)

    send_a, send_b = call(
        lead_kernel, (own,), [piece, piece], 10**5,
        (pltpu.SemaphoreType.DMA((2,)),), hbm=(0,),
    )
    got_a = lax.ppermute(send_a, "lat", lat_a)
    q, c_near, wo_near, late_b = call(
        project_q_kernel, (x, w_query, c, w_out, send_b),
        [tiled, ((points, width), BF), square, piece],
        points * product,
        (
            pltpu.VMEM((points, width), BF),
            pltpu.VMEM((width, width), BF),
            pltpu.SemaphoreType.DMA((7,)),
        ),
        hbm=(0, 1, 2, 3),
    )
    got_b = lax.ppermute(late_b, "lat", lat_b)
    da, bias = call(
        project_d_kernel, (c_near, wo_near, edges, edge_mask),
        [tiled, ((TILES, NODES, POINTS), F32)],
        points * product,
    )
    mid, edge_a, edge_b = call(
        assemble_kernel, (got_a, got_b, send_a, send_b, da),
        [((MIDDLE, width), BF), piece, piece], 10**8, loose=(4,),
    )
    edge_a = lax.ppermute(edge_a, "lon", lon_a)
    edge_b = lax.ppermute(edge_b, "lon", lon_b)
    k, v = call(
        pair_kernel, (mid, w_key, w_value), [((MIDDLE, width), BF)] * 2,
        2 * MIDDLE * product,
    )
    half = ((2, POINTS, width), BF)
    att_e, dq_e, dk, dv, edge_a, edge_b = call(
        edges_kernel, (edge_a, edge_b, k, v, w_key, w_value, q, da, bias),
        [half, half] + [((MIDDLE, width), F32)] * 2 + [piece] * 2,
        6 * 10**9,
        (pltpu.VMEM((2 * BLOCK, width), BF),) * 4 + PAIR_SCRATCH,
    )
    edge_a = lax.ppermute(edge_a, "lon", lon_a)
    edge_b = lax.ppermute(edge_b, "lon", lon_b)
    att_m, dq_m, part, dk_own, dv_own = call(
        middle_kernel, (k, v, w_key, w_value, q, da, bias, dk, dv),
        [half, half, ((2 * BLOCK, width), F32)] + [((2 * BLOCK, width), BF)] * 2,
        6 * 10**9,
        (pltpu.VMEM((MIDDLE, width), F32),) * 2 + PAIR_SCRATCH,
    )
    send_a, send_b = call(merge_kernel, (part, edge_a, edge_b), [piece, piece], 10**8)
    got_a = lax.ppermute(send_a, "lat", lat_a)
    out_scratch = (pltpu.VMEM((points, width), BF), pltpu.SemaphoreType.DMA((4,)))
    layer_out, late_b = call(
        layer_out_kernel, (x, att_e, att_m, w_out, send_b),
        [((points, width), BF), piece],
        points * product, out_scratch, hbm_out=(0,),
    )
    got_b = lax.ppermute(late_b, "lat", lat_b)
    grid_grad, kept = call(
        grid_grad_kernel,
        (c, dq_e, dq_m, w_query, dk_own, dv_own, w_key, w_value, edge_a, edge_b),
        [((points, width), BF), ((2 * BLOCK, width), F32)],
        points * product, out_scratch, hbm_out=(0,),
    )
    (mesh_grad,) = call(
        finish_kernel, (kept, got_a, got_b), [((2 * BLOCK, width), BF)], 10**6,
        (pltpu.VMEM((2 * BLOCK, width), BF), pltpu.SemaphoreType.DMA((2,))), hbm_out=(0,),
    )
    return (
        layer_out.reshape(grid_feat.shape),
        grid_grad.reshape(grid_feat.shape),
        mesh_grad.reshape(mesh_feat.shape),
    )


def solution(mesh):
    tiled = P("lat", "lon", None)
    placed = (tiled, tiled, P(None, "lat", "lon"), P(None, "lat", "lon")) + (P(),) * 4 + (tiled,)
    return jax.shard_map(
        local, mesh=mesh, in_specs=placed, out_specs=(tiled, tiled, tiled), check_vma=False
    )
```

time: 55.7 us -> 59.2 us (1.063)
  local copies, waits for them, and re-layouts: 6.79 us -> 0.04 us
  Pallas kernels: 24.9 us -> 30.9 us
  starting transfers between devices: 17.1 us -> 21.2 us
  waiting for transfers between devices: 4.25 us -> 5.79 us
  other arithmetic: 1.3 us -> 0 us
    unnamed x24 -> x16, local copies, waits for them, and re-layouts: 6.79 us -> 0.04 us
    pallas_call x8 -> x11, Pallas kernels: 24.9 us -> 30.9 us  [call(): pl.pallas_call(kernel, in_specs=[placed(i) for i in range(len(inputs))],...]
    ppermute x8, starting transfers between devices: 17.1 us -> 21.2 us  [the longest x2 12.4 us: local(): edge_b = lax.ppermute(edge_b, 'lon', lon_b)]
    ppermute x8, waiting for transfers between devices: 4.25 us -> 5.79 us  [the longest x2 2.58 us: local(): got_b = lax.ppermute(late_b, 'lat', lat_b)]
    select_n x8 -> x0, other arithmetic: 1.3 us -> none  [the longest x4 1.21 us: swap(): b = lax.ppermute(jnp.where(odd, high, low), axis, both(odd_pairs))]
  transfers between devices with their start and end apart: 8 -> 8, of which waited for: 2 -> 4; matrix products, arithmetic and copies ran while one was open for 0% -> 0% of each run, Pallas kernels for 28% -> 31%
where the time goes in v3:
time: 59.2 us; the launch traced here: 59 us
  Pallas kernels  30.9 us (52%)
  starting transfers between devices  21.2 us (36%)
  waiting for transfers between devices  5.79 us (10%)
  between operations  1.03 us (2%)
    pallas_call x11, Pallas kernels, call(): pl.pallas_call(kernel, in_specs=[placed(i) for i in range(len(inputs))],...  30.9 us
    ppermute x2, starting transfers between devices, local(): edge_b = lax.ppermute(edge_b, 'lon', lon_b)  12.4 us
    ppermute x2, starting transfers between devices, local(): got_b = lax.ppermute(late_b, 'lat', lat_b)  6.26 us
    ppermute x2, waiting for transfers between devices, local(): got_b = lax.ppermute(late_b, 'lat', lat_b)  2.58 us
    ppermute x2, starting transfers between devices, local(): got_a = lax.ppermute(send_a, 'lat', lat_a)  2.34 us
    ppermute x2, waiting for transfers between devices, local(): got_a = lax.ppermute(send_a, 'lat', lat_a)  1.85 us
    ppermute x2, waiting for transfers between devices, local(): edge_b = lax.ppermute(edge_b, 'lon', lon_b)  1.35 us
  transfers between devices with their start and end apart: 8, of which 4 were waited for; matrix products, arithmetic and copies ran while one was open for 0% of the time, Pallas kernels for 31%

profile of v3, /device:TPU:8, one launch (start us, length us, event | category | flops | bytes accessed | tf_op | source)
XLA Modules:
  0.0 59.0 jit_solution(10404226240526285527)
XLA Ops:
  0.6 1.0 %shard_map.112 = (bf16[64,1024]{1,0:T(8,128)(2,1)S(1)}, bf16[64,1024]{1,0:T(8,128)(2,1)S(1)}) custom-call(bf16[128,1024]{1,0:T(8,128)(2,1)} %bitcast.10), custom_call_target="tpu_custom_call" | custom-call | flops 100000 | bytes 262144 | tf_op jit(solution)/shard_map/pallas_call | solution.py:44
  1.6 2.2 %collective-permute-start = (bf16[64,1024]{1,0:T(8,128)(2,1)S(1)}, bf16[64,1024]{1,0:T(8,128)(2,1)S(1)}, u32[]{:S(2)}, u32[]{:S(2)}) collective-permute-start(bf16[64,1024]{1,0:T(8,128)(2,1)S(1)} %get-tuple-element.33.own_a), channel_id=1, source_target_pairs={{0,64},{128,192},{64,0},{192,128},{1,65},{129,193},{65,1},{193,129... | collective-permute-start | bytes 393224 | tf_op jit(solution)/shard_map/ppermute | solution.py:433
  3.9 0.0 copy-start.6
  3.9 0.0 copy-start.7
  3.9 4.2 %shard_map.113 = (bf16[4,128,1024]{2,1,0:T(8,128)(2,1)S(1)}, bf16[512,1024]{1,0:T(8,128)(2,1)S(1)}, bf16[1024,1024]{1,0:T(8,128)(2,1)S(1)}, bf16[64,1024]{1,0:T(8,128)(2,1)S(1)}) custom-call(bf16[512,1024]{1,0:T(8,128)(2,1)} %bitcast.8, bf16[1024,1024]{1,0:T(8,128)(2,1)} %wq_ref.1, bf16[512,1024]{1,0:T(8,128)(2,1)} %bitcast.6, bf16[1024,1024]{1,0:T(8,128)(2,1)} %wo_ref.1, ...), custom_call_target="tpu_custom_call" | custom-call | flops 1073741824 | bytes 6422528 | tf_op jit(solution)/shard_map/pallas_call | solution.py:44
  8.1 2.6 %collective-permute-start.1 = (bf16[64,1024]{1,0:T(8,128)(2,1)S(1)}, bf16[64,1024]{1,0:T(8,128)(2,1)S(1)}, u32[]{:S(2)}, u32[]{:S(2)}) collective-permute-start(bf16[64,1024]{1,0:T(8,128)(2,1)S(1)} %get-tuple-element.35), channel_id=1, source_target_pairs={{64,128},{128,64},{65,129},{129,65},{66,130},{130,66},{67,131},{13... | collective-permute-start | bytes 393224 | tf_op jit(solution)/shard_map/ppermute | solution.py:445
  10.8 0.0 copy-done.6
  10.8 0.0 copy-done.7
  10.8 0.0 copy-start.2
  10.8 0.0 copy-start.3
  10.8 1.9 %shard_map.114 = (bf16[4,128,1024]{2,1,0:T(8,128)(2,1)S(1)}, f32[4,192,128]{2,1,0:T(8,128)S(1)}) custom-call(bf16[512,1024]{1,0:T(8,128)(2,1)S(1)} %get-tuple-element.36.c_ref, bf16[1024,1024]{1,0:T(8,128)(2,1)S(1)} %get-tuple-element.37.wo_ref, s32[12,16,32]{2,1,0:T(8,128)S(1)} %copy-done.6, s32[12,16,32]{2,1,0:T(8,128)S(1)} %copy-done.7), custom_call_target="tpu_custom_call" | custom-call | flops 1073741824 | bytes 3194880 | tf_op jit(solution)/shard_map/pallas_call | solution.py:44
  12.7 0.0 collective-permute-done.got_a
  12.7 2.3 %collective-permute-done.1.got_b = bf16[64,1024]{1,0:T(8,128)(2,1)S(1)} collective-permute-done((bf16[64,1024]{1,0:T(8,128)(2,1)S(1)}, bf16[64,1024]{1,0:T(8,128)(2,1)S(1)}, u32[]{:S(2)}, u32[]{:S(2)}) %collective-permute-start.1) | collective-permute-done | bytes 131104 | tf_op jit(solution)/shard_map/ppermute | solution.py:445
  15.0 0.3 shard_map.115
  15.3 0.1 collective-permute-start.2
  15.4 7.1 %collective-permute-start.3 = (bf16[64,1024]{1,0:T(8,128)(2,1)S(1)}, bf16[64,1024]{1,0:T(8,128)(2,1)S(1)}, u32[]{:S(2)}, u32[]{:S(2)}) collective-permute-start(bf16[64,1024]{1,0:T(8,128)(2,1)S(1)} %get-tuple-element.40), channel_id=1, source_target_pairs={{1,2},{3,4},{5,6},{7,8},{9,10},{11,12},{13,14},{15,16},{17,18},{19... | collective-permute-start | bytes 393224 | tf_op jit(solution)/shard_map/ppermute | solution.py:456
  22.5 0.0 copy-done.2
  22.5 0.0 copy-done.3
  22.5 1.3 %shard_map.116 = (bf16[256,1024]{1,0:T(8,128)(2,1)S(1)}, bf16[256,1024]{1,0:T(8,128)(2,1)S(1)}) custom-call(bf16[256,1024]{1,0:T(8,128)(2,1)S(1)} %get-tuple-element.41.mid_ref, bf16[1024,1024]{1,0:T(8,128)(2,1)S(1)} %copy-done.2, bf16[1024,1024]{1,0:T(8,128)(2,1)S(1)} %copy-done.3), custom_call_target="tpu_custom_call" | custom-call | flops 1073741824 | bytes 4718592 | tf_op jit(solution)/shard_map/pallas_call | solution.py:44
  23.8 0.0 collective-permute-done.2.got_a
  23.8 1.4 %collective-permute-done.3.got_b = bf16[64,1024]{1,0:T(8,128)(2,1)S(1)} collective-permute-done((bf16[64,1024]{1,0:T(8,128)(2,1)S(1)}, bf16[64,1024]{1,0:T(8,128)(2,1)S(1)}, u32[]{:S(2)}, u32[]{:S(2)}) %collective-permute-start.3) | collective-permute-done | bytes 131104 | tf_op jit(solution)/shard_map/ppermute | solution.py:456
  25.2 8.3 %shard_map.117 = (bf16[2,128,1024]{2,1,0:T(8,128)(2,1)S(1)}, bf16[2,128,1024]{2,1,0:T(8,128)(2,1)S(1)}, f32[256,1024]{1,0:T(8,128)S(1)}, f32[256,1024]{1,0:T(8,1...) custom-call(bf16[64,1024]{1,0:T(8,128)(2,1)S(1)} %collective-permute-done.2.got_a, ...), custom_call_target="tpu_custom_call" | custom-call | flops 6000000000 | bytes 7995392 | tf_op jit(solution)/shard_map/pallas_call | solution.py:44
  33.5 0.1 collective-permute-start.4
  33.6 5.3 %collective-permute-start.5 = (bf16[64,1024]{1,0:T(8,128)(2,1)S(1)}, bf16[64,1024]{1,0:T(8,128)(2,1)S(1)}, u32[]{:S(2)}, u32[]{:S(2)}) collective-permute-start(bf16[64,1024]{1,0:T(8,128)(2,1)S(1)} %get-tuple-element.52), channel_id=1, source_target_pairs={{1,2},{3,4},{5,6},{7,8},{9,10},{11,12},{13,14},{15,16},{17,18},{19... | collective-permute-start | bytes 393224 | tf_op jit(solution)/shard_map/ppermute | solution.py:469
  38.9 0.0 copy-start
  38.9 0.0 copy-start.5
  38.9 8.0 %shard_map.118 = (bf16[2,128,1024]{2,1,0:T(8,128)(2,1)S(1)}, bf16[2,128,1024]{2,1,0:T(8,128)(2,1)S(1)}, f32[128,1024]{1,0:T(8,128)S(1)}, bf16[128,1024]{1,0:T(8,128)(2,1)S(1)}, bf16[128,1024]{1,0:T(8,128)(2,1)S(1)}) custom-call(bf16[256,1024]{1,0:T(8,128)(2,1)S(1)} %get-tuple-element.42.k_ref, bf16[256,1024]{1,0:T(8,128)(2,1)S(1)} %get-tuple-element.43.v_ref, ...), custom_call_target="tpu_custom_call" | custom-call | flops 6000000000 | bytes 9830400 | tf_op jit(solution)/shard_map/pallas_call | solution.py:44
  46.9 0.0 collective-permute-done.4.got_a
  46.9 0.0 collective-permute-done.5.got_b
  47.0 0.2 shard_map.119
  47.2 0.0 copy-done
  47.2 0.0 copy-done.5
  47.2 0.0 copy-start.1
  47.2 0.0 copy-start.4
  47.2 2.1 %shard_map.120 = (bf16[512,1024]{1,0:T(8,128)(2,1)}, bf16[64,1024]{1,0:T(8,128)(2,1)S(1)}) custom-call(bf16[512,1024]{1,0:T(8,128)(2,1)S(1)} %bitcast.9, bf16[2,128,1024]{2,1,0:T(8,128)(2,1)S(1)} %get-tuple-element.46.ae_ref, bf16[2,128,1024]{2,1,0:T(8,128)(2,1)S(1)} %get-tuple-element.49.am_ref, bf16[1024,1024]{1,0:T(8,128)(2,1)S(1)} %copy-done, ...), custom_call_target="tpu_custom_call" | custom-call | flops 1073741824 | bytes 4325376 | tf_op jit(solution)/shard_map/pallas_call | solution.py:44
  49.4 3.6 %collective-permute-start.7 = (bf16[64,1024]{1,0:T(8,128)(2,1)S(1)}, bf16[64,1024]{1,0:T(8,128)(2,1)S(1)}, u32[]{:S(2)}, u32[]{:S(2)}) collective-permute-start(bf16[64,1024]{1,0:T(8,128)(2,1)S(1)} %get-tuple-element.62), channel_id=1, source_target_pairs={{64,128},{128,64},{65,129},{129,65},{66,130},{130,66},{67,131},{13... | collective-permute-start | bytes 393224 | tf_op jit(solution)/shard_map/ppermute | solution.py:484
  53.0 0.1 collective-permute-start.6
  53.1 0.0 copy-done.1
  53.2 0.0 copy-done.4
  53.2 2.8 %shard_map.121 = (bf16[512,1024]{1,0:T(8,128)(2,1)}, f32[128,1024]{1,0:T(8,128)S(1)}) custom-call(bf16[512,1024]{1,0:T(8,128)(2,1)S(1)} %bitcast.7, bf16[2,128,1024]{2,1,0:T(8,128)(2,1)S(1)} %get-tuple-element.55.de_ref, bf16[2,128,1024]{2,1,0:T(8,128)(2,1)S(1)} %get-tuple-element.56.dm_ref, bf16[1024,1024]{1,0:T(8,128)(2,1)S(1)} %copy-done.1, ...), custom_call_target="tpu_custom_call" | custom-call | flops 1073741824 | bytes 9175040 | tf_op jit(solution)/shard_map/pallas_call | solution.py:44
  56.0 0.3 collective-permute-done.7.got_b
  56.3 1.8 %collective-permute-done.6.got_a = bf16[64,1024]{1,0:T(8,128)(2,1)S(1)} collective-permute-done((bf16[64,1024]{1,0:T(8,128)(2,1)S(1)}, bf16[64,1024]{1,0:T(8,128)(2,1)S(1)}, u32[]{:S(2)}, u32[]{:S(2)}) %collective-permute-start.6) | collective-permute-done | bytes 131104 | tf_op jit(solution)/shard_map/ppermute | solution.py:477
  58.1 0.7 %shard_map.122 = bf16[128,1024]{1,0:T(8,128)(2,1)} custom-call(f32[128,1024]{1,0:T(8,128)S(1)} %get-tuple-element.60.own_ref, bf16[64,1024]{1,0:T(8,128)(2,1)S(1)} %collective-permute-done.6.got_a, bf16[64,1024]{1,0:T(8,128)(2,1)S(1)} %collective-permute-done.7.got_b), custom_call_target="tpu_custom_call" | custom-call | flops 1000000 | bytes 786432 | tf_op jit(solution)/shard_map/pallas_call | solution.py:44
Async XLA Ops:
  1.6 11.1 %collective-permute-start = (bf16[64,1024]{1,0:T(8,128)(2,1)S(1)}, bf16[64,1024]{1,0:T(8,128)(2,1)S(1)}, u32[]{:S(2)}, u32[]{:S(2)}) collective-permute-start(bf16[64,1024]{1,0:T(8,128)(2,1)S(1)} %get-tuple-element.33.own_a), channel_id=1, source_target_pairs={{0,64},{128,192},{64,0},{192,128},{1,65},{129,193},{65,1},{193,129... | collective-permute-start | bytes 393224 | tf_op jit(solution)/shard_map/ppermute | solution.py:433
  3.9 6.9 %copy-start.6 = (s32[12,16,32]{2,1,0:T(8,128)S(1)}, s32[12,16,32]{2,1,0:T(8,128)}, u32[]{:S(2)}) copy-start(s32[12,16,32]{2,1,0:T(8,128)} %edges_ref.1) | copy-start | bytes 73732
  3.9 6.9 %copy-start.7 = (s32[12,16,32]{2,1,0:T(8,128)S(1)}, s32[12,16,32]{2,1,0:T(8,128)}, u32[]{:S(2)}) copy-start(s32[12,16,32]{2,1,0:T(8,128)} %mask_ref.1) | copy-start | bytes 73732
  8.1 6.9 %collective-permute-start.1 = (bf16[64,1024]{1,0:T(8,128)(2,1)S(1)}, bf16[64,1024]{1,0:T(8,128)(2,1)S(1)}, u32[]{:S(2)}, u32[]{:S(2)}) collective-permute-start(bf16[64,1024]{1,0:T(8,128)(2,1)S(1)} %get-tuple-element.35), channel_id=1, source_target_pairs={{64,128},{128,64},{65,129},{129,65},{66,130},{130,66},{67,131},{13... | collective-permute-start | bytes 393224 | tf_op jit(solution)/shard_map/ppermute | solution.py:445
  10.8 11.8 %copy-start.2 = (bf16[1024,1024]{1,0:T(8,128)(2,1)S(1)}, bf16[1024,1024]{1,0:T(8,128)(2,1)}, u32[]{:S(2)}) copy-start(bf16[1024,1024]{1,0:T(8,128)(2,1)} %wk_ref.7) | copy-start | bytes 6291460
  10.8 11.8 %copy-start.3 = (bf16[1024,1024]{1,0:T(8,128)(2,1)S(1)}, bf16[1024,1024]{1,0:T(8,128)(2,1)}, u32[]{:S(2)}) copy-start(bf16[1024,1024]{1,0:T(8,128)(2,1)} %wv_ref.7) | copy-start | bytes 6291460
  15.3 8.5 %collective-permute-start.2 = (bf16[64,1024]{1,0:T(8,128)(2,1)S(1)}, bf16[64,1024]{1,0:T(8,128)(2,1)S(1)}, u32[]{:S(2)}, u32[]{:S(2)}) collective-permute-start(bf16[64,1024]{1,0:T(8,128)(2,1)S(1)} %get-tuple-element.39), channel_id=1, source_target_pairs={{0,1},{2,3},{4,5},{6,7},{8,9},{10,11},{12,13},{14,15},{16,17},{18,... | collective-permute-start | bytes 393224 | tf_op jit(solution)/shard_map/ppermute | solution.py:455
  15.4 9.8 %collective-permute-start.3 = (bf16[64,1024]{1,0:T(8,128)(2,1)S(1)}, bf16[64,1024]{1,0:T(8,128)(2,1)S(1)}, u32[]{:S(2)}, u32[]{:S(2)}) collective-permute-start(bf16[64,1024]{1,0:T(8,128)(2,1)S(1)} %get-tuple-element.40), channel_id=1, source_target_pairs={{1,2},{3,4},{5,6},{7,8},{9,10},{11,12},{13,14},{15,16},{17,18},{19... | collective-permute-start | bytes 393224 | tf_op jit(solution)/shard_map/ppermute | solution.py:456
  33.5 13.5 %collective-permute-start.4 = (bf16[64,1024]{1,0:T(8,128)(2,1)S(1)}, bf16[64,1024]{1,0:T(8,128)(2,1)S(1)}, u32[]{:S(2)}, u32[]{:S(2)}) collective-permute-start(bf16[64,1024]{1,0:T(8,128)(2,1)S(1)} %get-tuple-element.51), channel_id=1, source_target_pairs={{0,1},{2,3},{4,5},{6,7},{8,9},{10,11},{12,13},{14,15},{16,17},{18,... | collective-permute-start | bytes 393224 | tf_op jit(solution)/shard_map/ppermute | solution.py:468
  33.6 13.4 %collective-permute-start.5 = (bf16[64,1024]{1,0:T(8,128)(2,1)S(1)}, bf16[64,1024]{1,0:T(8,128)(2,1)S(1)}, u32[]{:S(2)}, u32[]{:S(2)}) collective-permute-start(bf16[64,1024]{1,0:T(8,128)(2,1)S(1)} %get-tuple-element.52), channel_id=1, source_target_pairs={{1,2},{3,4},{5,6},{7,8},{9,10},{11,12},{13,14},{15,16},{17,18},{19... | collective-permute-start | bytes 393224 | tf_op jit(solution)/shard_map/ppermute | solution.py:469
  38.9 8.3 %copy-start = (bf16[1024,1024]{1,0:T(8,128)(2,1)S(1)}, bf16[1024,1024]{1,0:T(8,128)(2,1)}, u32[]{:S(2)}) copy-start(bf16[1024,1024]{1,0:T(8,128)(2,1)} %wo_ref.1) | copy-start | bytes 6291460
  38.9 8.3 %copy-start.5 = (bf16[16,32,1024]{2,1,0:T(8,128)(2,1)S(1)}, bf16[16,32,1024]{2,1,0:T(8,128)(2,1)}, u32[]{:S(2)}) copy-start(bf16[16,32,1024]{2,1,0:T(8,128)(2,1)} %param.9) | copy-start | bytes 3145732
  47.2 5.9 %copy-start.1 = (bf16[1024,1024]{1,0:T(8,128)(2,1)S(1)}, bf16[1024,1024]{1,0:T(8,128)(2,1)}, u32[]{:S(2)}) copy-start(bf16[1024,1024]{1,0:T(8,128)(2,1)} %wq_ref.1) | copy-start | bytes 6291460
  47.2 5.9 %copy-start.4 = (bf16[16,32,1024]{2,1,0:T(8,128)(2,1)S(1)}, bf16[16,32,1024]{2,1,0:T(8,128)(2,1)}, u32[]{:S(2)}) copy-start(bf16[16,32,1024]{2,1,0:T(8,128)(2,1)} %param.17) | copy-start | bytes 3145732
  49.4 6.9 %collective-permute-start.7 = (bf16[64,1024]{1,0:T(8,128)(2,1)S(1)}, bf16[64,1024]{1,0:T(8,128)(2,1)S(1)}, u32[]{:S(2)}, u32[]{:S(2)}) collective-permute-start(bf16[64,1024]{1,0:T(8,128)(2,1)S(1)} %get-tuple-element.62), channel_id=1, source_target_pairs={{64,128},{128,64},{65,129},{129,65},{66,130},{130,66},{67,131},{13... | collective-permute-start | bytes 393224 | tf_op jit(solution)/shard_map/ppermute | solution.py:484
  53.0 5.1 %collective-permute-start.6 = (bf16[64,1024]{1,0:T(8,128)(2,1)S(1)}, bf16[64,1024]{1,0:T(8,128)(2,1)S(1)}, u32[]{:S(2)}, u32[]{:S(2)}) collective-permute-start(bf16[64,1024]{1,0:T(8,128)(2,1)S(1)} %get-tuple-element.61), channel_id=1, source_target_pairs={{0,64},{128,192},{64,0},{192,128},{1,65},{129,193},{65,1},{193,129... | collective-permute-start | bytes 393224 | tf_op jit(solution)/shard_map/ppermute | solution.py:477

commit v4 on v3

--- a/solution.py
+++ b/solution.py
@@ -161,27 +161,36 @@
         send_a[:, lanes], send_b[:, lanes] = sort_pair("lon", mid[:BLOCK], mid[3 * BLOCK :])
 
 
-def pair_kernel(mid_ref, wk_ref, wv_ref, k_ref, v_ref):
-    for j in range(0, mid_ref.shape[-1], 256):
-        lanes = slice(j, j + 256)
-        k_ref[:, lanes] = mm(mid_ref[...], wk_ref[:, lanes], NN).astype(BF)
-        v_ref[:, lanes] = mm(mid_ref[...], wv_ref[:, lanes], NN).astype(BF)
-
-
-def spread(block):
-    head = lax.broadcasted_iota(jnp.int32, (1, WIDE), 1) // HEAD
-    return jnp.concatenate(
-        [block * jnp.where(head == h, 1.0, 0.0).astype(BF) for h in range(GROUP)], axis=0
-    )
+def half_masks():
+    head = lax.broadcasted_iota(jnp.int32, (1, 2 * HEAD), 1) // HEAD
+    return [jnp.where(head == h, 1.0, 0.0).astype(BF) for h in range(2)]
+
+
+def spread_pair(block):
+    return jnp.concatenate([block * m for m in half_masks()], axis=0)
+
+
+def spread_group(block):
+    zero = jnp.zeros((block.shape[0], 2 * HEAD), BF)
+    low, high = block[:, : 2 * HEAD], block[:, 2 * HEAD :]
+    masks = half_masks()
+    rows = [jnp.concatenate([low * m, zero], axis=1) for m in masks]
+    rows += [jnp.concatenate([zero, high * m], axis=1) for m in masks]
+    return jnp.concatenate(rows, axis=0)
+
+
+def pair_lanes(i):
+    return slice(i * 2 * HEAD, (i + 1) * 2 * HEAD), slice(i * 2 * POINTS, (i + 1) * 2 * POINTS)
 
 
 def score(keys, values, q4, d4, bufs):
     s_ref, d_ref, qs_ref, gs_ref = bufs[:4]
-    queries, grads = spread(q4), spread(d4)
-    qs_ref[...] = queries
-    gs_ref[...] = grads
-    s_ref[...] = mm(keys, queries, NT)
-    d_ref[...] = mm(values, grads, NT)
+    for i in range(GROUP // 2):
+        lanes, at = pair_lanes(i)
+        qs_ref[at, :] = spread_pair(q4[:, lanes])
+        gs_ref[at, :] = spread_pair(d4[:, lanes])
+        s_ref[:, at] = mm(keys[:, lanes], qs_ref[at, :], NT)
+        d_ref[:, at] = mm(values[:, lanes], gs_ref[at, :], NT)
 
 
 def soften(bias, bufs):
@@ -204,66 +213,83 @@
 
 def gather_grads(keys, values, bufs):
     _, _, qs_ref, gs_ref, pw, sw, pt, st = bufs
-    att = mm(pt[...], spread(values), TN).astype(BF)
-    dq = mm(st[...], spread(keys), TN).astype(BF)
-    dk = mm(sw[...], qs_ref[...], NN)
-    dv = mm(pw[...], gs_ref[...], NN)
-    return att, dq, dk, dv
+    att = mm(pt[...], spread_group(values), TN).astype(BF)
+    dq = mm(st[...], spread_group(keys), TN).astype(BF)
+    dk, dv = [], []
+    for i in range(GROUP // 2):
+        _, at = pair_lanes(i)
+        dk.append(mm(sw[:, at], qs_ref[at, :], NN))
+        dv.append(mm(pw[:, at], gs_ref[at, :], NN))
+    return att, dq, jnp.concatenate(dk, axis=1), jnp.concatenate(dv, axis=1)
 
 
 ITEM_SCRATCH = (
     (pltpu.VMEM((NODES, GROUP * POINTS), F32),) * 2
-    + (pltpu.VMEM((GROUP * POINTS, WIDE), BF),) * 2
+    + (pltpu.VMEM((GROUP * POINTS, 2 * HEAD), BF),) * 2
     + (pltpu.VMEM((NODES, GROUP * POINTS), BF),) * 2
     + (pltpu.VMEM((GROUP * NODES, POINTS), BF),) * 2
 )
 PAIR_SCRATCH = ITEM_SCRATCH * 2
 
 
-def attend_pair(tiles, load, store, q_ref, da_ref, bias_ref, scratch):
+def attend(tiles, load, store, q_ref, da_ref, bias_ref, scratch):
     n = len(ITEM_SCRATCH)
     bufs = (scratch[:n], scratch[n:])
-    groups = HEADS // GROUP
-
-    def lanes_of(g):
-        return pl.ds(pl.multiple_of(g * WIDE, WIDE), WIDE)
-
-    def do_score(g, i):
-        lanes = lanes_of(g)
+    items = [
+        (i, t, slice(j, j + WIDE))
+        for j in range(0, HEADS * HEAD, WIDE)
+        for i, t in enumerate(tiles)
+    ]
+
+    def do_score(k):
+        i, t, lanes = items[k]
         keys, values = load(i, lanes)
-        t = tiles[i]
-        score(keys, values, q_ref[t, :, lanes], da_ref[t, :, lanes], bufs[i])
-
-    def do_grads(g, i):
-        lanes = lanes_of(g)
+        score(keys, values, q_ref[t, :, lanes], da_ref[t, :, lanes], bufs[k % 2])
+
+    def do_grads(k):
+        i, _, lanes = items[k]
         keys, values = load(i, lanes)
-        store(i, lanes, *gather_grads(keys, values, bufs[i]))
-
-    for ref in bufs[1][2:]:
-        ref[...] = jnp.zeros_like(ref)
-    do_score(0, 0)
-
-    def step(g, carry):
-        do_grads(jnp.maximum(g - 1, 0), 1)
-        soften(bias_ref[tiles[0]], bufs[0])
-        do_score(g, 1)
-        do_grads(g, 0)
-        soften(bias_ref[tiles[1]], bufs[1])
-        do_score(jnp.minimum(g + 1, groups - 1), 0)
-        return carry
-
-    lax.fori_loop(0, groups, step, 0)
-    do_grads(groups - 1, 1)
+        store(i, lanes, *gather_grads(keys, values, bufs[k % 2]))
+
+    do_score(0)
+    for k, (_, t, _) in enumerate(items):
+        if k > 0:
+            do_grads(k - 1)
+        soften(bias_ref[t], bufs[k % 2])
+        if k + 1 < len(items):
+            do_score(k + 1)
+    do_grads(len(items) - 1)
+
+
+def first_kernel(
+    mid_ref, wk_ref, wv_ref, q_ref, da_ref, bias_ref,
+    k_ref, v_ref, att_ref, dq_ref, dk_ref, dv_ref, *scratch,
+):
+    for j in range(0, mid_ref.shape[-1], WIDE):
+        lanes = slice(j, j + WIDE)
+        k_ref[:, lanes] = mm(mid_ref[...], wk_ref[:, lanes], NN).astype(BF)
+        v_ref[:, lanes] = mm(mid_ref[...], wv_ref[:, lanes], NN).astype(BF)
+
+    def load(i, lanes):
+        return k_ref[:NODES, lanes], v_ref[:NODES, lanes]
+
+    def store(i, lanes, att, dq, dk, dv):
+        att_ref[:, lanes] = att
+        dq_ref[:, lanes] = dq
+        dk_ref[:, lanes] = dk
+        dv_ref[:, lanes] = dv
+
+    attend((1,), load, store, q_ref, da_ref, bias_ref, scratch)
 
 
 def edges_kernel(
-    got_a, got_b, k_ref, v_ref, wk_ref, wv_ref, q_ref, da_ref, bias_ref,
+    got_a, got_b, k_ref, v_ref, wk_ref, wv_ref, q_ref, da_ref, bias_ref, dk1_ref, dv1_ref,
     att_ref, dq_ref, dk_ref, dv_ref, send_a, send_b,
     kl, vl, dkl, dvl, *scratch,
 ):
     rim = jnp.concatenate(sort_pair("lon", got_a[...], got_b[...]), axis=0)
-    for j in range(0, rim.shape[-1], 256):
-        lanes = slice(j, j + 256)
+    for j in range(0, rim.shape[-1], WIDE):
+        lanes = slice(j, j + WIDE)
         kl[:, lanes] = mm(rim, wk_ref[:, lanes], NN).astype(BF)
         vl[:, lanes] = mm(rim, wv_ref[:, lanes], NN).astype(BF)
 
@@ -278,56 +304,54 @@
     def store(i, lanes, att, dq, dk, dv):
         att_ref[i, :, lanes] = att
         dq_ref[i, :, lanes] = dq
-        rim_at = slice(i * BLOCK, (i + 1) * BLOCK)
-        mid_at = slice(i * 2 * BLOCK, (i + 1) * 2 * BLOCK)
-        r = slice(0, BLOCK) if i == 0 else slice(2 * BLOCK, NODES)
-        m = slice(BLOCK, NODES) if i == 0 else slice(0, 2 * BLOCK)
-        dkl[rim_at, lanes] = (dk[r] * (1.0 / SCALE)).astype(BF)
-        dvl[rim_at, lanes] = (dv[r] * (1.0 / SCALE)).astype(BF)
-        dk_ref[mid_at, lanes] = dk[m]
-        dv_ref[mid_at, lanes] = dv[m]
-
-    attend_pair((0, 3), load, store, q_ref, da_ref, bias_ref, scratch)
-    for j in range(0, rim.shape[-1], 256):
-        lanes = slice(j, j + 256)
+        rows = slice(i * BLOCK, (i + 1) * BLOCK)
+        for grad, rim, so_far, out in ((dk, dkl, dk1_ref, dk_ref), (dv, dvl, dv1_ref, dv_ref)):
+            if i == 0:
+                rim[rows, lanes] = (grad[:BLOCK] * (1.0 / SCALE)).astype(BF)
+                out[: 2 * BLOCK, lanes] = grad[BLOCK:] + so_far[: 2 * BLOCK, lanes]
+            else:
+                rim[rows, lanes] = (grad[2 * BLOCK :] * (1.0 / SCALE)).astype(BF)
+                out[2 * BLOCK : 3 * BLOCK, lanes] = grad[:BLOCK] + so_far[2 * BLOCK :, lanes]
+                out[3 * BLOCK :, lanes] = grad[BLOCK : 2 * BLOCK]
+
+    attend((0, 3), load, store, q_ref, da_ref, bias_ref, scratch)
+    for j in range(0, rim.shape[-1], WIDE):
+        lanes = slice(j, j + WIDE)
         part = mm(dkl[...], wk_ref[lanes, :], NT) + mm(dvl[...], wv_ref[lanes, :], NT)
         send_a[:, lanes], send_b[:, lanes] = sort_pair(
             "lon", part[:BLOCK].astype(BF), part[BLOCK:].astype(BF)
         )
 
 
-def middle_kernel(
+def last_kernel(
     k_ref, v_ref, wk_ref, wv_ref, q_ref, da_ref, bias_ref, dk_ref, dv_ref,
     att_ref, dq_ref, part_ref, dko_ref, dvo_ref,
     dks, dvs, *scratch,
 ):
-    dks[...] = dk_ref[...]
-    dvs[...] = dv_ref[...]
-
     def load(i, lanes):
-        at = slice(i * BLOCK, i * BLOCK + NODES)
-        return k_ref[at, lanes], v_ref[at, lanes]
+        return k_ref[BLOCK:, lanes], v_ref[BLOCK:, lanes]
 
     def store(i, lanes, att, dq, dk, dv):
-        at = slice(i * BLOCK, i * BLOCK + NODES)
-        att_ref[i, :, lanes] = att
-        dq_ref[i, :, lanes] = dq
-        dks[at, lanes] += dk
-        dvs[at, lanes] += dv
-
-    attend_pair((1, 2), load, store, q_ref, da_ref, bias_ref, scratch)
+        att_ref[:, lanes] = att
+        dq_ref[:, lanes] = dq
+        for grad, so_far, out in ((dk, dk_ref, dks), (dv, dv_ref, dvs)):
+            out[:BLOCK, lanes] = (so_far[:BLOCK, lanes] * (1.0 / SCALE)).astype(BF)
+            total = grad + so_far[BLOCK:, lanes]
+            out[BLOCK:, lanes] = (total * (1.0 / SCALE)).astype(BF)
+
+    attend((2,), load, store, q_ref, da_ref, bias_ref, scratch)
     row = lax.broadcasted_iota(jnp.int32, (MIDDLE, MIDDLE), 0)
     src = lax.broadcasted_iota(jnp.int32, (MIDDLE, MIDDLE), 1)
     nodes = jnp.where(
         row < BLOCK, row, jnp.where(row < 2 * BLOCK, row + 2 * BLOCK, row - BLOCK)
     )
     pick = jnp.where(src == node_of(nodes), 1.0, 0.0).astype(BF)
-    dk = mm(pick, (dks[...] * (1.0 / SCALE)).astype(BF), NN).astype(BF)
-    dv = mm(pick, (dvs[...] * (1.0 / SCALE)).astype(BF), NN).astype(BF)
+    dk = mm(pick, dks[...], NN).astype(BF)
+    dv = mm(pick, dvs[...], NN).astype(BF)
     dko_ref[...] = dk[2 * BLOCK :]
     dvo_ref[...] = dv[2 * BLOCK :]
-    for j in range(0, part_ref.shape[-1], 256):
-        lanes = slice(j, j + 256)
+    for j in range(0, part_ref.shape[-1], WIDE):
+        lanes = slice(j, j + WIDE)
         part_ref[:, lanes] = mm(dk[: 2 * BLOCK], wk_ref[lanes, :], NT) + mm(
             dv[: 2 * BLOCK], wv_ref[lanes, :], NT
         )
@@ -352,8 +376,8 @@
         )
 
 
-def emit(res_ref, rows_e, rows_m, w_ref, dims, out_hbm, out_scr, sem):
-    rows = jnp.concatenate([rows_e[0], rows_m[0], rows_m[1], rows_e[1]], axis=0)
+def emit(res_ref, edge, first, last, w_ref, dims, out_hbm, out_scr, sem):
+    rows = jnp.concatenate([edge[0], first[...], last[...], edge[1]], axis=0)
     copies = []
     for i, j in enumerate(range(0, out_scr.shape[-1], 256)):
         lanes = slice(j, j + 256)
@@ -368,18 +392,18 @@
 
 
 def layer_out_kernel(
-    x_ref, ae_ref, am_ref, wo_ref, piece_ref, out_hbm, pass_ref, out_scr, sem
+    x_ref, ae_ref, af_ref, al_ref, wo_ref, piece_ref, out_hbm, pass_ref, out_scr, sem
 ):
     pass_ref[...] = piece_ref[...]
-    for copy in emit(x_ref, ae_ref, am_ref, wo_ref, NN, out_hbm, out_scr, sem):
+    for copy in emit(x_ref, ae_ref, af_ref, al_ref, wo_ref, NN, out_hbm, out_scr, sem):
         copy.wait()
 
 
 def grid_grad_kernel(
-    c_ref, de_ref, dm_ref, wq_ref, dk_ref, dv_ref, wk_ref, wv_ref, got_a, got_b,
+    c_ref, de_ref, df_ref, dl_ref, wq_ref, dk_ref, dv_ref, wk_ref, wv_ref, got_a, got_b,
     grad_hbm, own_ref, out_scr, sem,
 ):
-    copies = emit(c_ref, de_ref, dm_ref, wq_ref, NT, grad_hbm, out_scr, sem)
+    copies = emit(c_ref, de_ref, df_ref, dl_ref, wq_ref, NT, grad_hbm, out_scr, sem)
     pick = rim_pick(BLOCK, 2 * BLOCK)
     rims = jnp.concatenate(sort_pair("lon", got_a[...], got_b[...]), axis=0)
     for j in range(0, own_ref.shape[-1], 256):
@@ -454,37 +478,41 @@
     )
     edge_a = lax.ppermute(edge_a, "lon", lon_a)
     edge_b = lax.ppermute(edge_b, "lon", lon_b)
-    k, v = call(
-        pair_kernel, (mid, w_key, w_value), [((MIDDLE, width), BF)] * 2,
-        2 * MIDDLE * product,
-    )
-    half = ((2, POINTS, width), BF)
+    rows, total = ((POINTS, width), BF), ((MIDDLE, width), F32)
+    k, v, att_f, dq_f, dk, dv = call(
+        first_kernel, (mid, w_key, w_value, q, da, bias),
+        [((MIDDLE, width), BF)] * 2 + [rows] * 2 + [((NODES, width), F32)] * 2,
+        4 * 10**9,
+        PAIR_SCRATCH,
+    )
+    both = ((2, POINTS, width), BF)
     att_e, dq_e, dk, dv, edge_a, edge_b = call(
-        edges_kernel, (edge_a, edge_b, k, v, w_key, w_value, q, da, bias),
-        [half, half] + [((MIDDLE, width), F32)] * 2 + [piece] * 2,
+        edges_kernel,
+        (edge_a, edge_b, k, v, w_key, w_value, q, da, bias, dk, dv),
+        [both] * 2 + [total] * 2 + [piece] * 2,
         6 * 10**9,
         (pltpu.VMEM((2 * BLOCK, width), BF),) * 4 + PAIR_SCRATCH,
     )
     edge_a = lax.ppermute(edge_a, "lon", lon_a)
     edge_b = lax.ppermute(edge_b, "lon", lon_b)
-    att_m, dq_m, part, dk_own, dv_own = call(
-        middle_kernel, (k, v, w_key, w_value, q, da, bias, dk, dv),
-        [half, half, ((2 * BLOCK, width), F32)] + [((2 * BLOCK, width), BF)] * 2,
-        6 * 10**9,
-        (pltpu.VMEM((MIDDLE, width), F32),) * 2 + PAIR_SCRATCH,
+    att_l, dq_l, part, dk_own, dv_own = call(
+        last_kernel, (k, v, w_key, w_value, q, da, bias, dk, dv),
+        [rows] * 2 + [((2 * BLOCK, width), F32)] + [((2 * BLOCK, width), BF)] * 2,
+        4 * 10**9,
+        (pltpu.VMEM((MIDDLE, width), BF),) * 2 + PAIR_SCRATCH,
     )
     send_a, send_b = call(merge_kernel, (part, edge_a, edge_b), [piece, piece], 10**8)
     got_a = lax.ppermute(send_a, "lat", lat_a)
     out_scratch = (pltpu.VMEM((points, width), BF), pltpu.SemaphoreType.DMA((4,)))
     layer_out, late_b = call(
-        layer_out_kernel, (x, att_e, att_m, w_out, send_b),
+        layer_out_kernel, (x, att_e, att_f, att_l, w_out, send_b),
         [((points, width), BF), piece],
         points * product, out_scratch, hbm_out=(0,),
     )
     got_b = lax.ppermute(late_b, "lat", lat_b)
     grid_grad, kept = call(
         grid_grad_kernel,
-        (c, dq_e, dq_m, w_query, dk_own, dv_own, w_key, w_value, edge_a, edge_b),
+        (c, dq_e, dq_f, dq_l, w_query, dk_own, dv_own, w_key, w_value, edge_a, edge_b),
         [((points, width), BF), ((2 * BLOCK, width), F32)],
         points * product, out_scratch, hbm_out=(0,),
     )

time: 59.2 us -> 52.7 us (0.89)
  Pallas kernels: 30.9 us -> 26.6 us
  waiting for transfers between devices: 5.79 us -> 4.44 us
  starting transfers between devices: 21.2 us -> 20.4 us
    pallas_call x11, Pallas kernels: 30.9 us -> 26.6 us  [call(): pl.pallas_call(kernel, in_specs=[placed(i) for i in range(len(inputs))],...]
    ppermute x2, waiting for transfers between devices: 1.35 us -> 0.01 us  [local(): edge_b = lax.ppermute(edge_b, 'lon', lon_b)]
    ppermute x2, starting transfers between devices: 12.4 us -> 11.6 us  [local(): edge_b = lax.ppermute(edge_b, 'lon', lon_b)]
  transfers between devices with their start and end apart: 8 -> 8, of which waited for: 4 -> 3; matrix products, arithmetic and copies ran while one was open for 0% -> 0% of each run, Pallas kernels for 31% -> 31%
where the time goes in v4:
time: 52.7 us; the launch traced here: 52.5 us
  Pallas kernels  26.6 us (50%)
  starting transfers between devices  20.4 us (39%)
  waiting for transfers between devices  4.44 us (8%)
  between operations  1.05 us (2%)
    pallas_call x11, Pallas kernels, call(): pl.pallas_call(kernel, in_specs=[placed(i) for i in range(len(inputs))],...  26.6 us
    ppermute x2, starting transfers between devices, local(): edge_b = lax.ppermute(edge_b, 'lon', lon_b)  11.6 us
    ppermute x2, starting transfers between devices, local(): got_b = lax.ppermute(late_b, 'lat', lat_b)  6.27 us
    ppermute x2, waiting for transfers between devices, local(): got_b = lax.ppermute(late_b, 'lat', lat_b)  2.56 us
    ppermute x2, starting transfers between devices, local(): got_a = lax.ppermute(send_a, 'lat', lat_a)  2.34 us
    ppermute x2, waiting for transfers between devices, local(): got_a = lax.ppermute(send_a, 'lat', lat_a)  1.87 us
  transfers between devices with their start and end apart: 8, of which 3 were waited for; matrix products, arithmetic and copies ran while one was open for 0% of the time, Pallas kernels for 31%

profile of v4, /device:TPU:8, one launch (start us, length us, event | category | flops | bytes accessed | tf_op | source)
XLA Modules:
  0.0 52.5 jit_solution(11171618829239319448)
XLA Ops:
  0.6 1.0 %shard_map.112 = (bf16[64,1024]{1,0:T(8,128)(2,1)S(1)}, bf16[64,1024]{1,0:T(8,128)(2,1)S(1)}) custom-call(bf16[128,1024]{1,0:T(8,128)(2,1)} %bitcast.10), custom_call_target="tpu_custom_call" | custom-call | flops 100000 | bytes 262144 | tf_op jit(solution)/shard_map/pallas_call | solution.py:44
  1.6 2.2 %collective-permute-start = (bf16[64,1024]{1,0:T(8,128)(2,1)S(1)}, bf16[64,1024]{1,0:T(8,128)(2,1)S(1)}, u32[]{:S(2)}, u32[]{:S(2)}) collective-permute-start(bf16[64,1024]{1,0:T(8,128)(2,1)S(1)} %get-tuple-element.37.own_a), channel_id=1, source_target_pairs={{0,64},{128,192},{64,0},{192,128},{1,65},{129,193},{65,1},{193,129... | collective-permute-start | bytes 393224 | tf_op jit(solution)/shard_map/ppermute | solution.py:457
  3.9 0.0 copy-start.6
  3.9 0.0 copy-start.7
  3.9 4.2 %shard_map.113 = (bf16[4,128,1024]{2,1,0:T(8,128)(2,1)S(1)}, bf16[512,1024]{1,0:T(8,128)(2,1)S(1)}, bf16[1024,1024]{1,0:T(8,128)(2,1)S(1)}, bf16[64,1024]{1,0:T(8,128)(2,1)S(1)}) custom-call(bf16[512,1024]{1,0:T(8,128)(2,1)} %bitcast.8, bf16[1024,1024]{1,0:T(8,128)(2,1)} %wq_ref.1, bf16[512,1024]{1,0:T(8,128)(2,1)} %bitcast.6, bf16[1024,1024]{1,0:T(8,128)(2,1)} %wo_ref.1, ...), custom_call_target="tpu_custom_call" | custom-call | flops 1073741824 | bytes 6422528 | tf_op jit(solution)/shard_map/pallas_call | solution.py:44
  8.1 2.6 %collective-permute-start.1 = (bf16[64,1024]{1,0:T(8,128)(2,1)S(1)}, bf16[64,1024]{1,0:T(8,128)(2,1)S(1)}, u32[]{:S(2)}, u32[]{:S(2)}) collective-permute-start(bf16[64,1024]{1,0:T(8,128)(2,1)S(1)} %get-tuple-element.39), channel_id=1, source_target_pairs={{64,128},{128,64},{65,129},{129,65},{66,130},{130,66},{67,131},{13... | collective-permute-start | bytes 393224 | tf_op jit(solution)/shard_map/ppermute | solution.py:469
  10.8 0.0 copy-done.6
  10.8 0.0 copy-done.7
  10.8 0.0 copy-start.4
  10.8 0.0 copy-start.5
  10.8 1.9 %shard_map.114 = (bf16[4,128,1024]{2,1,0:T(8,128)(2,1)S(1)}, f32[4,192,128]{2,1,0:T(8,128)S(1)}) custom-call(bf16[512,1024]{1,0:T(8,128)(2,1)S(1)} %get-tuple-element.40.c_ref, bf16[1024,1024]{1,0:T(8,128)(2,1)S(1)} %get-tuple-element.41.wo_ref, s32[12,16,32]{2,1,0:T(8,128)S(1)} %copy-done.6, s32[12,16,32]{2,1,0:T(8,128)S(1)} %copy-done.7), custom_call_target="tpu_custom_call" | custom-call | flops 1073741824 | bytes 3194880 | tf_op jit(solution)/shard_map/pallas_call | solution.py:44
  12.7 0.0 collective-permute-done.got_a
  12.7 2.3 %collective-permute-done.1.got_b = bf16[64,1024]{1,0:T(8,128)(2,1)S(1)} collective-permute-done((bf16[64,1024]{1,0:T(8,128)(2,1)S(1)}, bf16[64,1024]{1,0:T(8,128)(2,1)S(1)}, u32[]{:S(2)}, u32[]{:S(2)}) %collective-permute-start.1) | collective-permute-done | bytes 131104 | tf_op jit(solution)/shard_map/ppermute | solution.py:469
  15.0 0.3 shard_map.115
  15.3 0.1 collective-permute-start.2
  15.4 7.1 %collective-permute-start.3 = (bf16[64,1024]{1,0:T(8,128)(2,1)S(1)}, bf16[64,1024]{1,0:T(8,128)(2,1)S(1)}, u32[]{:S(2)}, u32[]{:S(2)}) collective-permute-start(bf16[64,1024]{1,0:T(8,128)(2,1)S(1)} %get-tuple-element.44), channel_id=1, source_target_pairs={{1,2},{3,4},{5,6},{7,8},{9,10},{11,12},{13,14},{15,16},{17,18},{19... | collective-permute-start | bytes 393224 | tf_op jit(solution)/shard_map/ppermute | solution.py:480
  22.5 0.0 copy-done.4
  22.5 0.0 copy-done.5
  22.5 3.4 %shard_map.116 = (bf16[256,1024]{1,0:T(8,128)(2,1)S(1)}, bf16[256,1024]{1,0:T(8,128)(2,1)S(1)}, bf16[128,1024]{1,0:T(8,128)(2,1)S(1)}, bf16[128,1024]{1,0:T(8,12...) custom-call(bf16[256,1024]{1,0:T(8,128)(2,1)S(1)} %get-tuple-element.45.mid_ref, ...), custom_call_target="tpu_custom_call" | custom-call | flops 4000000000 | bytes 7208960 | tf_op jit(solution)/shard_map/pallas_call | solution.py:44
  26.0 0.0 collective-permute-done.2.got_a
  26.0 0.0 collective-permute-done.3.got_b
  26.0 6.1 %shard_map.117 = (bf16[2,128,1024]{2,1,0:T(8,128)(2,1)S(1)}, bf16[2,128,1024]{2,1,0:T(8,128)(2,1)S(1)}, f32[256,1024]{1,0:T(8,128)S(1)}, f32[256,1024]{1,0:T(8,1...) custom-call(bf16[64,1024]{1,0:T(8,128)(2,1)S(1)} %collective-permute-done.2.got_a, ...), custom_call_target="tpu_custom_call" | custom-call | flops 6000000000 | bytes 9568256 | tf_op jit(solution)/shard_map/pallas_call | solution.py:44
  32.1 0.1 collective-permute-start.4
  32.2 4.5 %collective-permute-start.5 = (bf16[64,1024]{1,0:T(8,128)(2,1)S(1)}, bf16[64,1024]{1,0:T(8,128)(2,1)S(1)}, u32[]{:S(2)}, u32[]{:S(2)}) collective-permute-start(bf16[64,1024]{1,0:T(8,128)(2,1)S(1)} %get-tuple-element.59), channel_id=1, source_target_pairs={{1,2},{3,4},{5,6},{7,8},{9,10},{11,12},{13,14},{15,16},{17,18},{19... | collective-permute-start | bytes 393224 | tf_op jit(solution)/shard_map/ppermute | solution.py:497
  36.7 0.0 copy-start
  36.7 0.0 copy-start.3
  36.7 3.7 %shard_map.118 = (bf16[128,1024]{1,0:T(8,128)(2,1)S(1)}, bf16[128,1024]{1,0:T(8,128)(2,1)S(1)}, f32[128,1024]{1,0:T(8,128)S(1)}, bf16[128,1024]{1,0:T(8,128)(2,1)S(1)}, bf16[128,1024]{1,0:T(8,128)(2,1)S(1)}) custom-call(bf16[256,1024]{1,0:T(8,128)(2,1)S(1)} %get-tuple-element.48.k_ref, bf16[256,1024]{1,0:T(8,128)(2,1)S(1)} %get-tuple-element.49.v_ref, ...), custom_call_target="tpu_custom_call" | custom-call | flops 4000000000 | bytes 9830400 | tf_op jit(solution)/shard_map/pallas_call | solution.py:44
  40.4 0.0 collective-permute-done.4.got_a
  40.4 0.0 collective-permute-done.5.got_b
  40.4 0.2 shard_map.119
  40.7 0.0 copy-done
  40.7 0.0 copy-done.3
  40.7 0.0 copy-start.1
  40.7 0.0 copy-start.2
  40.7 2.1 %shard_map.120 = (bf16[512,1024]{1,0:T(8,128)(2,1)}, bf16[64,1024]{1,0:T(8,128)(2,1)S(1)}) custom-call(bf16[512,1024]{1,0:T(8,128)(2,1)S(1)} %bitcast.9, bf16[2,128,1024]{2,1,0:T(8,128)(2,1)S(1)} %get-tuple-element.52.ae_ref, bf16[128,1024]{1,0:T(8,128)(2,1)S(1)} %get-tuple-element.53.af_ref, bf16[128,1024]{1,0:T(8,128)(2,1)S(1)} %get-tuple-element.56.al_ref, ...), custom_call_target="tpu_custom_call" | custom-call | flops 1073741824 | bytes 4325376 | tf_op jit(solution)/shard_map/pallas_call | solution.py:44
  42.9 3.7 %collective-permute-start.7 = (bf16[64,1024]{1,0:T(8,128)(2,1)S(1)}, bf16[64,1024]{1,0:T(8,128)(2,1)S(1)}, u32[]{:S(2)}, u32[]{:S(2)}) collective-permute-start(bf16[64,1024]{1,0:T(8,128)(2,1)S(1)} %get-tuple-element.70), channel_id=1, source_target_pairs={{64,128},{128,64},{65,129},{129,65},{66,130},{130,66},{67,131},{13... | collective-permute-start | bytes 393224 | tf_op jit(solution)/shard_map/ppermute | solution.py:512
  46.6 0.1 collective-permute-start.6
  46.7 0.0 copy-done.1
  46.7 0.0 copy-done.2
  46.7 2.8 %shard_map.121 = (bf16[512,1024]{1,0:T(8,128)(2,1)}, f32[128,1024]{1,0:T(8,128)S(1)}) custom-call(bf16[512,1024]{1,0:T(8,128)(2,1)S(1)} %bitcast.7, bf16[2,128,1024]{2,1,0:T(8,128)(2,1)S(1)} %get-tuple-element.62.de_ref, bf16[128,1024]{1,0:T(8,128)(2,1)S(1)} %get-tuple-element.63.df_ref, bf16[128,1024]{1,0:T(8,128)(2,1)S(1)} %get-tuple-element.64.dl_ref, ...), custom_call_target="tpu_custom_call" | custom-call | flops 1073741824 | bytes 9175040 | tf_op jit(solution)/shard_map/pallas_call | solution.py:44
  49.5 0.3 collective-permute-done.7.got_b
  49.7 1.9 %collective-permute-done.6.got_a = bf16[64,1024]{1,0:T(8,128)(2,1)S(1)} collective-permute-done((bf16[64,1024]{1,0:T(8,128)(2,1)S(1)}, bf16[64,1024]{1,0:T(8,128)(2,1)S(1)}, u32[]{:S(2)}, u32[]{:S(2)}) %collective-permute-start.6) | collective-permute-done | bytes 131104 | tf_op jit(solution)/shard_map/ppermute | solution.py:505
  51.6 0.7 %shard_map.122 = bf16[128,1024]{1,0:T(8,128)(2,1)} custom-call(f32[128,1024]{1,0:T(8,128)S(1)} %get-tuple-element.68.own_ref, bf16[64,1024]{1,0:T(8,128)(2,1)S(1)} %collective-permute-done.6.got_a, bf16[64,1024]{1,0:T(8,128)(2,1)S(1)} %collective-permute-done.7.got_b), custom_call_target="tpu_custom_call" | custom-call | flops 1000000 | bytes 786432 | tf_op jit(solution)/shard_map/pallas_call | solution.py:44
Async XLA Ops:
  1.6 11.1 %collective-permute-start = (bf16[64,1024]{1,0:T(8,128)(2,1)S(1)}, bf16[64,1024]{1,0:T(8,128)(2,1)S(1)}, u32[]{:S(2)}, u32[]{:S(2)}) collective-permute-start(bf16[64,1024]{1,0:T(8,128)(2,1)S(1)} %get-tuple-element.37.own_a), channel_id=1, source_target_pairs={{0,64},{128,192},{64,0},{192,128},{1,65},{129,193},{65,1},{193,129... | collective-permute-start | bytes 393224 | tf_op jit(solution)/shard_map/ppermute | solution.py:457
  3.9 6.9 %copy-start.6 = (s32[12,16,32]{2,1,0:T(8,128)S(1)}, s32[12,16,32]{2,1,0:T(8,128)}, u32[]{:S(2)}) copy-start(s32[12,16,32]{2,1,0:T(8,128)} %edges_ref.1) | copy-start | bytes 73732
  3.9 6.9 %copy-start.7 = (s32[12,16,32]{2,1,0:T(8,128)S(1)}, s32[12,16,32]{2,1,0:T(8,128)}, u32[]{:S(2)}) copy-start(s32[12,16,32]{2,1,0:T(8,128)} %mask_ref.1) | copy-start | bytes 73732
  8.1 6.9 %collective-permute-start.1 = (bf16[64,1024]{1,0:T(8,128)(2,1)S(1)}, bf16[64,1024]{1,0:T(8,128)(2,1)S(1)}, u32[]{:S(2)}, u32[]{:S(2)}) collective-permute-start(bf16[64,1024]{1,0:T(8,128)(2,1)S(1)} %get-tuple-element.39), channel_id=1, source_target_pairs={{64,128},{128,64},{65,129},{129,65},{66,130},{130,66},{67,131},{13... | collective-permute-start | bytes 393224 | tf_op jit(solution)/shard_map/ppermute | solution.py:469
  10.8 11.8 %copy-start.4 = (bf16[1024,1024]{1,0:T(8,128)(2,1)S(1)}, bf16[1024,1024]{1,0:T(8,128)(2,1)}, u32[]{:S(2)}) copy-start(bf16[1024,1024]{1,0:T(8,128)(2,1)} %wk_ref.7) | copy-start | bytes 6291460
  10.8 11.8 %copy-start.5 = (bf16[1024,1024]{1,0:T(8,128)(2,1)S(1)}, bf16[1024,1024]{1,0:T(8,128)(2,1)}, u32[]{:S(2)}) copy-start(bf16[1024,1024]{1,0:T(8,128)(2,1)} %wv_ref.7) | copy-start | bytes 6291460
  15.3 10.7 %collective-permute-start.2 = (bf16[64,1024]{1,0:T(8,128)(2,1)S(1)}, bf16[64,1024]{1,0:T(8,128)(2,1)S(1)}, u32[]{:S(2)}, u32[]{:S(2)}) collective-permute-start(bf16[64,1024]{1,0:T(8,128)(2,1)S(1)} %get-tuple-element.43), channel_id=1, source_target_pairs={{0,1},{2,3},{4,5},{6,7},{8,9},{10,11},{12,13},{14,15},{16,17},{18,... | collective-permute-start | bytes 393224 | tf_op jit(solution)/shard_map/ppermute | solution.py:479
  15.4 10.6 %collective-permute-start.3 = (bf16[64,1024]{1,0:T(8,128)(2,1)S(1)}, bf16[64,1024]{1,0:T(8,128)(2,1)S(1)}, u32[]{:S(2)}, u32[]{:S(2)}) collective-permute-start(bf16[64,1024]{1,0:T(8,128)(2,1)S(1)} %get-tuple-element.44), channel_id=1, source_target_pairs={{1,2},{3,4},{5,6},{7,8},{9,10},{11,12},{13,14},{15,16},{17,18},{19... | collective-permute-start | bytes 393224 | tf_op jit(solution)/shard_map/ppermute | solution.py:480
  32.1 8.3 %collective-permute-start.4 = (bf16[64,1024]{1,0:T(8,128)(2,1)S(1)}, bf16[64,1024]{1,0:T(8,128)(2,1)S(1)}, u32[]{:S(2)}, u32[]{:S(2)}) collective-permute-start(bf16[64,1024]{1,0:T(8,128)(2,1)S(1)} %get-tuple-element.58), channel_id=1, source_target_pairs={{0,1},{2,3},{4,5},{6,7},{8,9},{10,11},{12,13},{14,15},{16,17},{18,... | collective-permute-start | bytes 393224 | tf_op jit(solution)/shard_map/ppermute | solution.py:496
  32.2 8.3 %collective-permute-start.5 = (bf16[64,1024]{1,0:T(8,128)(2,1)S(1)}, bf16[64,1024]{1,0:T(8,128)(2,1)S(1)}, u32[]{:S(2)}, u32[]{:S(2)}) collective-permute-start(bf16[64,1024]{1,0:T(8,128)(2,1)S(1)} %get-tuple-element.59), channel_id=1, source_target_pairs={{1,2},{3,4},{5,6},{7,8},{9,10},{11,12},{13,14},{15,16},{17,18},{19... | collective-permute-start | bytes 393224 | tf_op jit(solution)/shard_map/ppermute | solution.py:497
  36.7 4.0 %copy-start = (bf16[1024,1024]{1,0:T(8,128)(2,1)S(1)}, bf16[1024,1024]{1,0:T(8,128)(2,1)}, u32[]{:S(2)}) copy-start(bf16[1024,1024]{1,0:T(8,128)(2,1)} %wo_ref.1) | copy-start | bytes 6291460
  36.7 4.0 %copy-start.3 = (bf16[16,32,1024]{2,1,0:T(8,128)(2,1)S(1)}, bf16[16,32,1024]{2,1,0:T(8,128)(2,1)}, u32[]{:S(2)}) copy-start(bf16[16,32,1024]{2,1,0:T(8,128)(2,1)} %param.9) | copy-start | bytes 3145732
  40.7 5.9 %copy-start.1 = (bf16[1024,1024]{1,0:T(8,128)(2,1)S(1)}, bf16[1024,1024]{1,0:T(8,128)(2,1)}, u32[]{:S(2)}) copy-start(bf16[1024,1024]{1,0:T(8,128)(2,1)} %wq_ref.1) | copy-start | bytes 6291460
  40.7 5.9 %copy-start.2 = (bf16[16,32,1024]{2,1,0:T(8,128)(2,1)S(1)}, bf16[16,32,1024]{2,1,0:T(8,128)(2,1)}, u32[]{:S(2)}) copy-start(bf16[16,32,1024]{2,1,0:T(8,128)(2,1)} %param.17) | copy-start | bytes 3145732
  42.9 6.9 %collective-permute-start.7 = (bf16[64,1024]{1,0:T(8,128)(2,1)S(1)}, bf16[64,1024]{1,0:T(8,128)(2,1)S(1)}, u32[]{:S(2)}, u32[]{:S(2)}) collective-permute-start(bf16[64,1024]{1,0:T(8,128)(2,1)S(1)} %get-tuple-element.70), channel_id=1, source_target_pairs={{64,128},{128,64},{65,129},{129,65},{66,130},{130,66},{67,131},{13... | collective-permute-start | bytes 393224 | tf_op jit(solution)/shard_map/ppermute | solution.py:512
  46.6 5.1 %collective-permute-start.6 = (bf16[64,1024]{1,0:T(8,128)(2,1)S(1)}, bf16[64,1024]{1,0:T(8,128)(2,1)S(1)}, u32[]{:S(2)}, u32[]{:S(2)}) collective-permute-start(bf16[64,1024]{1,0:T(8,128)(2,1)S(1)} %get-tuple-element.69), channel_id=1, source_target_pairs={{0,64},{128,192},{64,0},{192,128},{1,65},{129,193},{65,1},{193,129... | collective-permute-start | bytes 393224 | tf_op jit(solution)/shard_map/ppermute | solution.py:505

commit v5 on v4

v5 whole, which is shorter than its diff:
```python
import jax
import jax.numpy as jnp
from jax import lax
from jax.experimental import pallas as pl
from jax.experimental.pallas import tpu as pltpu
from jax.sharding import PartitionSpec as P


HEADS = 16
HEAD = 64
SLOTS = 12
REACH = 4
NEG_FILL = -1e30
SCALE = 0.125
GROUP = 4
WIDE = GROUP * HEAD

TILES = 4
POINTS = 128
BLOCK = 64
NODES = 3 * BLOCK
MIDDLE = 4 * BLOCK
HALO = 16
HALF = 48

BF = jnp.bfloat16
F32 = jnp.float32
NT = (((1,), (1,)), ((), ()))
NN = (((1,), (0,)), ((), ()))
TN = (((0,), (0,)), ((), ()))
IN_VMEM = pl.BlockSpec(memory_space=pltpu.VMEM)
IN_HBM = pl.BlockSpec(memory_space=pltpu.MemorySpace.HBM)
IN_PLACE = pl.BlockSpec(memory_space=pl.ANY)


def mm(a, b, dims):
    return lax.dot_general(a, b, dims, preferred_element_type=F32)


def call(kernel, inputs, outs, flops, scratch=(), hbm=(), loose=(), hbm_out=(), limit=16 << 20):
    moved = sum(a.size * a.dtype.itemsize for a in inputs)

    def placed(i):
        return IN_HBM if i in hbm else IN_PLACE if i in loose else IN_VMEM

    return pl.pallas_call(
        kernel,
        in_specs=[placed(i) for i in range(len(inputs))],
        out_specs=[IN_HBM if i in hbm_out else IN_VMEM for i in range(len(outs))],
        out_shape=[
            jax.ShapeDtypeStruct(s, d) if i in hbm_out else pltpu.VMEM(s, d)
            for i, (s, d) in enumerate(outs)
        ],
        scratch_shapes=list(scratch),
        compiler_params=pltpu.CompilerParams(vmem_limit_bytes=limit),
        cost_estimate=pl.CostEstimate(flops=flops, bytes_accessed=moved, transcendentals=0),
    )(
        *(
            pltpu.with_memory_space_constraint(a, pltpu.MemorySpace.HBM) if i in hbm else a
            for i, a in enumerate(inputs)
        )
    )


def to_tiles(rows):
    cut = rows.reshape(16, TILES, 8, rows.shape[-1])
    parts = (cut[:, 0], cut[:8, 1:3], cut[8:, 1:3], cut[:, 3])
    return [part.reshape(POINTS, rows.shape[-1]) for part in parts]


def from_tiles(tiles):
    n = tiles[0].shape[-1]
    upper, lower = (t.reshape(8, 2, 8, n) for t in tiles[1:3])
    left, right = (t.reshape(16, 1, 8, n) for t in (tiles[0], tiles[3]))
    middle = jnp.concatenate([upper, lower], axis=0)
    return jnp.concatenate([left, middle, right], axis=1).reshape(TILES * POINTS, n)


def select(count, dst_of_src):
    dst = lax.broadcasted_iota(jnp.int32, (count, count), 0)
    src = lax.broadcasted_iota(jnp.int32, (count, count), 1)
    return jnp.where(dst == dst_of_src(src), 1.0, 0.0).astype(BF)


def to_blocks(rows):
    return lambda i: ((i % 16) // 4) * (4 * rows) + (i // 16) * 4 + i % 4


def is_odd(axis):
    return lax.axis_index(axis) % 2 == 1


def lead_kernel(mesh_ref, a_ref, b_ref, sem):
    odd = lax.axis_index("lat") % 2
    first = pltpu.make_async_copy(mesh_ref.at[pl.ds((1 - odd) * BLOCK, BLOCK)], a_ref, sem.at[0])
    second = pltpu.make_async_copy(mesh_ref.at[pl.ds(odd * BLOCK, BLOCK)], b_ref, sem.at[1])
    first.start()
    second.start()
    first.wait()
    second.wait()


def project_q_kernel(
    x_hbm, wq_hbm, c_hbm, wo_hbm, q_ref, c_ref, wo_ref, x_scr, wq_scr, sem
):
    copies = [pltpu.make_async_copy(x_hbm, x_scr, sem.at[0])]
    width = q_ref.shape[-1]
    blocks = [slice(j, j + 256) for j in range(0, width, 256)]
    for i, lanes in enumerate(blocks):
        copies.append(
            pltpu.make_async_copy(wq_hbm.at[:, lanes], wq_scr.at[:, lanes], sem.at[1 + i])
        )
    copies.append(pltpu.make_async_copy(c_hbm, c_ref, sem.at[5]))
    copies.append(pltpu.make_async_copy(wo_hbm, wo_ref, sem.at[6]))
    for copy in copies:
        copy.start()
    copies[0].wait()
    for i, lanes in enumerate(blocks):
        copies[1 + i].wait()
        q = to_tiles(mm(x_scr[...], wq_scr[:, lanes], NN))
        for t in range(TILES):
            q_ref[t, :, lanes] = q[t].astype(BF) * SCALE
    copies[5].wait()
    copies[6].wait()


def project_d_kernel(c_ref, wo_ref, edges_ref, mask_ref, piece_ref, da_ref, bias_ref, pass_ref):
    pass_ref[...] = piece_ref[...]
    lat_start = lax.axis_index("lat") * 8
    lon_start = lax.axis_index("lon") * 16
    edges = edges_ref[...]
    row = (edges >> 10) - lat_start + REACH
    col = (edges - lon_start + REACH) & 1023
    point_row = lax.broadcasted_iota(jnp.int32, edges.shape, 1)
    point_col = lax.broadcasted_iota(jnp.int32, edges.shape, 2)
    block, inner = col >> 2, row * 4 + (col & 3)
    slot = jnp.where(
        point_col < 8,
        block * BLOCK + inner,
        jnp.where(
            point_col >= 24,
            jnp.where(block == 5, 0, block - 2) * BLOCK + inner,
            (block - 1) * HALF + inner - jnp.where(point_row < 8, 0, HALO),
        ),
    )
    slot = jnp.where(mask_ref[...] > 0, slot, -1).astype(F32).astype(BF)
    slot = slot.reshape(SLOTS * 16, 32)

    def point(lane):
        tile, i = lane >> 7, lane & 127
        outer = (tile == 0) | (tile == 3)
        row = jnp.where(outer, i >> 3, (i >> 4) + jnp.where(tile == 2, 8, 0))
        col = jnp.where(outer, (i & 7) + tile * 8, (i & 15) + 8)
        return row, col

    src = lax.broadcasted_iota(jnp.int32, (32, TILES * POINTS), 0)
    dst = lax.broadcasted_iota(jnp.int32, (32, TILES * POINTS), 1)
    pick = jnp.where(src == point(dst)[1], 1.0, 0.0).astype(BF)
    wide = mm(slot, pick, NN).reshape(SLOTS, 16, TILES * POINTS)
    lane = lax.broadcasted_iota(jnp.int32, (16, TILES * POINTS), 1)
    own_row = lax.broadcasted_iota(jnp.int32, lane.shape, 0) == point(lane)[0]
    slots = jnp.sum(jnp.where(own_row[None], wide, 0.0), axis=1)
    node = lax.broadcasted_iota(jnp.int32, (NODES, POINTS), 0).astype(F32)
    for t in range(TILES):
        at = slice(t * POINTS, (t + 1) * POINTS)
        hit = node == slots[0:1, at]
        for e in range(1, SLOTS):
            hit = hit | (node == slots[e : e + 1, at])
        bias_ref[t] = jnp.where(hit, 0.0, NEG_FILL)
    for j in range(0, da_ref.shape[-1], 256):
        lanes = slice(j, j + 256)
        d = to_tiles(mm(c_ref[...], wo_ref[lanes, :], NT))
        for t in range(TILES):
            da_ref[t, :, lanes] = d[t].astype(BF) * SCALE


def sort_pair(axis, a, b):
    odd = lax.axis_index(axis) % 2 == 1
    return jnp.where(odd, a, b), jnp.where(odd, b, a)


def assemble_kernel(half_ref, got_b, rest_ref, send_a, send_b):
    pick = select(BLOCK, to_blocks(4))
    first = is_odd("lat")
    for j in range(0, rest_ref.shape[-1], WIDE):
        lanes = slice(j, j + WIDE)
        rest = mm(pick, got_b[:, lanes], NN).astype(BF)
        rest_ref[:, lanes] = rest

        def column(i):
            most = half_ref[i * HALF : (i + 1) * HALF, lanes]
            few = rest[i * HALO : (i + 1) * HALO]
            return jnp.where(
                first, jnp.concatenate([most, few], axis=0), jnp.concatenate([few, most], axis=0)
            )

        send_a[:, lanes], send_b[:, lanes] = sort_pair("lon", column(0), column(3))


def half_masks():
    head = lax.broadcasted_iota(jnp.int32, (1, 2 * HEAD), 1) // HEAD
    return [jnp.where(head == h, 1.0, 0.0).astype(BF) for h in range(2)]


def spread_pair(block):
    return jnp.concatenate([block * m for m in half_masks()], axis=0)


def spread_group(block):
    zero = jnp.zeros((block.shape[0], 2 * HEAD), BF)
    low, high = block[:, : 2 * HEAD], block[:, 2 * HEAD :]
    masks = half_masks()
    rows = [jnp.concatenate([low * m, zero], axis=1) for m in masks]
    rows += [jnp.concatenate([zero, high * m], axis=1) for m in masks]
    return jnp.concatenate(rows, axis=0)


def pair_lanes(i):
    return slice(i * 2 * HEAD, (i + 1) * 2 * HEAD), slice(i * 2 * POINTS, (i + 1) * 2 * POINTS)


def score(keys, values, q4, d4, bufs):
    s_ref, d_ref, qs_ref, gs_ref = bufs[:4]
    for i in range(GROUP // 2):
        lanes, at = pair_lanes(i)
        qs_ref[at, :] = spread_pair(q4[:, lanes])
        gs_ref[at, :] = spread_pair(d4[:, lanes])
        s_ref[:, at] = mm(keys[:, lanes], qs_ref[at, :], NT)
        d_ref[:, at] = mm(values[:, lanes], gs_ref[at, :], NT)


def soften(bias, bufs):
    s_ref, d_ref, _, _, pw, sw, pt, st = bufs
    for h in range(GROUP):
        at = slice(h * POINTS, (h + 1) * POINTS)
        tall = slice(h * NODES, (h + 1) * NODES)
        top = jnp.max(s_ref[:, at] + bias, axis=0, keepdims=True)
        e = jnp.exp(s_ref[:, at] + bias - top)
        s_ref[:, at] = e
        inverse = 1.0 / jnp.sum(e, axis=0, keepdims=True)
        centred = jnp.sum(e * d_ref[:, at], axis=0, keepdims=True) * inverse
        p = s_ref[:, at] * inverse
        half = p.astype(BF)
        ds = (p * (d_ref[:, at] - centred)).astype(BF)
        pw[:, at] = half
        sw[:, at] = ds
        pt[tall, :] = half
        st[tall, :] = ds


def gather_grads(keys, values, bufs):
    _, _, qs_ref, gs_ref, pw, sw, pt, st = bufs
    att = mm(pt[...], spread_group(values), TN).astype(BF)
    dq = mm(st[...], spread_group(keys), TN).astype(BF)
    dk, dv = [], []
    for i in range(GROUP // 2):
        _, at = pair_lanes(i)
        dk.append(mm(sw[:, at], qs_ref[at, :], NN))
        dv.append(mm(pw[:, at], gs_ref[at, :], NN))
    return att, dq, jnp.concatenate(dk, axis=1), jnp.concatenate(dv, axis=1)


ITEM_SCRATCH = (
    (pltpu.VMEM((NODES, GROUP * POINTS), F32),) * 2
    + (pltpu.VMEM((GROUP * POINTS, 2 * HEAD), BF),) * 2
    + (pltpu.VMEM((NODES, GROUP * POINTS), BF),) * 2
    + (pltpu.VMEM((GROUP * NODES, POINTS), BF),) * 2
)
PAIR_SCRATCH = ITEM_SCRATCH * 2


def attend(tile, load, store, q_ref, da_ref, bias_ref, scratch):
    n = len(ITEM_SCRATCH)
    bufs = (scratch[:n], scratch[n:])
    items = [slice(j, j + WIDE) for j in range(0, HEADS * HEAD, WIDE)]

    def do_score(k):
        lanes = items[k]
        score(*load(lanes), q_ref[tile, :, lanes], da_ref[tile, :, lanes], bufs[k % 2])

    def do_grads(k):
        store(items[k], *gather_grads(*load(items[k]), bufs[k % 2]))

    do_score(0)
    for k in range(len(items)):
        if k > 0:
            do_grads(k - 1)
        soften(bias_ref[tile], bufs[k % 2])
        if k + 1 < len(items):
            do_score(k + 1)
    do_grads(len(items) - 1)


def store_all(*refs):
    def store(lanes, *values):
        for ref, value in zip(refs, values):
            ref[:, lanes] = value

    return store


def first_kernel(
    got_a, own_a, own_b, wk_ref, wv_ref, q_ref, da_ref, bias_ref,
    half_ref, k_ref, v_ref, att_ref, dq_ref, dk_ref, dv_ref, *scratch,
):
    upper = is_odd("lat")
    top = jnp.where(upper, got_a[...], own_b[...])
    bottom = jnp.where(upper, own_b[...], got_a[...])
    rows = jnp.concatenate([top, own_a[...], bottom], axis=0)
    pick = select(NODES, to_blocks(12))
    for j in range(0, half_ref.shape[-1], WIDE):
        lanes = slice(j, j + WIDE)
        half_ref[:, lanes] = mm(pick, rows[:, lanes], NN).astype(BF)
    for j in range(0, half_ref.shape[-1], WIDE):
        lanes = slice(j, j + WIDE)
        k_ref[:, lanes] = mm(half_ref[...], wk_ref[:, lanes], NN).astype(BF)
        v_ref[:, lanes] = mm(half_ref[...], wv_ref[:, lanes], NN).astype(BF)

    def load(lanes):
        return k_ref[:, lanes], v_ref[:, lanes]

    tile = jnp.where(upper, 1, 2)
    store = store_all(att_ref, dq_ref, dk_ref, dv_ref)
    attend(tile, load, store, q_ref, da_ref, bias_ref, scratch)


def edge_tile(left, k_ref, v_ref, kr, vr, outs, q_ref, da_ref, bias_ref, scratch):
    att_ref, dq_ref, dk_ref, dv_ref, dkr, dvr = outs
    start = pl.multiple_of(jnp.where(left, 0, 2 * BLOCK), 2 * BLOCK)

    def load(lanes):
        def one(rim, mid):
            return jnp.concatenate([rim[:, lanes], mid[pl.ds(start, 2 * BLOCK), lanes]], axis=0)

        return one(kr, k_ref), one(vr, v_ref)

    def store(lanes, att, dq, dk, dv):
        att_ref[:, lanes] = att
        dq_ref[:, lanes] = dq
        for grad, rim, out in ((dk, dkr, dk_ref), (dv, dvr, dv_ref)):
            rim[:, lanes] = (grad[:BLOCK] * (1.0 / SCALE)).astype(BF)
            out[:, lanes] = grad[BLOCK:]

    attend(jnp.where(left, 0, 3), load, store, q_ref, da_ref, bias_ref, scratch)


def near_kernel(
    got_a, rest_ref, kh_ref, vh_ref, wk_ref, wv_ref, q_ref, da_ref, bias_ref,
    k_ref, v_ref, att_ref, dq_ref, dk_ref, dv_ref, dkr, dvr,
    kr, vr, *scratch,
):
    rows = jnp.concatenate([got_a[...], rest_ref[...]], axis=0)
    first = is_odd("lat")
    for rim, mid, half, w in ((kr, k_ref, kh_ref, wk_ref), (vr, v_ref, vh_ref, wv_ref)):
        for j in range(0, rows.shape[-1], WIDE):
            lanes = slice(j, j + WIDE)
            made = mm(rows, w[:, lanes], NN).astype(BF)
            rim[:, lanes] = made[:BLOCK]
            for i in range(4):
                most = half[i * HALF : (i + 1) * HALF, lanes]
                few = made[BLOCK + i * HALO : BLOCK + (i + 1) * HALO]
                mid[i * BLOCK : (i + 1) * BLOCK, lanes] = jnp.where(
                    first,
                    jnp.concatenate([most, few], axis=0),
                    jnp.concatenate([few, most], axis=0),
                )
    outs = (att_ref, dq_ref, dk_ref, dv_ref, dkr, dvr)
    edge_tile(is_odd("lon"), k_ref, v_ref, kr, vr, outs, q_ref, da_ref, bias_ref, scratch)


def far_kernel(
    got_b, k_ref, v_ref, wk_ref, wv_ref, q_ref, da_ref, bias_ref, near_dkr, near_dvr,
    att_ref, dq_ref, dk_ref, dv_ref, send_a, send_b,
    kr, vr, dkr, dvr, *scratch,
):
    for j in range(0, kr.shape[-1], WIDE):
        lanes = slice(j, j + WIDE)
        kr[:, lanes] = mm(got_b[...], wk_ref[:, lanes], NN).astype(BF)
        vr[:, lanes] = mm(got_b[...], wv_ref[:, lanes], NN).astype(BF)
    outs = (att_ref, dq_ref, dk_ref, dv_ref, dkr, dvr)
    left = lax.axis_index("lon") % 2 == 0
    edge_tile(left, k_ref, v_ref, kr, vr, outs, q_ref, da_ref, bias_ref, scratch)
    dk = jnp.concatenate([near_dkr[...], dkr[...]], axis=0)
    dv = jnp.concatenate([near_dvr[...], dvr[...]], axis=0)
    for j in range(0, kr.shape[-1], WIDE):
        lanes = slice(j, j + WIDE)
        part = mm(dk, wk_ref[lanes, :], NT) + mm(dv, wv_ref[lanes, :], NT)
        send_a[:, lanes] = part[:BLOCK].astype(BF)
        send_b[:, lanes] = part[BLOCK:].astype(BF)


def last_kernel(
    k_ref, v_ref, wk_ref, wv_ref, q_ref, da_ref, bias_ref,
    dkh_ref, dvh_ref, dkn_ref, dvn_ref, dkf_ref, dvf_ref,
    att_ref, dq_ref, part_ref, dko_ref, dvo_ref,
    dkr, dvr, *scratch,
):
    upper_done = is_odd("lat")
    offset = jnp.where(upper_done, HALO, 0)

    def load(lanes):
        def one(ref):
            starts = [pl.multiple_of(i * BLOCK + offset, HALO) for i in range(4)]
            return jnp.concatenate([ref[pl.ds(at, HALF), lanes] for at in starts], axis=0)

        return one(k_ref), one(v_ref)

    def store(lanes, att, dq, dk, dv):
        att_ref[:, lanes] = att
        dq_ref[:, lanes] = dq
        for grad, half, near, far, rims, own in (
            (dk, dkh_ref, dkn_ref, dkf_ref, dkr, dko_ref),
            (dv, dvh_ref, dvn_ref, dvf_ref, dvr, dvo_ref),
        ):
            sides = sort_pair("lon", near[:, lanes], far[:, lanes])
            for i in range(4):
                edge = sides[i // 2][(i % 2) * BLOCK : (i % 2 + 1) * BLOCK]
                a = half[i * HALF : (i + 1) * HALF, lanes]
                b = grad[i * HALF : (i + 1) * HALF]
                up = jnp.where(upper_done, a, b)
                down = jnp.where(upper_done, b, a)
                low = edge[:HALO] + up[:HALO]
                mine = edge[HALO:HALF] + up[HALO:] + down[: HALF - HALO]
                high = edge[HALF:] + down[HALF - HALO :]
                low, mine, high = ((x * (1.0 / SCALE)).astype(BF) for x in (low, mine, high))
                rims[i * HALO : (i + 1) * HALO, lanes] = low
                rims[BLOCK + i * HALO : BLOCK + (i + 1) * HALO, lanes] = high
                own[i * 2 * HALO : (i + 1) * 2 * HALO, lanes] = mine

    attend(jnp.where(upper_done, 2, 1), load, store, q_ref, da_ref, bias_ref, scratch)
    for j in range(0, part_ref.shape[-1], WIDE):
        lanes = slice(j, j + WIDE)
        part_ref[:, lanes] = mm(dkr[...], wk_ref[lanes, :], NT) + mm(dvr[...], wv_ref[lanes, :], NT)


def merge_kernel(part_ref, got_a, got_b, send_a, send_b):
    left, right = (x.astype(F32) for x in sort_pair("lon", got_a[...], got_b[...]))
    sides = []
    for i, rows in enumerate((slice(0, HALO), slice(HALF, BLOCK))):
        part = part_ref[i * BLOCK : (i + 1) * BLOCK]
        parts = [part[:HALO] + left[rows], part[HALO:HALF], part[HALF:] + right[rows]]
        sides.append(jnp.concatenate(parts, axis=0).astype(BF))
    send_a[...], send_b[...] = sort_pair("lat", *sides)


def emit(res_ref, tiles, w_ref, dims, out_hbm, out_scr, sem):
    first, near, far, last = (ref[...] for ref in tiles)
    rows = jnp.concatenate(
        [*sort_pair("lon", near, far)[:1], *sort_pair("lat", first, last), sort_pair("lon", near, far)[1]],
        axis=0,
    )
    copies = []
    for i, j in enumerate(range(0, out_scr.shape[-1], 256)):
        lanes = slice(j, j + 256)
        w = w_ref[:, lanes] if dims is NN else w_ref[lanes, :]
        product = mm(rows, w, dims)
        tiles = [product[t * POINTS : (t + 1) * POINTS] for t in range(TILES)]
        out_scr[:, lanes] = (res_ref[:, lanes].astype(F32) + from_tiles(tiles)).astype(BF)
        copy = pltpu.make_async_copy(out_scr.at[:, lanes], out_hbm.at[:, lanes], sem.at[i])
        copy.start()
        copies.append(copy)
    return copies


def layer_out_kernel(
    x_ref, first, near, far, last, wo_ref, piece_ref, out_hbm, pass_ref, out_scr, sem
):
    pass_ref[...] = piece_ref[...]
    for copy in emit(x_ref, (first, near, far, last), wo_ref, NN, out_hbm, out_scr, sem):
        copy.wait()


def grid_grad_kernel(
    c_ref, first, near, far, last, wq_ref, dk_ref, dv_ref, wk_ref, wv_ref, got_a, got_b,
    grad_hbm, own_ref, out_scr, sem,
):
    copies = emit(c_ref, (first, near, far, last), wq_ref, NT, grad_hbm, out_scr, sem)
    left, right = (x.astype(F32)[HALO:HALF] for x in sort_pair("lon", got_a[...], got_b[...]))
    none = jnp.zeros((BLOCK, WIDE), F32)
    for j in range(0, own_ref.shape[-1], WIDE):
        lanes = slice(j, j + WIDE)
        rims = jnp.concatenate([left[:, lanes], none, right[:, lanes]], axis=0)
        own_ref[:, lanes] = (
            mm(dk_ref[...], wk_ref[lanes, :], NT) + mm(dv_ref[...], wv_ref[lanes, :], NT) + rims
        )
    for copy in copies:
        copy.wait()


def finish_kernel(own_ref, got_a, got_b, out_hbm, out_scr, sem):
    sides = [x.astype(F32) for x in sort_pair("lat", got_a[...], got_b[...])]
    parts = [side[i * HALO : (i + 1) * HALO] for i in range(4) for side in sides]
    total = (own_ref[...] + jnp.concatenate(parts, axis=0)).astype(BF)
    dst = lax.broadcasted_iota(jnp.int32, (2 * BLOCK, 2 * BLOCK), 0)
    src = lax.broadcasted_iota(jnp.int32, (2 * BLOCK, 2 * BLOCK), 1)
    pick = jnp.where(src == to_blocks(8)(dst), 1.0, 0.0).astype(BF)
    out_scr[...] = mm(pick, total, NN).astype(BF)
    copy = pltpu.make_async_copy(out_scr, out_hbm, sem)
    copy.start()
    copy.wait()


def pairs_of(axis, ring):
    count = lax.axis_size(axis)
    even = [(i, i + 1) for i in range(0, count, 2)]
    odd = [(i, i + 1) for i in range(1, count - 1, 2)]
    if ring:
        odd.append((count - 1, 0))
    return tuple(pairs + [(b, a) for a, b in pairs] for pairs in (even, odd))


def local(grid_feat, mesh_feat, edges, edge_mask, w_query, w_key, w_value, w_out, cotangent):
    width = grid_feat.shape[-1]
    points = TILES * POINTS
    x = grid_feat.reshape(points, width)
    c = cotangent.reshape(points, width)
    own = mesh_feat.reshape(2 * BLOCK, width)
    product = 2 * width * width
    lat_a, lat_b = pairs_of("lat", False)
    lon_a, lon_b = pairs_of("lon", True)
    piece = ((BLOCK, width), BF)
    tiled = ((TILES, POINTS, width), BF)
    square = ((width, width), BF)

    send_a, send_b = call(
        lead_kernel, (own,), [piece, piece], 10**5,
        (pltpu.SemaphoreType.DMA((2,)),), hbm=(0,),
    )
    got_a = lax.ppermute(send_a, "lat", lat_a)
    q, c_near, wo_near = call(
        project_q_kernel, (x, w_query, c, w_out),
        [tiled, ((points, width), BF), square],
        points * product,
        (
            pltpu.VMEM((points, width), BF),
            pltpu.VMEM((width, width), BF),
            pltpu.SemaphoreType.DMA((7,)),
        ),
        hbm=(0, 1, 2, 3),
    )
    da, bias, late_b = call(
        project_d_kernel, (c_near, wo_near, edges, edge_mask, send_b),
        [tiled, ((TILES, NODES, POINTS), F32), piece],
        points * product,
    )
    got_b = lax.ppermute(late_b, "lat", lat_b)
    common = (w_key, w_value, q, da, bias)
    rows = ((POINTS, width), BF)
    half, half_grad = ((NODES, width), BF), ((NODES, width), F32)
    mid, mid_grad = ((MIDDLE, width), BF), ((2 * BLOCK, width), F32)
    half_rows, kh, vh, att_first, dq_first, dkh, dvh = call(
        first_kernel, (got_a, send_a, send_b, *common),
        [half] * 3 + [rows] * 2 + [half_grad] * 2,
        4 * 10**9, PAIR_SCRATCH,
    )
    rest, edge_a, edge_b = call(assemble_kernel, (half_rows, got_b), [piece] * 3, 10**8)
    edge_a = lax.ppermute(edge_a, "lon", lon_a)
    edge_b = lax.ppermute(edge_b, "lon", lon_b)
    k, v, att_near, dq_near, dkn, dvn, rim_dk, rim_dv = call(
        near_kernel, (edge_a, rest, kh, vh, *common),
        [mid] * 2 + [rows] * 2 + [mid_grad] * 2 + [piece] * 2,
        4 * 10**9, (pltpu.VMEM((BLOCK, width), BF),) * 2 + PAIR_SCRATCH,
    )
    att_far, dq_far, dkf, dvf, edge_a, edge_b = call(
        far_kernel, (edge_b, k, v, *common, rim_dk, rim_dv),
        [rows] * 2 + [mid_grad] * 2 + [piece] * 2,
        4 * 10**9, (pltpu.VMEM((BLOCK, width), BF),) * 4 + PAIR_SCRATCH,
    )
    edge_a = lax.ppermute(edge_a, "lon", lon_a)
    edge_b = lax.ppermute(edge_b, "lon", lon_b)
    att_last, dq_last, part, dk_own, dv_own = call(
        last_kernel, (k, v, *common, dkh, dvh, dkn, dvn, dkf, dvf),
        [rows] * 2 + [mid_grad] + [((2 * BLOCK, width), BF)] * 2,
        4 * 10**9, (pltpu.VMEM((2 * BLOCK, width), BF),) * 2 + PAIR_SCRATCH,
    )
    send_a, send_b = call(merge_kernel, (part, edge_a, edge_b), [piece, piece], 10**8)
    got_a = lax.ppermute(send_a, "lat", lat_a)
    out_scratch = (pltpu.VMEM((points, width), BF), pltpu.SemaphoreType.DMA((4,)))
    layer_out, late_b = call(
        layer_out_kernel, (x, att_first, att_near, att_far, att_last, w_out, send_b),
        [((points, width), BF), piece],
        points * product, out_scratch, hbm_out=(0,),
    )
    got_b = lax.ppermute(late_b, "lat", lat_b)
    grid_grad, kept = call(
        grid_grad_kernel,
        (c, dq_first, dq_near, dq_far, dq_last, w_query, dk_own, dv_own, w_key, w_value, edge_a, edge_b),
        [((points, width), BF), ((2 * BLOCK, width), F32)],
        points * product, out_scratch, hbm_out=(0,),
    )
    (mesh_grad,) = call(
        finish_kernel, (kept, got_a, got_b), [((2 * BLOCK, width), BF)], 10**6,
        (pltpu.VMEM((2 * BLOCK, width), BF), pltpu.SemaphoreType.DMA), hbm_out=(0,),
    )
    return (
        layer_out.reshape(grid_feat.shape),
        grid_grad.reshape(grid_feat.shape),
        mesh_grad.reshape(mesh_feat.shape),
    )


def solution(mesh):
    tiled = P("lat", "lon", None)
    placed = (tiled, tiled, P(None, "lat", "lon"), P(None, "lat", "lon")) + (P(),) * 4 + (tiled,)
    return jax.shard_map(
        local, mesh=mesh, in_specs=placed, out_specs=(tiled, tiled, tiled), check_vma=False
    )
```

time: 52.7 us -> 52.6 us (level)
  waiting for transfers between devices: 4.44 us -> 3.1 us
  Pallas kernels: 26.6 us -> 27.3 us
    ppermute x2, waiting for transfers between devices: 2.56 us -> 1.26 us  [local(): got_b = lax.ppermute(late_b, 'lat', lat_b)]
    pallas_call x11 -> x12, Pallas kernels: 26.6 us -> 27.3 us  [call(): pl.pallas_call(kernel, in_specs=[placed(i) for i in range(len(inputs))],...]
    ppermute x2, starting transfers between devices: 11.6 us -> 12.2 us  [local(): edge_b = lax.ppermute(edge_b, 'lon', lon_b)]
  transfers between devices with their start and end apart: 8 -> 8, of which waited for: 3 -> 3; matrix products, arithmetic and copies ran while one was open for 0% -> 0% of each run, Pallas kernels for 31% -> 36%
where the time goes in v5:
time: 52.6 us; the launch traced here: 52.5 us
  Pallas kernels  27.3 us (52%)
  starting transfers between devices  20.9 us (40%)
  waiting for transfers between devices  3.1 us (6%)
  between operations  1.04 us (2%)
    pallas_call x12, Pallas kernels, call(): pl.pallas_call(kernel, in_specs=[placed(i) for i in range(len(inputs))],...  27.3 us
    ppermute x2, starting transfers between devices, local(): edge_b = lax.ppermute(edge_b, 'lon', lon_b)  12.2 us
    ppermute x2, starting transfers between devices, local(): got_b = lax.ppermute(late_b, 'lat', lat_b)  6.24 us
    ppermute x2, starting transfers between devices, local(): got_a = lax.ppermute(send_a, 'lat', lat_a)  2.34 us
    ppermute x2, waiting for transfers between devices, local(): got_a = lax.ppermute(send_a, 'lat', lat_a)  1.83 us
    ppermute x2, waiting for transfers between devices, local(): got_b = lax.ppermute(late_b, 'lat', lat_b)  1.26 us
  transfers between devices with their start and end apart: 8, of which 3 were waited for; matrix products, arithmetic and copies ran while one was open for 0% of the time, Pallas kernels for 36%

profile of v5, /device:TPU:8, one launch (start us, length us, event | category | flops | bytes accessed | tf_op | source)
XLA Modules:
  0.0 52.5 jit_solution(10017213739100516361)
XLA Ops:
  0.6 1.0 %shard_map.112 = (bf16[64,1024]{1,0:T(8,128)(2,1)S(1)}, bf16[64,1024]{1,0:T(8,128)(2,1)S(1)}) custom-call(bf16[128,1024]{1,0:T(8,128)(2,1)} %bitcast.10), custom_call_target="tpu_custom_call" | custom-call | flops 100000 | bytes 262144 | tf_op jit(solution)/shard_map/pallas_call | solution.py:46
  1.6 2.2 %collective-permute-start = (bf16[64,1024]{1,0:T(8,128)(2,1)S(1)}, bf16[64,1024]{1,0:T(8,128)(2,1)S(1)}, u32[]{:S(2)}, u32[]{:S(2)}) collective-permute-start(bf16[64,1024]{1,0:T(8,128)(2,1)S(1)} %get-tuple-element.46.own_a), channel_id=1, source_target_pairs={{0,64},{128,192},{64,0},{192,128},{1,65},{129,193},{65,1},{193,129... | collective-permute-start | bytes 393224 | tf_op jit(solution)/shard_map/ppermute | solution.py:529
  3.9 0.0 copy-start.6
  3.9 0.0 copy-start.7
  3.9 0.0 copy-start.5
  3.9 4.4 %shard_map.113 = (bf16[4,128,1024]{2,1,0:T(8,128)(2,1)S(1)}, bf16[512,1024]{1,0:T(8,128)(2,1)S(1)}, bf16[1024,1024]{1,0:T(8,128)(2,1)S(1)}) custom-call(bf16[512,1024]{1,0:T(8,128)(2,1)} %bitcast.8, bf16[1024,1024]{1,0:T(8,128)(2,1)} %wq_ref.1, bf16[512,1024]{1,0:T(8,128)(2,1)} %bitcast.6, bf16[1024,1024]{1,0:T(8,128)(2,1)} %wo_ref.1), custom_call_target="tpu_custom_call" | custom-call | flops 1073741824 | bytes 6291456 | tf_op jit(solution)/shard_map/pallas_call | solution.py:46
  8.2 0.0 copy-start.4
  8.3 0.0 copy-done.6
  8.3 0.0 copy-done.7
  8.3 1.9 %shard_map.114 = (bf16[4,128,1024]{2,1,0:T(8,128)(2,1)S(1)}, f32[4,192,128]{2,1,0:T(8,128)S(1)}, bf16[64,1024]{1,0:T(8,128)(2,1)S(1)}) custom-call(bf16[512,1024]{1,0:T(8,128)(2,1)S(1)} %get-tuple-element.49.c_ref, bf16[1024,1024]{1,0:T(8,128)(2,1)S(1)} %get-tuple-element.50.wo_ref, s32[12,16,32]{2,1,0:T(8,128)S(1)} %copy-done.6, ...), custom_call_target="tpu_custom_call" | custom-call | flops 1073741824 | bytes 3325952 | tf_op jit(solution)/shard_map/pallas_call | solution.py:46
  10.2 2.6 %collective-permute-start.1 = (bf16[64,1024]{1,0:T(8,128)(2,1)S(1)}, bf16[64,1024]{1,0:T(8,128)(2,1)S(1)}, u32[]{:S(2)}, u32[]{:S(2)}) collective-permute-start(bf16[64,1024]{1,0:T(8,128)(2,1)S(1)} %get-tuple-element.55), channel_id=1, source_target_pairs={{64,128},{128,64},{65,129},{129,65},{66,130},{130,66},{67,131},{13... | collective-permute-start | bytes 393224 | tf_op jit(solution)/shard_map/ppermute | solution.py:546
  12.8 0.0 collective-permute-done.got_a
  12.8 0.0 copy-done.5
  12.8 0.0 copy-done.4
  12.8 3.2 %shard_map.115 = (bf16[192,1024]{1,0:T(8,128)(2,1)S(1)}, bf16[192,1024]{1,0:T(8,128)(2,1)S(1)}, bf16[192,1024]{1,0:T(8,128)(2,1)S(1)}, bf16[128,1024]{1,0:T(8,12...) custom-call(bf16[64,1024]{1,0:T(8,128)(2,1)S(1)} %collective-permute-done.got_a, ...), custom_call_target="tpu_custom_call" | custom-call | flops 4000000000 | bytes 7077888 | tf_op jit(solution)/shard_map/pallas_call | solution.py:46
  16.0 1.0 %collective-permute-done.1.got_b = bf16[64,1024]{1,0:T(8,128)(2,1)S(1)} collective-permute-done((bf16[64,1024]{1,0:T(8,128)(2,1)S(1)}, bf16[64,1024]{1,0:T(8,128)(2,1)S(1)}, u32[]{:S(2)}, u32[]{:S(2)}) %collective-permute-start.1) | collective-permute-done | bytes 131104 | tf_op jit(solution)/shard_map/ppermute | solution.py:546
  17.0 0.2 shard_map.116
  17.2 0.1 collective-permute-start.2
  17.3 7.1 %collective-permute-start.3 = (bf16[64,1024]{1,0:T(8,128)(2,1)S(1)}, bf16[64,1024]{1,0:T(8,128)(2,1)S(1)}, u32[]{:S(2)}, u32[]{:S(2)}) collective-permute-start(bf16[64,1024]{1,0:T(8,128)(2,1)S(1)} %get-tuple-element.61), channel_id=1, source_target_pairs={{1,2},{3,4},{5,6},{7,8},{9,10},{11,12},{13,14},{15,16},{17,18},{19... | collective-permute-start | bytes 393224 | tf_op jit(solution)/shard_map/ppermute | solution.py:558
  24.4 0.0 collective-permute-done.2.got_a
  24.4 2.7 %shard_map.117 = (bf16[256,1024]{1,0:T(8,128)(2,1)S(1)}, bf16[256,1024]{1,0:T(8,128)(2,1)S(1)}, bf16[128,1024]{1,0:T(8,128)(2,1)S(1)}, bf16[128,1024]{1,0:T(8,12...) custom-call(bf16[64,1024]{1,0:T(8,128)(2,1)S(1)} %collective-permute, ...), custom_call_target="tpu_custom_call" | custom-call | flops 4000000000 | bytes 7733248 | tf_op jit(solution)/shard_map/pallas_call | solution.py:46
  27.2 0.0 collective-permute-done.3.got_b
  27.2 4.2 %shard_map.118 = (bf16[128,1024]{1,0:T(8,128)(2,1)S(1)}, bf16[128,1024]{1,0:T(8,128)(2,1)S(1)}, f32[128,1024]{1,0:T(8,128)S(1)}, f32[128,1024]{1,0:T(8,128)S(1)}...) custom-call(bf16[64,1024]{1,0:T(8,128)(2,1)S(1)} %collective-permute-done.3.got_b, ...), custom_call_target="tpu_custom_call" | custom-call | flops 4000000000 | bytes 8126464 | tf_op jit(solution)/shard_map/pallas_call | solution.py:46
  31.4 0.1 collective-permute-start.4
  31.5 5.1 %collective-permute-start.5 = (bf16[64,1024]{1,0:T(8,128)(2,1)S(1)}, bf16[64,1024]{1,0:T(8,128)(2,1)S(1)}, u32[]{:S(2)}, u32[]{:S(2)}) collective-permute-start(bf16[64,1024]{1,0:T(8,128)(2,1)S(1)} %get-tuple-element.76), channel_id=1, source_target_pairs={{1,2},{3,4},{5,6},{7,8},{9,10},{11,12},{13,14},{15,16},{17,18},{19... | collective-permute-start | bytes 393224 | tf_op jit(solution)/shard_map/ppermute | solution.py:570
  36.5 0.0 copy-start
  36.5 0.0 copy-start.3
  36.5 3.8 %shard_map.119 = (bf16[128,1024]{1,0:T(8,128)(2,1)S(1)}, bf16[128,1024]{1,0:T(8,128)(2,1)S(1)}, f32[128,1024]{1,0:T(8,128)S(1)}, bf16[128,1024]{1,0:T(8,128)(2,1)S(1)}, bf16[128,1024]{1,0:T(8,128)(2,1)S(1)}) custom-call(bf16[256,1024]{1,0:T(8,128)(2,1)S(1)} %get-tuple-element.62.k_ref, bf16[256,1024]{1,0:T(8,128)(2,1)S(1)} %get-tuple-element.63.v_ref, ...), custom_call_target="tpu_custom_call" | custom-call | flops 4000000000 | bytes 11403264 | tf_op jit(solution)/shard_map/pallas_call | solution.py:46
  40.3 0.0 collective-permute-done.4.got_a
  40.4 0.0 collective-permute-done.5.got_b
  40.4 0.1 shard_map.120
  40.4 0.0 copy-done
  40.4 0.0 copy-done.3
  40.5 0.0 copy-start.1
  40.5 0.0 copy-start.2
  40.5 2.1 %shard_map.121 = (bf16[512,1024]{1,0:T(8,128)(2,1)}, bf16[64,1024]{1,0:T(8,128)(2,1)S(1)}) custom-call(bf16[512,1024]{1,0:T(8,128)(2,1)S(1)} %bitcast.9, bf16[128,1024]{1,0:T(8,128)(2,1)S(1)} %get-tuple-element.53.first, bf16[128,1024]{1,0:T(8,128)(2,1)S(1)} %get-tuple-element.60.near, bf16[128,1024]{1,0:T(8,128)(2,1)S(1)} %get-tuple-element.66.far, ...), custom_call_target="tpu_custom_call" | custom-call | flops 1073741824 | bytes 4325376 | tf_op jit(solution)/shard_map/pallas_call | solution.py:46
  42.6 3.6 %collective-permute-start.7 = (bf16[64,1024]{1,0:T(8,128)(2,1)S(1)}, bf16[64,1024]{1,0:T(8,128)(2,1)S(1)}, u32[]{:S(2)}, u32[]{:S(2)}) collective-permute-start(bf16[64,1024]{1,0:T(8,128)(2,1)S(1)} %get-tuple-element.88), channel_id=1, source_target_pairs={{64,128},{128,64},{65,129},{129,65},{66,130},{130,66},{67,131},{13... | collective-permute-start | bytes 393224 | tf_op jit(solution)/shard_map/ppermute | solution.py:584
  46.3 0.1 collective-permute-start.6
  46.4 0.0 copy-done.1
  46.4 0.0 copy-done.2
  46.4 2.9 %shard_map.122 = (bf16[512,1024]{1,0:T(8,128)(2,1)}, f32[128,1024]{1,0:T(8,128)S(1)}) custom-call(bf16[512,1024]{1,0:T(8,128)(2,1)S(1)} %bitcast.7, bf16[128,1024]{1,0:T(8,128)(2,1)S(1)} %get-tuple-element.79.first, bf16[128,1024]{1,0:T(8,128)(2,1)S(1)} %get-tuple-element.80.near, bf16[128,1024]{1,0:T(8,128)(2,1)S(1)} %get-tuple-element.81.far, ...), custom_call_target="tpu_custom_call" | custom-call | flops 1073741824 | bytes 9175040 | tf_op jit(solution)/shard_map/pallas_call | solution.py:46
  49.3 0.2 collective-permute-done.7.got_b
  49.5 1.8 %collective-permute-done.6.got_a = bf16[64,1024]{1,0:T(8,128)(2,1)S(1)} collective-permute-done((bf16[64,1024]{1,0:T(8,128)(2,1)S(1)}, bf16[64,1024]{1,0:T(8,128)(2,1)S(1)}, u32[]{:S(2)}, u32[]{:S(2)}) %collective-permute-start.6) | collective-permute-done | bytes 131104 | tf_op jit(solution)/shard_map/ppermute | solution.py:577
  51.3 1.0 %shard_map.123 = bf16[128,1024]{1,0:T(8,128)(2,1)} custom-call(f32[128,1024]{1,0:T(8,128)S(1)} %get-tuple-element.86.own_ref, bf16[64,1024]{1,0:T(8,128)(2,1)S(1)} %collective-permute-done.6.got_a, bf16[64,1024]{1,0:T(8,128)(2,1)S(1)} %collective-permute-done.7.got_b), custom_call_target="tpu_custom_call" | custom-call | flops 1000000 | bytes 786432 | tf_op jit(solution)/shard_map/pallas_call | solution.py:46
Async XLA Ops:
  1.6 11.2 %collective-permute-start = (bf16[64,1024]{1,0:T(8,128)(2,1)S(1)}, bf16[64,1024]{1,0:T(8,128)(2,1)S(1)}, u32[]{:S(2)}, u32[]{:S(2)}) collective-permute-start(bf16[64,1024]{1,0:T(8,128)(2,1)S(1)} %get-tuple-element.46.own_a), channel_id=1, source_target_pairs={{0,64},{128,192},{64,0},{192,128},{1,65},{129,193},{65,1},{193,129... | collective-permute-start | bytes 393224 | tf_op jit(solution)/shard_map/ppermute | solution.py:529
  3.9 4.4 %copy-start.6 = (s32[12,16,32]{2,1,0:T(8,128)S(1)}, s32[12,16,32]{2,1,0:T(8,128)}, u32[]{:S(2)}) copy-start(s32[12,16,32]{2,1,0:T(8,128)} %edges_ref.1) | copy-start | bytes 73732
  3.9 4.4 %copy-start.7 = (s32[12,16,32]{2,1,0:T(8,128)S(1)}, s32[12,16,32]{2,1,0:T(8,128)}, u32[]{:S(2)}) copy-start(s32[12,16,32]{2,1,0:T(8,128)} %mask_ref.1) | copy-start | bytes 73732
  3.9 8.9 %copy-start.5 = (bf16[1024,1024]{1,0:T(8,128)(2,1)S(1)}, bf16[1024,1024]{1,0:T(8,128)(2,1)}, u32[]{:S(2)}) copy-start(bf16[1024,1024]{1,0:T(8,128)(2,1)} %wv_ref.9) | copy-start | bytes 6291460
  8.2 4.6 %copy-start.4 = (bf16[1024,1024]{1,0:T(8,128)(2,1)S(1)}, bf16[1024,1024]{1,0:T(8,128)(2,1)}, u32[]{:S(2)}) copy-start(bf16[1024,1024]{1,0:T(8,128)(2,1)} %wk_ref.9) | copy-start | bytes 6291460
  10.2 6.9 %collective-permute-start.1 = (bf16[64,1024]{1,0:T(8,128)(2,1)S(1)}, bf16[64,1024]{1,0:T(8,128)(2,1)S(1)}, u32[]{:S(2)}, u32[]{:S(2)}) collective-permute-start(bf16[64,1024]{1,0:T(8,128)(2,1)S(1)} %get-tuple-element.55), channel_id=1, source_target_pairs={{64,128},{128,64},{65,129},{129,65},{66,130},{130,66},{67,131},{13... | collective-permute-start | bytes 393224 | tf_op jit(solution)/shard_map/ppermute | solution.py:546
  17.2 7.2 %collective-permute-start.2 = (bf16[64,1024]{1,0:T(8,128)(2,1)S(1)}, bf16[64,1024]{1,0:T(8,128)(2,1)S(1)}, u32[]{:S(2)}, u32[]{:S(2)}) collective-permute-start(bf16[64,1024]{1,0:T(8,128)(2,1)S(1)} %get-tuple-element.56), channel_id=1, source_target_pairs={{0,1},{2,3},{4,5},{6,7},{8,9},{10,11},{12,13},{14,15},{16,17},{18,... | collective-permute-start | bytes 393224 | tf_op jit(solution)/shard_map/ppermute | solution.py:557
  17.3 9.9 %collective-permute-start.3 = (bf16[64,1024]{1,0:T(8,128)(2,1)S(1)}, bf16[64,1024]{1,0:T(8,128)(2,1)S(1)}, u32[]{:S(2)}, u32[]{:S(2)}) collective-permute-start(bf16[64,1024]{1,0:T(8,128)(2,1)S(1)} %get-tuple-element.61), channel_id=1, source_target_pairs={{1,2},{3,4},{5,6},{7,8},{9,10},{11,12},{13,14},{15,16},{17,18},{19... | collective-permute-start | bytes 393224 | tf_op jit(solution)/shard_map/ppermute | solution.py:558
  31.4 9.0 %collective-permute-start.4 = (bf16[64,1024]{1,0:T(8,128)(2,1)S(1)}, bf16[64,1024]{1,0:T(8,128)(2,1)S(1)}, u32[]{:S(2)}, u32[]{:S(2)}) collective-permute-start(bf16[64,1024]{1,0:T(8,128)(2,1)S(1)} %get-tuple-element.75), channel_id=1, source_target_pairs={{0,1},{2,3},{4,5},{6,7},{8,9},{10,11},{12,13},{14,15},{16,17},{18,... | collective-permute-start | bytes 393224 | tf_op jit(solution)/shard_map/ppermute | solution.py:569
  31.5 8.9 %collective-permute-start.5 = (bf16[64,1024]{1,0:T(8,128)(2,1)S(1)}, bf16[64,1024]{1,0:T(8,128)(2,1)S(1)}, u32[]{:S(2)}, u32[]{:S(2)}) collective-permute-start(bf16[64,1024]{1,0:T(8,128)(2,1)S(1)} %get-tuple-element.76), channel_id=1, source_target_pairs={{1,2},{3,4},{5,6},{7,8},{9,10},{11,12},{13,14},{15,16},{17,18},{19... | collective-permute-start | bytes 393224 | tf_op jit(solution)/shard_map/ppermute | solution.py:570
  36.5 3.9 %copy-start = (bf16[1024,1024]{1,0:T(8,128)(2,1)S(1)}, bf16[1024,1024]{1,0:T(8,128)(2,1)}, u32[]{:S(2)}) copy-start(bf16[1024,1024]{1,0:T(8,128)(2,1)} %wo_ref.1) | copy-start | bytes 6291460
  36.5 3.9 %copy-start.3 = (bf16[16,32,1024]{2,1,0:T(8,128)(2,1)S(1)}, bf16[16,32,1024]{2,1,0:T(8,128)(2,1)}, u32[]{:S(2)}) copy-start(bf16[16,32,1024]{2,1,0:T(8,128)(2,1)} %param.9) | copy-start | bytes 3145732
  40.5 5.9 %copy-start.1 = (bf16[1024,1024]{1,0:T(8,128)(2,1)S(1)}, bf16[1024,1024]{1,0:T(8,128)(2,1)}, u32[]{:S(2)}) copy-start(bf16[1024,1024]{1,0:T(8,128)(2,1)} %wq_ref.1) | copy-start | bytes 6291460
  40.5 5.9 %copy-start.2 = (bf16[16,32,1024]{2,1,0:T(8,128)(2,1)S(1)}, bf16[16,32,1024]{2,1,0:T(8,128)(2,1)}, u32[]{:S(2)}) copy-start(bf16[16,32,1024]{2,1,0:T(8,128)(2,1)} %param.17) | copy-start | bytes 3145732
  42.6 6.9 %collective-permute-start.7 = (bf16[64,1024]{1,0:T(8,128)(2,1)S(1)}, bf16[64,1024]{1,0:T(8,128)(2,1)S(1)}, u32[]{:S(2)}, u32[]{:S(2)}) collective-permute-start(bf16[64,1024]{1,0:T(8,128)(2,1)S(1)} %get-tuple-element.88), channel_id=1, source_target_pairs={{64,128},{128,64},{65,129},{129,65},{66,130},{130,66},{67,131},{13... | collective-permute-start | bytes 393224 | tf_op jit(solution)/shard_map/ppermute | solution.py:584
  46.3 5.1 %collective-permute-start.6 = (bf16[64,1024]{1,0:T(8,128)(2,1)S(1)}, bf16[64,1024]{1,0:T(8,128)(2,1)S(1)}, u32[]{:S(2)}, u32[]{:S(2)}) collective-permute-start(bf16[64,1024]{1,0:T(8,128)(2,1)S(1)} %get-tuple-element.87), channel_id=1, source_target_pairs={{0,64},{128,192},{64,0},{192,128},{1,65},{129,193},{65,1},{193,129... | collective-permute-start | bytes 393224 | tf_op jit(solution)/shard_map/ppermute | solution.py:577

commit v6 on v5

--- a/solution.py
+++ b/solution.py
@@ -100,32 +100,37 @@
     second.wait()
 
 
-def project_q_kernel(
-    x_hbm, wq_hbm, c_hbm, wo_hbm, q_ref, c_ref, wo_ref, x_scr, wq_scr, sem
+def project_kernel(
+    edges_hbm, mask_hbm, x_hbm, wq_hbm, c_hbm, wo_hbm, wk_hbm, wv_hbm, piece_ref,
+    q_ref, da_ref, bias_ref, pass_ref, wk_ref, wv_ref,
+    edges_scr, mask_scr, x_scr, wq_scr, c_scr, wo_scr, sem,
 ):
-    copies = [pltpu.make_async_copy(x_hbm, x_scr, sem.at[0])]
-    width = q_ref.shape[-1]
-    blocks = [slice(j, j + 256) for j in range(0, width, 256)]
-    for i, lanes in enumerate(blocks):
-        copies.append(
-            pltpu.make_async_copy(wq_hbm.at[:, lanes], wq_scr.at[:, lanes], sem.at[1 + i])
-        )
-    copies.append(pltpu.make_async_copy(c_hbm, c_ref, sem.at[5]))
-    copies.append(pltpu.make_async_copy(wo_hbm, wo_ref, sem.at[6]))
+    pairs = (
+        (edges_hbm, edges_scr), (mask_hbm, mask_scr), (x_hbm, x_scr), (wq_hbm, wq_scr),
+        (c_hbm, c_scr), (wo_hbm, wo_scr), (wk_hbm, wk_ref), (wv_hbm, wv_ref),
+    )
+    copies = [pltpu.make_async_copy(a, b, sem.at[i]) for i, (a, b) in enumerate(pairs)]
     for copy in copies:
         copy.start()
+    pass_ref[...] = piece_ref[...]
     copies[0].wait()
-    for i, lanes in enumerate(blocks):
-        copies[1 + i].wait()
-        q = to_tiles(mm(x_scr[...], wq_scr[:, lanes], NN))
-        for t in range(TILES):
-            q_ref[t, :, lanes] = q[t].astype(BF) * SCALE
-    copies[5].wait()
+    copies[1].wait()
+    make_bias(edges_scr, mask_scr, bias_ref)
+    for first, out_ref, project in (
+        (2, q_ref, lambda lanes: mm(x_scr[...], wq_scr[:, lanes], NN)),
+        (4, da_ref, lambda lanes: mm(c_scr[...], wo_scr[lanes, :], NT)),
+    ):
+        copies[first].wait()
+        copies[first + 1].wait()
+        for j in range(0, q_ref.shape[-1], 256):
+            lanes = slice(j, j + 256)
+            for t, rows in enumerate(to_tiles(project(lanes))):
+                out_ref[t, :, lanes] = rows.astype(BF) * SCALE
     copies[6].wait()
-
-
-def project_d_kernel(c_ref, wo_ref, edges_ref, mask_ref, piece_ref, da_ref, bias_ref, pass_ref):
-    pass_ref[...] = piece_ref[...]
+    copies[7].wait()
+
+
+def make_bias(edges_ref, mask_ref, bias_ref):
     lat_start = lax.axis_index("lat") * 8
     lon_start = lax.axis_index("lon") * 16
     edges = edges_ref[...]
@@ -167,11 +172,6 @@
         for e in range(1, SLOTS):
             hit = hit | (node == slots[e : e + 1, at])
         bias_ref[t] = jnp.where(hit, 0.0, NEG_FILL)
-    for j in range(0, da_ref.shape[-1], 256):
-        lanes = slice(j, j + 256)
-        d = to_tiles(mm(c_ref[...], wo_ref[lanes, :], NT))
-        for t in range(TILES):
-            da_ref[t, :, lanes] = d[t].astype(BF) * SCALE
 
 
 def sort_pair(axis, a, b):
@@ -301,7 +301,7 @@
 
 def first_kernel(
     got_a, own_a, own_b, wk_ref, wv_ref, q_ref, da_ref, bias_ref,
-    half_ref, k_ref, v_ref, att_ref, dq_ref, dk_ref, dv_ref, *scratch,
+    half_ref, k_ref, v_ref, att_ref, dq_ref, dk_ref, dv_ref, wkt_ref, wvt_ref, *scratch,
 ):
     upper = is_odd("lat")
     top = jnp.where(upper, got_a[...], own_b[...])
@@ -315,6 +315,10 @@
         lanes = slice(j, j + WIDE)
         k_ref[:, lanes] = mm(half_ref[...], wk_ref[:, lanes], NN).astype(BF)
         v_ref[:, lanes] = mm(half_ref[...], wv_ref[:, lanes], NN).astype(BF)
+        for i in range(0, half_ref.shape[-1], WIDE):
+            rows = slice(i, i + WIDE)
+            wkt_ref[lanes, rows] = wk_ref[rows, lanes].T
+            wvt_ref[lanes, rows] = wv_ref[rows, lanes].T
 
     def load(lanes):
         return k_ref[:, lanes], v_ref[:, lanes]
@@ -370,6 +374,7 @@
 
 def far_kernel(
     got_b, k_ref, v_ref, wk_ref, wv_ref, q_ref, da_ref, bias_ref, near_dkr, near_dvr,
+    wkt_ref, wvt_ref,
     att_ref, dq_ref, dk_ref, dv_ref, send_a, send_b,
     kr, vr, dkr, dvr, *scratch,
 ):
@@ -384,13 +389,13 @@
     dv = jnp.concatenate([near_dvr[...], dvr[...]], axis=0)
     for j in range(0, kr.shape[-1], WIDE):
         lanes = slice(j, j + WIDE)
-        part = mm(dk, wk_ref[lanes, :], NT) + mm(dv, wv_ref[lanes, :], NT)
+        part = mm(dk, wkt_ref[:, lanes], NN) + mm(dv, wvt_ref[:, lanes], NN)
         send_a[:, lanes] = part[:BLOCK].astype(BF)
         send_b[:, lanes] = part[BLOCK:].astype(BF)
 
 
 def last_kernel(
-    k_ref, v_ref, wk_ref, wv_ref, q_ref, da_ref, bias_ref,
+    k_ref, v_ref, wkt_ref, wvt_ref, q_ref, da_ref, bias_ref,
     dkh_ref, dvh_ref, dkn_ref, dvn_ref, dkf_ref, dvf_ref,
     att_ref, dq_ref, part_ref, dko_ref, dvo_ref,
     dkr, dvr, *scratch,
@@ -430,7 +435,7 @@
     attend(jnp.where(upper_done, 2, 1), load, store, q_ref, da_ref, bias_ref, scratch)
     for j in range(0, part_ref.shape[-1], WIDE):
         lanes = slice(j, j + WIDE)
-        part_ref[:, lanes] = mm(dkr[...], wk_ref[lanes, :], NT) + mm(dvr[...], wv_ref[lanes, :], NT)
+        part_ref[:, lanes] = mm(dkr[...], wkt_ref[:, lanes], NN) + mm(dvr[...], wvt_ref[:, lanes], NN)
 
 
 def merge_kernel(part_ref, got_a, got_b, send_a, send_b):
@@ -471,7 +476,7 @@
 
 
 def grid_grad_kernel(
-    c_ref, first, near, far, last, wq_ref, dk_ref, dv_ref, wk_ref, wv_ref, got_a, got_b,
+    c_ref, first, near, far, last, wq_ref, dk_ref, dv_ref, wkt_ref, wvt_ref, got_a, got_b,
     grad_hbm, own_ref, out_scr, sem,
 ):
     copies = emit(c_ref, (first, near, far, last), wq_ref, NT, grad_hbm, out_scr, sem)
@@ -481,7 +486,7 @@
         lanes = slice(j, j + WIDE)
         rims = jnp.concatenate([left[:, lanes], none, right[:, lanes]], axis=0)
         own_ref[:, lanes] = (
-            mm(dk_ref[...], wk_ref[lanes, :], NT) + mm(dv_ref[...], wv_ref[lanes, :], NT) + rims
+            mm(dk_ref[...], wkt_ref[:, lanes], NN) + mm(dv_ref[...], wvt_ref[:, lanes], NN) + rims
         )
     for copy in copies:
         copy.wait()
@@ -494,19 +499,26 @@
     dst = lax.broadcasted_iota(jnp.int32, (2 * BLOCK, 2 * BLOCK), 0)
     src = lax.broadcasted_iota(jnp.int32, (2 * BLOCK, 2 * BLOCK), 1)
     pick = jnp.where(src == to_blocks(8)(dst), 1.0, 0.0).astype(BF)
-    out_scr[...] = mm(pick, total, NN).astype(BF)
-    copy = pltpu.make_async_copy(out_scr, out_hbm, sem)
-    copy.start()
-    copy.wait()
+    copies = []
+    for i, j in enumerate(range(0, out_scr.shape[-1], 256)):
+        lanes = slice(j, j + 256)
+        out_scr[:, lanes] = mm(pick, total[:, lanes], NN).astype(BF)
+        copy = pltpu.make_async_copy(out_scr.at[:, lanes], out_hbm.at[:, lanes], sem.at[i])
+        copy.start()
+        copies.append(copy)
+    for copy in copies:
+        copy.wait()
 
 
 def pairs_of(axis, ring):
     count = lax.axis_size(axis)
     even = [(i, i + 1) for i in range(0, count, 2)]
     odd = [(i, i + 1) for i in range(1, count - 1, 2)]
+    alone = [] if ring else [(0, 0), (count - 1, count - 1)]
     if ring:
         odd.append((count - 1, 0))
-    return tuple(pairs + [(b, a) for a, b in pairs] for pairs in (even, odd))
+    even, odd = (pairs + [(b, a) for a, b in pairs] for pairs in (even, odd))
+    return even, odd + alone
 
 
 def local(grid_feat, mesh_feat, edges, edge_mask, w_query, w_key, w_value, w_out, cotangent):
@@ -527,30 +539,24 @@
         (pltpu.SemaphoreType.DMA((2,)),), hbm=(0,),
     )
     got_a = lax.ppermute(send_a, "lat", lat_a)
-    q, c_near, wo_near = call(
-        project_q_kernel, (x, w_query, c, w_out),
-        [tiled, ((points, width), BF), square],
-        points * product,
-        (
-            pltpu.VMEM((points, width), BF),
-            pltpu.VMEM((width, width), BF),
-            pltpu.SemaphoreType.DMA((7,)),
-        ),
-        hbm=(0, 1, 2, 3),
-    )
-    da, bias, late_b = call(
-        project_d_kernel, (c_near, wo_near, edges, edge_mask, send_b),
-        [tiled, ((TILES, NODES, POINTS), F32), piece],
-        points * product,
+    q, da, bias, late_b, wk, wv = call(
+        project_kernel,
+        (edges, edge_mask, x, w_query, c, w_out, w_key, w_value, send_b),
+        [tiled, tiled, ((TILES, NODES, POINTS), F32), piece, square, square],
+        2 * points * product,
+        (pltpu.VMEM(edges.shape, jnp.int32),) * 2
+        + (pltpu.VMEM((points, width), BF), pltpu.VMEM((width, width), BF)) * 2
+        + (pltpu.SemaphoreType.DMA((8,)),),
+        hbm=tuple(range(8)),
     )
     got_b = lax.ppermute(late_b, "lat", lat_b)
-    common = (w_key, w_value, q, da, bias)
+    common = (wk, wv, q, da, bias)
     rows = ((POINTS, width), BF)
     half, half_grad = ((NODES, width), BF), ((NODES, width), F32)
     mid, mid_grad = ((MIDDLE, width), BF), ((2 * BLOCK, width), F32)
-    half_rows, kh, vh, att_first, dq_first, dkh, dvh = call(
+    half_rows, kh, vh, att_first, dq_first, dkh, dvh, wkt, wvt = call(
         first_kernel, (got_a, send_a, send_b, *common),
-        [half] * 3 + [rows] * 2 + [half_grad] * 2,
+        [half] * 3 + [rows] * 2 + [half_grad] * 2 + [square] * 2,
         4 * 10**9, PAIR_SCRATCH,
     )
     rest, edge_a, edge_b = call(assemble_kernel, (half_rows, got_b), [piece] * 3, 10**8)
@@ -562,14 +568,14 @@
         4 * 10**9, (pltpu.VMEM((BLOCK, width), BF),) * 2 + PAIR_SCRATCH,
     )
     att_far, dq_far, dkf, dvf, edge_a, edge_b = call(
-        far_kernel, (edge_b, k, v, *common, rim_dk, rim_dv),
+        far_kernel, (edge_b, k, v, *common, rim_dk, rim_dv, wkt, wvt),
         [rows] * 2 + [mid_grad] * 2 + [piece] * 2,
         4 * 10**9, (pltpu.VMEM((BLOCK, width), BF),) * 4 + PAIR_SCRATCH,
     )
     edge_a = lax.ppermute(edge_a, "lon", lon_a)
     edge_b = lax.ppermute(edge_b, "lon", lon_b)
     att_last, dq_last, part, dk_own, dv_own = call(
-        last_kernel, (k, v, *common, dkh, dvh, dkn, dvn, dkf, dvf),
+        last_kernel, (k, v, wkt, wvt, q, da, bias, dkh, dvh, dkn, dvn, dkf, dvf),
         [rows] * 2 + [mid_grad] + [((2 * BLOCK, width), BF)] * 2,
         4 * 10**9, (pltpu.VMEM((2 * BLOCK, width), BF),) * 2 + PAIR_SCRATCH,
     )
@@ -584,13 +590,13 @@
     got_b = lax.ppermute(late_b, "lat", lat_b)
     grid_grad, kept = call(
         grid_grad_kernel,
-        (c, dq_first, dq_near, dq_far, dq_last, w_query, dk_own, dv_own, w_key, w_value, edge_a, edge_b),
+        (c, dq_first, dq_near, dq_far, dq_last, w_query, dk_own, dv_own, wkt, wvt, edge_a, edge_b),
         [((points, width), BF), ((2 * BLOCK, width), F32)],
         points * product, out_scratch, hbm_out=(0,),
     )
     (mesh_grad,) = call(
         finish_kernel, (kept, got_a, got_b), [((2 * BLOCK, width), BF)], 10**6,
-        (pltpu.VMEM((2 * BLOCK, width), BF), pltpu.SemaphoreType.DMA), hbm_out=(0,),
+        (pltpu.VMEM((2 * BLOCK, width), BF), pltpu.SemaphoreType.DMA((4,))), hbm_out=(0,),
     )
     return (
         layer_out.reshape(grid_feat.shape),

time: 52.6 us -> 49.5 us (0.941)
  Pallas kernels: 27.3 us -> 24.3 us
    pallas_call x12 -> x11, Pallas kernels: 27.3 us -> 24.3 us  [call(): pl.pallas_call(kernel, in_specs=[placed(i) for i in range(len(inputs))],...]
  transfers between devices with their start and end apart: 8 -> 8, of which waited for: 3 -> 3; matrix products, arithmetic and copies ran while one was open for 0% -> 0% of each run, Pallas kernels for 36% -> 34%
where the time goes in v6:
time: 49.5 us; the launch traced here: 49.3 us
  Pallas kernels  24.3 us (49%)
  starting transfers between devices  20.9 us (42%)
  waiting for transfers between devices  3.09 us (6%)
  between operations  0.99 us (2%)
    pallas_call x11, Pallas kernels, call(): pl.pallas_call(kernel, in_specs=[placed(i) for i in range(len(inputs))],...  24.3 us
    ppermute x2, starting transfers between devices, local(): edge_b = lax.ppermute(edge_b, 'lon', lon_b)  12.6 us
    ppermute x2, starting transfers between devices, local(): got_b = lax.ppermute(late_b, 'lat', lat_b)  5.78 us
    ppermute x2, starting transfers between devices, local(): got_a = lax.ppermute(send_a, 'lat', lat_a)  2.34 us
    ppermute x2, waiting for transfers between devices, local(): got_b = lax.ppermute(late_b, 'lat', lat_b)  1.71 us
    ppermute x2, waiting for transfers between devices, local(): got_a = lax.ppermute(send_a, 'lat', lat_a)  1.37 us
  transfers between devices with their start and end apart: 8, of which 3 were waited for; matrix products, arithmetic and copies ran while one was open for 0% of the time, Pallas kernels for 34%

profile of v6, /device:TPU:8, one launch (start us, length us, event | category | flops | bytes accessed | tf_op | source)
XLA Modules:
  0.0 49.3 jit_solution(15980447578514145661)
XLA Ops:
  0.6 1.0 %shard_map.112 = (bf16[64,1024]{1,0:T(8,128)(2,1)S(1)}, bf16[64,1024]{1,0:T(8,128)(2,1)S(1)}) custom-call(bf16[128,1024]{1,0:T(8,128)(2,1)} %bitcast.10), custom_call_target="tpu_custom_call" | custom-call | flops 100000 | bytes 262144 | tf_op jit(solution)/shard_map/pallas_call | solution.py:46
  1.6 2.2 %collective-permute-start = (bf16[64,1024]{1,0:T(8,128)(2,1)S(1)}, bf16[64,1024]{1,0:T(8,128)(2,1)S(1)}, u32[]{:S(2)}, u32[]{:S(2)}) collective-permute-start(bf16[64,1024]{1,0:T(8,128)(2,1)S(1)} %get-tuple-element.48.own_a), channel_id=1, source_target_pairs={{0,64},{128,192},{64,0},{192,128},{1,65},{129,193},{65,1},{193,129... | collective-permute-start | bytes 393224 | tf_op jit(solution)/shard_map/ppermute | solution.py:541
  3.9 4.6 %shard_map.113 = (bf16[4,128,1024]{2,1,0:T(8,128)(2,1)S(1)}, bf16[4,128,1024]{2,1,0:T(8,128)(2,1)S(1)}, f32[4,192,128]{2,1,0:T(8,128)S(1)}, bf16[64,1024]{1,0:T(...) custom-call(s32[12,16,32]{2,1,0:T(8,128)} %edges_hbm.1, s32[12,16,32]{2,1,0:T(8,128)} %mask_hbm.1, ...), custom_call_target="tpu_custom_call" | custom-call | flops 2147483648 | bytes 10665984 | tf_op jit(solution)/shard_map/pallas_call | solution.py:46
  8.5 2.6 %collective-permute-start.1 = (bf16[64,1024]{1,0:T(8,128)(2,1)S(1)}, bf16[64,1024]{1,0:T(8,128)(2,1)S(1)}, u32[]{:S(2)}, u32[]{:S(2)}) collective-permute-start(bf16[64,1024]{1,0:T(8,128)(2,1)S(1)} %get-tuple-element.57), channel_id=1, source_target_pairs={{64,128},{128,64},{0,0},{192,192},{65,129},{129,65},{1,1},{193,193... | collective-permute-start | bytes 393224 | tf_op jit(solution)/shard_map/ppermute | solution.py:552
  11.2 0.0 collective-permute-done.got_a
  11.2 3.7 %shard_map.114 = (bf16[192,1024]{1,0:T(8,128)(2,1)S(1)}, bf16[192,1024]{1,0:T(8,128)(2,1)S(1)}, bf16[192,1024]{1,0:T(8,128)(2,1)S(1)}, bf16[128,1024]{1,0:T(8,12...) custom-call(bf16[64,1024]{1,0:T(8,128)(2,1)S(1)} %collective-permute, ...), custom_call_target="tpu_custom_call" | custom-call | flops 4000000000 | bytes 7077888 | tf_op jit(solution)/shard_map/pallas_call | solution.py:46
  14.8 0.6 %collective-permute-done.1.got_b = bf16[64,1024]{1,0:T(8,128)(2,1)S(1)} collective-permute-done((bf16[64,1024]{1,0:T(8,128)(2,1)S(1)}, bf16[64,1024]{1,0:T(8,128)(2,1)S(1)}, u32[]{:S(2)}, u32[]{:S(2)}) %collective-permute-start.1) | collective-permute-done | bytes 131104 | tf_op jit(solution)/shard_map/ppermute | solution.py:552
  15.4 0.2 shard_map.115
  15.6 0.1 collective-permute-start.2
  15.7 7.6 %collective-permute-start.3 = (bf16[64,1024]{1,0:T(8,128)(2,1)S(1)}, bf16[64,1024]{1,0:T(8,128)(2,1)S(1)}, u32[]{:S(2)}, u32[]{:S(2)}) collective-permute-start(bf16[64,1024]{1,0:T(8,128)(2,1)S(1)} %get-tuple-element.63), channel_id=1, source_target_pairs={{1,2},{3,4},{5,6},{7,8},{9,10},{11,12},{13,14},{15,16},{17,18},{19... | collective-permute-start | bytes 393224 | tf_op jit(solution)/shard_map/ppermute | solution.py:564
  23.3 0.0 collective-permute-done.2.got_a
  23.3 2.7 %shard_map.116 = (bf16[256,1024]{1,0:T(8,128)(2,1)S(1)}, bf16[256,1024]{1,0:T(8,128)(2,1)S(1)}, bf16[128,1024]{1,0:T(8,128)(2,1)S(1)}, bf16[128,1024]{1,0:T(8,12...) custom-call(bf16[64,1024]{1,0:T(8,128)(2,1)S(1)} %collective-permute, ...), custom_call_target="tpu_custom_call" | custom-call | flops 4000000000 | bytes 7733248 | tf_op jit(solution)/shard_map/pallas_call | solution.py:46
  26.0 0.0 collective-permute-done.3.got_b
  26.0 3.4 %shard_map.117 = (bf16[128,1024]{1,0:T(8,128)(2,1)S(1)}, bf16[128,1024]{1,0:T(8,128)(2,1)S(1)}, f32[128,1024]{1,0:T(8,128)S(1)}, f32[128,1024]{1,0:T(8,128)S(1)}...) custom-call(bf16[64,1024]{1,0:T(8,128)(2,1)S(1)} %collective-permute-done.3.got_b, ...), custom_call_target="tpu_custom_call" | custom-call | flops 4000000000 | bytes 12320768 | tf_op jit(solution)/shard_map/pallas_call | solution.py:46
  29.4 0.1 collective-permute-start.4
  29.5 5.1 %collective-permute-start.5 = (bf16[64,1024]{1,0:T(8,128)(2,1)S(1)}, bf16[64,1024]{1,0:T(8,128)(2,1)S(1)}, u32[]{:S(2)}, u32[]{:S(2)}) collective-permute-start(bf16[64,1024]{1,0:T(8,128)(2,1)S(1)} %get-tuple-element.80), channel_id=1, source_target_pairs={{1,2},{3,4},{5,6},{7,8},{9,10},{11,12},{13,14},{15,16},{17,18},{19... | collective-permute-start | bytes 393224 | tf_op jit(solution)/shard_map/ppermute | solution.py:576
  34.6 0.0 copy-start
  34.6 0.0 copy-start.3
  34.6 3.1 %shard_map.118 = (bf16[128,1024]{1,0:T(8,128)(2,1)S(1)}, bf16[128,1024]{1,0:T(8,128)(2,1)S(1)}, f32[128,1024]{1,0:T(8,128)S(1)}, bf16[128,1024]{1,0:T(8,128)(2,1)S(1)}, bf16[128,1024]{1,0:T(8,128)(2,1)S(1)}) custom-call(bf16[256,1024]{1,0:T(8,128)(2,1)S(1)} %get-tuple-element.64.k_ref, bf16[256,1024]{1,0:T(8,128)(2,1)S(1)} %get-tuple-element.65.v_ref, ...), custom_call_target="tpu_custom_call" | custom-call | flops 4000000000 | bytes 11403264 | tf_op jit(solution)/shard_map/pallas_call | solution.py:46
  37.7 0.0 collective-permute-done.4.got_a
  37.7 0.0 collective-permute-done.5.got_b
  37.7 0.1 shard_map.119
  37.8 0.0 copy-done
  37.8 0.0 copy-done.3
  37.8 0.0 copy-start.1
  37.8 0.0 copy-start.2
  37.8 2.1 %shard_map.120 = (bf16[512,1024]{1,0:T(8,128)(2,1)}, bf16[64,1024]{1,0:T(8,128)(2,1)S(1)}) custom-call(bf16[512,1024]{1,0:T(8,128)(2,1)S(1)} %bitcast.9, bf16[128,1024]{1,0:T(8,128)(2,1)S(1)} %get-tuple-element.55.first, bf16[128,1024]{1,0:T(8,128)(2,1)S(1)} %get-tuple-element.62.near, bf16[128,1024]{1,0:T(8,128)(2,1)S(1)} %get-tuple-element.70.far, ...), custom_call_target="tpu_custom_call" | custom-call | flops 1073741824 | bytes 4325376 | tf_op jit(solution)/shard_map/pallas_call | solution.py:46
  40.0 3.2 %collective-permute-start.7 = (bf16[64,1024]{1,0:T(8,128)(2,1)S(1)}, bf16[64,1024]{1,0:T(8,128)(2,1)S(1)}, u32[]{:S(2)}, u32[]{:S(2)}) collective-permute-start(bf16[64,1024]{1,0:T(8,128)(2,1)S(1)} %get-tuple-element.92), channel_id=1, source_target_pairs={{64,128},{128,64},{0,0},{192,192},{65,129},{129,65},{1,1},{193,193... | collective-permute-start | bytes 393224 | tf_op jit(solution)/shard_map/ppermute | solution.py:590
  43.1 0.1 collective-permute-start.6
  43.2 0.0 copy-done.1
  43.3 0.0 copy-done.2
  43.3 2.4 %shard_map.121 = (bf16[512,1024]{1,0:T(8,128)(2,1)}, f32[128,1024]{1,0:T(8,128)S(1)}) custom-call(bf16[512,1024]{1,0:T(8,128)(2,1)S(1)} %bitcast.7, bf16[128,1024]{1,0:T(8,128)(2,1)S(1)} %get-tuple-element.83.first, bf16[128,1024]{1,0:T(8,128)(2,1)S(1)} %get-tuple-element.84.near, bf16[128,1024]{1,0:T(8,128)(2,1)S(1)} %get-tuple-element.85.far, ...), custom_call_target="tpu_custom_call" | custom-call | flops 1073741824 | bytes 9175040 | tf_op jit(solution)/shard_map/pallas_call | solution.py:46
  45.7 1.1 %collective-permute-done.7.got_b = bf16[64,1024]{1,0:T(8,128)(2,1)S(1)} collective-permute-done((bf16[64,1024]{1,0:T(8,128)(2,1)S(1)}, bf16[64,1024]{1,0:T(8,128)(2,1)S(1)}, u32[]{:S(2)}, u32[]{:S(2)}) %collective-permute-start.7) | collective-permute-done | bytes 131104 | tf_op jit(solution)/shard_map/ppermute | solution.py:590
  46.8 1.4 %collective-permute-done.6.got_a = bf16[64,1024]{1,0:T(8,128)(2,1)S(1)} collective-permute-done((bf16[64,1024]{1,0:T(8,128)(2,1)S(1)}, bf16[64,1024]{1,0:T(8,128)(2,1)S(1)}, u32[]{:S(2)}, u32[]{:S(2)}) %collective-permute-start.6) | collective-permute-done | bytes 131104 | tf_op jit(solution)/shard_map/ppermute | solution.py:583
  48.2 0.9 %shard_map.122 = bf16[128,1024]{1,0:T(8,128)(2,1)} custom-call(f32[128,1024]{1,0:T(8,128)S(1)} %get-tuple-element.90.own_ref, bf16[64,1024]{1,0:T(8,128)(2,1)S(1)} %collective-permute-done.6.got_a, bf16[64,1024]{1,0:T(8,128)(2,1)S(1)} %collective-permute-done.7.got_b), custom_call_target="tpu_custom_call" | custom-call | flops 1000000 | bytes 786432 | tf_op jit(solution)/shard_map/pallas_call | solution.py:46
Async XLA Ops:
  1.6 9.5 %collective-permute-start = (bf16[64,1024]{1,0:T(8,128)(2,1)S(1)}, bf16[64,1024]{1,0:T(8,128)(2,1)S(1)}, u32[]{:S(2)}, u32[]{:S(2)}) collective-permute-start(bf16[64,1024]{1,0:T(8,128)(2,1)S(1)} %get-tuple-element.48.own_a), channel_id=1, source_target_pairs={{0,64},{128,192},{64,0},{192,128},{1,65},{129,193},{65,1},{193,129... | collective-permute-start | bytes 393224 | tf_op jit(solution)/shard_map/ppermute | solution.py:541
  8.5 6.9 %collective-permute-start.1 = (bf16[64,1024]{1,0:T(8,128)(2,1)S(1)}, bf16[64,1024]{1,0:T(8,128)(2,1)S(1)}, u32[]{:S(2)}, u32[]{:S(2)}) collective-permute-start(bf16[64,1024]{1,0:T(8,128)(2,1)S(1)} %get-tuple-element.57), channel_id=1, source_target_pairs={{64,128},{128,64},{0,0},{192,192},{65,129},{129,65},{1,1},{193,193... | collective-permute-start | bytes 393224 | tf_op jit(solution)/shard_map/ppermute | solution.py:552
  15.6 7.7 %collective-permute-start.2 = (bf16[64,1024]{1,0:T(8,128)(2,1)S(1)}, bf16[64,1024]{1,0:T(8,128)(2,1)S(1)}, u32[]{:S(2)}, u32[]{:S(2)}) collective-permute-start(bf16[64,1024]{1,0:T(8,128)(2,1)S(1)} %get-tuple-element.58), channel_id=1, source_target_pairs={{0,1},{2,3},{4,5},{6,7},{8,9},{10,11},{12,13},{14,15},{16,17},{18,... | collective-permute-start | bytes 393224 | tf_op jit(solution)/shard_map/ppermute | solution.py:563
  15.7 10.3 %collective-permute-start.3 = (bf16[64,1024]{1,0:T(8,128)(2,1)S(1)}, bf16[64,1024]{1,0:T(8,128)(2,1)S(1)}, u32[]{:S(2)}, u32[]{:S(2)}) collective-permute-start(bf16[64,1024]{1,0:T(8,128)(2,1)S(1)} %get-tuple-element.63), channel_id=1, source_target_pairs={{1,2},{3,4},{5,6},{7,8},{9,10},{11,12},{13,14},{15,16},{17,18},{19... | collective-permute-start | bytes 393224 | tf_op jit(solution)/shard_map/ppermute | solution.py:564
  29.4 8.3 %collective-permute-start.4 = (bf16[64,1024]{1,0:T(8,128)(2,1)S(1)}, bf16[64,1024]{1,0:T(8,128)(2,1)S(1)}, u32[]{:S(2)}, u32[]{:S(2)}) collective-permute-start(bf16[64,1024]{1,0:T(8,128)(2,1)S(1)} %get-tuple-element.79), channel_id=1, source_target_pairs={{0,1},{2,3},{4,5},{6,7},{8,9},{10,11},{12,13},{14,15},{16,17},{18,... | collective-permute-start | bytes 393224 | tf_op jit(solution)/shard_map/ppermute | solution.py:575
  29.5 8.2 %collective-permute-start.5 = (bf16[64,1024]{1,0:T(8,128)(2,1)S(1)}, bf16[64,1024]{1,0:T(8,128)(2,1)S(1)}, u32[]{:S(2)}, u32[]{:S(2)}) collective-permute-start(bf16[64,1024]{1,0:T(8,128)(2,1)S(1)} %get-tuple-element.80), channel_id=1, source_target_pairs={{1,2},{3,4},{5,6},{7,8},{9,10},{11,12},{13,14},{15,16},{17,18},{19... | collective-permute-start | bytes 393224 | tf_op jit(solution)/shard_map/ppermute | solution.py:576
  34.6 3.2 %copy-start = (bf16[1024,1024]{1,0:T(8,128)(2,1)S(1)}, bf16[1024,1024]{1,0:T(8,128)(2,1)}, u32[]{:S(2)}) copy-start(bf16[1024,1024]{1,0:T(8,128)(2,1)} %wo_ref.1) | copy-start | bytes 6291460
  34.6 3.2 %copy-start.3 = (bf16[16,32,1024]{2,1,0:T(8,128)(2,1)S(1)}, bf16[16,32,1024]{2,1,0:T(8,128)(2,1)}, u32[]{:S(2)}) copy-start(bf16[16,32,1024]{2,1,0:T(8,128)(2,1)} %param.9) | copy-start | bytes 3145732
  37.8 5.5 %copy-start.1 = (bf16[1024,1024]{1,0:T(8,128)(2,1)S(1)}, bf16[1024,1024]{1,0:T(8,128)(2,1)}, u32[]{:S(2)}) copy-start(bf16[1024,1024]{1,0:T(8,128)(2,1)} %wq_ref.1) | copy-start | bytes 6291460
  37.8 5.4 %copy-start.2 = (bf16[16,32,1024]{2,1,0:T(8,128)(2,1)S(1)}, bf16[16,32,1024]{2,1,0:T(8,128)(2,1)}, u32[]{:S(2)}) copy-start(bf16[16,32,1024]{2,1,0:T(8,128)(2,1)} %param.17) | copy-start | bytes 3145732
  40.0 6.9 %collective-permute-start.7 = (bf16[64,1024]{1,0:T(8,128)(2,1)S(1)}, bf16[64,1024]{1,0:T(8,128)(2,1)S(1)}, u32[]{:S(2)}, u32[]{:S(2)}) collective-permute-start(bf16[64,1024]{1,0:T(8,128)(2,1)S(1)} %get-tuple-element.92), channel_id=1, source_target_pairs={{64,128},{128,64},{0,0},{192,192},{65,129},{129,65},{1,1},{193,193... | collective-permute-start | bytes 393224 | tf_op jit(solution)/shard_map/ppermute | solution.py:590
  43.1 5.1 %collective-permute-start.6 = (bf16[64,1024]{1,0:T(8,128)(2,1)S(1)}, bf16[64,1024]{1,0:T(8,128)(2,1)S(1)}, u32[]{:S(2)}, u32[]{:S(2)}) collective-permute-start(bf16[64,1024]{1,0:T(8,128)(2,1)S(1)} %get-tuple-element.91), channel_id=1, source_target_pairs={{0,64},{128,192},{64,0},{192,128},{1,65},{129,193},{65,1},{193,129... | collective-permute-start | bytes 393224 | tf_op jit(solution)/shard_map/ppermute | solution.py:583

commit v7 on v6

--- a/solution.py
+++ b/solution.py
@@ -510,15 +510,11 @@
         copy.wait()
 
 
-def pairs_of(axis, ring):
+def pairs_of(axis):
     count = lax.axis_size(axis)
     even = [(i, i + 1) for i in range(0, count, 2)]
-    odd = [(i, i + 1) for i in range(1, count - 1, 2)]
-    alone = [] if ring else [(0, 0), (count - 1, count - 1)]
-    if ring:
-        odd.append((count - 1, 0))
-    even, odd = (pairs + [(b, a) for a, b in pairs] for pairs in (even, odd))
-    return even, odd + alone
+    odd = [(i, (i + 1) % count) for i in range(1, count, 2)]
+    return [pairs + [(b, a) for a, b in pairs] for pairs in (even, odd)]
 
 
 def local(grid_feat, mesh_feat, edges, edge_mask, w_query, w_key, w_value, w_out, cotangent):
@@ -528,8 +524,8 @@
     c = cotangent.reshape(points, width)
     own = mesh_feat.reshape(2 * BLOCK, width)
     product = 2 * width * width
-    lat_a, lat_b = pairs_of("lat", False)
-    lon_a, lon_b = pairs_of("lon", True)
+    lat_a, lat_b = pairs_of("lat")
+    lon_a, lon_b = pairs_of("lon")
     piece = ((BLOCK, width), BF)
     tiled = ((TILES, POINTS, width), BF)
     square = ((width, width), BF)

time: 49.5 us -> 46.2 us (0.933)
  waiting for transfers between devices: 3.09 us -> 1.11 us
  starting transfers between devices: 20.9 us -> 19.8 us
    ppermute x2, starting transfers between devices: 5.78 us -> 2.15 us  [local(): got_b = lax.ppermute(late_b, 'lat', lat_b)]
    ppermute x2, starting transfers between devices: 2.34 us -> 4.8 us  [local(): got_a = lax.ppermute(send_a, 'lat', lat_a)]
    ppermute x2, waiting for transfers between devices: 1.71 us -> 0.59 us  [local(): got_b = lax.ppermute(late_b, 'lat', lat_b)]
    ppermute x2, waiting for transfers between devices: 1.37 us -> 0.51 us  [local(): got_a = lax.ppermute(send_a, 'lat', lat_a)]
  transfers between devices with their start and end apart: 8 -> 8, of which waited for: 3 -> 2; matrix products, arithmetic and copies ran while one was open for 0% -> 0% of each run, Pallas kernels for 34% -> 36%
where the time goes in v7:
time: 46.2 us; the launch traced here: 46.1 us
  Pallas kernels  24.3 us (53%)
  starting transfers between devices  19.8 us (43%)
  waiting for transfers between devices  1.11 us (2%)
  between operations  0.95 us (2%)
    pallas_call x11, Pallas kernels, call(): pl.pallas_call(kernel, in_specs=[placed(i) for i in range(len(inputs))],...  24.3 us
    ppermute x2, starting transfers between devices, local(): edge_b = lax.ppermute(edge_b, 'lon', lon_b)  12.6 us
    ppermute x2, starting transfers between devices, local(): got_a = lax.ppermute(send_a, 'lat', lat_a)  4.8 us
    ppermute x2, starting transfers between devices, local(): got_b = lax.ppermute(late_b, 'lat', lat_b)  2.15 us
  transfers between devices with their start and end apart: 8, of which 2 were waited for; matrix products, arithmetic and copies ran while one was open for 0% of the time, Pallas kernels for 36%

profile of v7, /device:TPU:8, one launch (start us, length us, event | category | flops | bytes accessed | tf_op | source)
XLA Modules:
  0.0 46.1 jit_solution(9512674403476792983)
XLA Ops:
  0.6 1.0 %shard_map.112 = (bf16[64,1024]{1,0:T(8,128)(2,1)S(1)}, bf16[64,1024]{1,0:T(8,128)(2,1)S(1)}) custom-call(bf16[128,1024]{1,0:T(8,128)(2,1)} %bitcast.10), custom_call_target="tpu_custom_call" | custom-call | flops 100000 | bytes 262144 | tf_op jit(solution)/shard_map/pallas_call | solution.py:46
  1.6 2.2 %collective-permute-start = (bf16[64,1024]{1,0:T(8,128)(2,1)S(1)}, bf16[64,1024]{1,0:T(8,128)(2,1)S(1)}, u32[]{:S(2)}, u32[]{:S(2)}) collective-permute-start(bf16[64,1024]{1,0:T(8,128)(2,1)S(1)} %get-tuple-element.48.own_a), channel_id=1, source_target_pairs={{0,64},{128,192},{64,0},{192,128},{1,65},{129,193},{65,1},{193,129... | collective-permute-start | bytes 393224 | tf_op jit(solution)/shard_map/ppermute | solution.py:537
  3.9 4.6 %shard_map.113 = (bf16[4,128,1024]{2,1,0:T(8,128)(2,1)S(1)}, bf16[4,128,1024]{2,1,0:T(8,128)(2,1)S(1)}, f32[4,192,128]{2,1,0:T(8,128)S(1)}, bf16[64,1024]{1,0:T(...) custom-call(s32[12,16,32]{2,1,0:T(8,128)} %edges_hbm.1, s32[12,16,32]{2,1,0:T(8,128)} %mask_hbm.1, ...), custom_call_target="tpu_custom_call" | custom-call | flops 2147483648 | bytes 10665984 | tf_op jit(solution)/shard_map/pallas_call | solution.py:46
  8.5 0.8 %collective-permute-start.1 = (bf16[64,1024]{1,0:T(8,128)(2,1)S(1)}, bf16[64,1024]{1,0:T(8,128)(2,1)S(1)}, u32[]{:S(2)}, u32[]{:S(2)}) collective-permute-start(bf16[64,1024]{1,0:T(8,128)(2,1)S(1)} %get-tuple-element.57), channel_id=1, source_target_pairs={{64,128},{192,0},{128,64},{0,192},{65,129},{193,1},{129,65},{1,193... | collective-permute-start | bytes 393224 | tf_op jit(solution)/shard_map/ppermute | solution.py:548
  9.3 0.0 collective-permute-done.got_a
  9.3 3.7 %shard_map.114 = (bf16[192,1024]{1,0:T(8,128)(2,1)S(1)}, bf16[192,1024]{1,0:T(8,128)(2,1)S(1)}, bf16[192,1024]{1,0:T(8,128)(2,1)S(1)}, bf16[128,1024]{1,0:T(8,12...) custom-call(bf16[64,1024]{1,0:T(8,128)(2,1)S(1)} %collective-permute, ...), custom_call_target="tpu_custom_call" | custom-call | flops 4000000000 | bytes 7077888 | tf_op jit(solution)/shard_map/pallas_call | solution.py:46
  13.0 0.6 %collective-permute-done.1.got_b = bf16[64,1024]{1,0:T(8,128)(2,1)S(1)} collective-permute-done((bf16[64,1024]{1,0:T(8,128)(2,1)S(1)}, bf16[64,1024]{1,0:T(8,128)(2,1)S(1)}, u32[]{:S(2)}, u32[]{:S(2)}) %collective-permute-start.1) | collective-permute-done | bytes 131104 | tf_op jit(solution)/shard_map/ppermute | solution.py:548
  13.6 0.2 shard_map.115
  13.8 0.1 collective-permute-start.2
  13.9 7.6 %collective-permute-start.3 = (bf16[64,1024]{1,0:T(8,128)(2,1)S(1)}, bf16[64,1024]{1,0:T(8,128)(2,1)S(1)}, u32[]{:S(2)}, u32[]{:S(2)}) collective-permute-start(bf16[64,1024]{1,0:T(8,128)(2,1)S(1)} %get-tuple-element.63), channel_id=1, source_target_pairs={{1,2},{3,4},{5,6},{7,8},{9,10},{11,12},{13,14},{15,16},{17,18},{19... | collective-permute-start | bytes 393224 | tf_op jit(solution)/shard_map/ppermute | solution.py:560
  21.5 0.0 collective-permute-done.2.got_a
  21.5 2.7 %shard_map.116 = (bf16[256,1024]{1,0:T(8,128)(2,1)S(1)}, bf16[256,1024]{1,0:T(8,128)(2,1)S(1)}, bf16[128,1024]{1,0:T(8,128)(2,1)S(1)}, bf16[128,1024]{1,0:T(8,12...) custom-call(bf16[64,1024]{1,0:T(8,128)(2,1)S(1)} %collective-permute, ...), custom_call_target="tpu_custom_call" | custom-call | flops 4000000000 | bytes 7733248 | tf_op jit(solution)/shard_map/pallas_call | solution.py:46
  24.2 0.0 collective-permute-done.3.got_b
  24.2 3.4 %shard_map.117 = (bf16[128,1024]{1,0:T(8,128)(2,1)S(1)}, bf16[128,1024]{1,0:T(8,128)(2,1)S(1)}, f32[128,1024]{1,0:T(8,128)S(1)}, f32[128,1024]{1,0:T(8,128)S(1)}...) custom-call(bf16[64,1024]{1,0:T(8,128)(2,1)S(1)} %collective-permute-done.3.got_b, ...), custom_call_target="tpu_custom_call" | custom-call | flops 4000000000 | bytes 12320768 | tf_op jit(solution)/shard_map/pallas_call | solution.py:46
  27.6 0.1 collective-permute-start.4
  27.7 5.1 %collective-permute-start.5 = (bf16[64,1024]{1,0:T(8,128)(2,1)S(1)}, bf16[64,1024]{1,0:T(8,128)(2,1)S(1)}, u32[]{:S(2)}, u32[]{:S(2)}) collective-permute-start(bf16[64,1024]{1,0:T(8,128)(2,1)S(1)} %get-tuple-element.80), channel_id=1, source_target_pairs={{1,2},{3,4},{5,6},{7,8},{9,10},{11,12},{13,14},{15,16},{17,18},{19... | collective-permute-start | bytes 393224 | tf_op jit(solution)/shard_map/ppermute | solution.py:572
  32.8 0.0 copy-start
  32.8 0.0 copy-start.3
  32.8 3.1 %shard_map.118 = (bf16[128,1024]{1,0:T(8,128)(2,1)S(1)}, bf16[128,1024]{1,0:T(8,128)(2,1)S(1)}, f32[128,1024]{1,0:T(8,128)S(1)}, bf16[128,1024]{1,0:T(8,128)(2,1)S(1)}, bf16[128,1024]{1,0:T(8,128)(2,1)S(1)}) custom-call(bf16[256,1024]{1,0:T(8,128)(2,1)S(1)} %get-tuple-element.64.k_ref, bf16[256,1024]{1,0:T(8,128)(2,1)S(1)} %get-tuple-element.65.v_ref, ...), custom_call_target="tpu_custom_call" | custom-call | flops 4000000000 | bytes 11403264 | tf_op jit(solution)/shard_map/pallas_call | solution.py:46
  35.9 0.0 collective-permute-done.4.got_a
  35.9 0.0 collective-permute-done.5.got_b
  35.9 0.1 shard_map.119
  36.0 0.0 copy-done
  36.0 0.0 copy-done.3
  36.0 0.0 copy-start.1
  36.0 0.0 copy-start.2
  36.0 2.1 %shard_map.120 = (bf16[512,1024]{1,0:T(8,128)(2,1)}, bf16[64,1024]{1,0:T(8,128)(2,1)S(1)}) custom-call(bf16[512,1024]{1,0:T(8,128)(2,1)S(1)} %bitcast.9, bf16[128,1024]{1,0:T(8,128)(2,1)S(1)} %get-tuple-element.55.first, bf16[128,1024]{1,0:T(8,128)(2,1)S(1)} %get-tuple-element.62.near, bf16[128,1024]{1,0:T(8,128)(2,1)S(1)} %get-tuple-element.70.far, ...), custom_call_target="tpu_custom_call" | custom-call | flops 1073741824 | bytes 4325376 | tf_op jit(solution)/shard_map/pallas_call | solution.py:46
  38.1 1.4 %collective-permute-start.7 = (bf16[64,1024]{1,0:T(8,128)(2,1)S(1)}, bf16[64,1024]{1,0:T(8,128)(2,1)S(1)}, u32[]{:S(2)}, u32[]{:S(2)}) collective-permute-start(bf16[64,1024]{1,0:T(8,128)(2,1)S(1)} %get-tuple-element.92), channel_id=1, source_target_pairs={{64,128},{192,0},{128,64},{0,192},{65,129},{193,1},{129,65},{1,193... | collective-permute-start | bytes 393224 | tf_op jit(solution)/shard_map/ppermute | solution.py:586
  39.5 2.6 %collective-permute-start.6 = (bf16[64,1024]{1,0:T(8,128)(2,1)S(1)}, bf16[64,1024]{1,0:T(8,128)(2,1)S(1)}, u32[]{:S(2)}, u32[]{:S(2)}) collective-permute-start(bf16[64,1024]{1,0:T(8,128)(2,1)S(1)} %get-tuple-element.91), channel_id=1, source_target_pairs={{0,64},{128,192},{64,0},{192,128},{1,65},{129,193},{65,1},{193,129... | collective-permute-start | bytes 393224 | tf_op jit(solution)/shard_map/ppermute | solution.py:579
  42.1 0.0 copy-done.1
  42.1 0.0 copy-done.2
  42.1 2.4 %shard_map.121 = (bf16[512,1024]{1,0:T(8,128)(2,1)}, f32[128,1024]{1,0:T(8,128)S(1)}) custom-call(bf16[512,1024]{1,0:T(8,128)(2,1)S(1)} %bitcast.7, bf16[128,1024]{1,0:T(8,128)(2,1)S(1)} %get-tuple-element.83.first, bf16[128,1024]{1,0:T(8,128)(2,1)S(1)} %get-tuple-element.84.near, bf16[128,1024]{1,0:T(8,128)(2,1)S(1)} %get-tuple-element.85.far, ...), custom_call_target="tpu_custom_call" | custom-call | flops 1073741824 | bytes 9175040 | tf_op jit(solution)/shard_map/pallas_call | solution.py:46
  44.5 0.0 collective-permute-done.7.got_b
  44.5 0.5 %collective-permute-done.6.got_a = bf16[64,1024]{1,0:T(8,128)(2,1)S(1)} collective-permute-done((bf16[64,1024]{1,0:T(8,128)(2,1)S(1)}, bf16[64,1024]{1,0:T(8,128)(2,1)S(1)}, u32[]{:S(2)}, u32[]{:S(2)}) %collective-permute-start.6) | collective-permute-done | bytes 131104 | tf_op jit(solution)/shard_map/ppermute | solution.py:579
  45.0 0.9 %shard_map.122 = bf16[128,1024]{1,0:T(8,128)(2,1)} custom-call(f32[128,1024]{1,0:T(8,128)S(1)} %get-tuple-element.90.own_ref, bf16[64,1024]{1,0:T(8,128)(2,1)S(1)} %collective-permute-done.6.got_a, bf16[64,1024]{1,0:T(8,128)(2,1)S(1)} %collective-permute-done.7.got_b), custom_call_target="tpu_custom_call" | custom-call | flops 1000000 | bytes 786432 | tf_op jit(solution)/shard_map/pallas_call | solution.py:46
Async XLA Ops:
  1.6 7.7 %collective-permute-start = (bf16[64,1024]{1,0:T(8,128)(2,1)S(1)}, bf16[64,1024]{1,0:T(8,128)(2,1)S(1)}, u32[]{:S(2)}, u32[]{:S(2)}) collective-permute-start(bf16[64,1024]{1,0:T(8,128)(2,1)S(1)} %get-tuple-element.48.own_a), channel_id=1, source_target_pairs={{0,64},{128,192},{64,0},{192,128},{1,65},{129,193},{65,1},{193,129... | collective-permute-start | bytes 393224 | tf_op jit(solution)/shard_map/ppermute | solution.py:537
  8.5 5.1 %collective-permute-start.1 = (bf16[64,1024]{1,0:T(8,128)(2,1)S(1)}, bf16[64,1024]{1,0:T(8,128)(2,1)S(1)}, u32[]{:S(2)}, u32[]{:S(2)}) collective-permute-start(bf16[64,1024]{1,0:T(8,128)(2,1)S(1)} %get-tuple-element.57), channel_id=1, source_target_pairs={{64,128},{192,0},{128,64},{0,192},{65,129},{193,1},{129,65},{1,193... | collective-permute-start | bytes 393224 | tf_op jit(solution)/shard_map/ppermute | solution.py:548
  13.8 7.7 %collective-permute-start.2 = (bf16[64,1024]{1,0:T(8,128)(2,1)S(1)}, bf16[64,1024]{1,0:T(8,128)(2,1)S(1)}, u32[]{:S(2)}, u32[]{:S(2)}) collective-permute-start(bf16[64,1024]{1,0:T(8,128)(2,1)S(1)} %get-tuple-element.58), channel_id=1, source_target_pairs={{0,1},{2,3},{4,5},{6,7},{8,9},{10,11},{12,13},{14,15},{16,17},{18,... | collective-permute-start | bytes 393224 | tf_op jit(solution)/shard_map/ppermute | solution.py:559
  13.9 10.3 %collective-permute-start.3 = (bf16[64,1024]{1,0:T(8,128)(2,1)S(1)}, bf16[64,1024]{1,0:T(8,128)(2,1)S(1)}, u32[]{:S(2)}, u32[]{:S(2)}) collective-permute-start(bf16[64,1024]{1,0:T(8,128)(2,1)S(1)} %get-tuple-element.63), channel_id=1, source_target_pairs={{1,2},{3,4},{5,6},{7,8},{9,10},{11,12},{13,14},{15,16},{17,18},{19... | collective-permute-start | bytes 393224 | tf_op jit(solution)/shard_map/ppermute | solution.py:560
  27.6 8.3 %collective-permute-start.4 = (bf16[64,1024]{1,0:T(8,128)(2,1)S(1)}, bf16[64,1024]{1,0:T(8,128)(2,1)S(1)}, u32[]{:S(2)}, u32[]{:S(2)}) collective-permute-start(bf16[64,1024]{1,0:T(8,128)(2,1)S(1)} %get-tuple-element.79), channel_id=1, source_target_pairs={{0,1},{2,3},{4,5},{6,7},{8,9},{10,11},{12,13},{14,15},{16,17},{18,... | collective-permute-start | bytes 393224 | tf_op jit(solution)/shard_map/ppermute | solution.py:571
  27.7 8.2 %collective-permute-start.5 = (bf16[64,1024]{1,0:T(8,128)(2,1)S(1)}, bf16[64,1024]{1,0:T(8,128)(2,1)S(1)}, u32[]{:S(2)}, u32[]{:S(2)}) collective-permute-start(bf16[64,1024]{1,0:T(8,128)(2,1)S(1)} %get-tuple-element.80), channel_id=1, source_target_pairs={{1,2},{3,4},{5,6},{7,8},{9,10},{11,12},{13,14},{15,16},{17,18},{19... | collective-permute-start | bytes 393224 | tf_op jit(solution)/shard_map/ppermute | solution.py:572
  32.8 3.2 %copy-start = (bf16[1024,1024]{1,0:T(8,128)(2,1)S(1)}, bf16[1024,1024]{1,0:T(8,128)(2,1)}, u32[]{:S(2)}) copy-start(bf16[1024,1024]{1,0:T(8,128)(2,1)} %wo_ref.1) | copy-start | bytes 6291460
  32.8 3.2 %copy-start.3 = (bf16[16,32,1024]{2,1,0:T(8,128)(2,1)S(1)}, bf16[16,32,1024]{2,1,0:T(8,128)(2,1)}, u32[]{:S(2)}) copy-start(bf16[16,32,1024]{2,1,0:T(8,128)(2,1)} %param.9) | copy-start | bytes 3145732
  36.0 6.1 %copy-start.1 = (bf16[1024,1024]{1,0:T(8,128)(2,1)S(1)}, bf16[1024,1024]{1,0:T(8,128)(2,1)}, u32[]{:S(2)}) copy-start(bf16[1024,1024]{1,0:T(8,128)(2,1)} %wq_ref.1) | copy-start | bytes 6291460
  36.0 6.1 %copy-start.2 = (bf16[16,32,1024]{2,1,0:T(8,128)(2,1)S(1)}, bf16[16,32,1024]{2,1,0:T(8,128)(2,1)}, u32[]{:S(2)}) copy-start(bf16[16,32,1024]{2,1,0:T(8,128)(2,1)} %param.17) | copy-start | bytes 3145732
  38.1 6.4 %collective-permute-start.7 = (bf16[64,1024]{1,0:T(8,128)(2,1)S(1)}, bf16[64,1024]{1,0:T(8,128)(2,1)S(1)}, u32[]{:S(2)}, u32[]{:S(2)}) collective-permute-start(bf16[64,1024]{1,0:T(8,128)(2,1)S(1)} %get-tuple-element.92), channel_id=1, source_target_pairs={{64,128},{192,0},{128,64},{0,192},{65,129},{193,1},{129,65},{1,193... | collective-permute-start | bytes 393224 | tf_op jit(solution)/shard_map/ppermute | solution.py:586
  39.5 5.5 %collective-permute-start.6 = (bf16[64,1024]{1,0:T(8,128)(2,1)S(1)}, bf16[64,1024]{1,0:T(8,128)(2,1)S(1)}, u32[]{:S(2)}, u32[]{:S(2)}) collective-permute-start(bf16[64,1024]{1,0:T(8,128)(2,1)S(1)} %get-tuple-element.91), channel_id=1, source_target_pairs={{0,64},{128,192},{64,0},{192,128},{1,65},{129,193},{65,1},{193,129... | collective-permute-start | bytes 393224 | tf_op jit(solution)/shard_map/ppermute | solution.py:579

commit v8 on v7

--- a/solution.py
+++ b/solution.py
@@ -101,8 +101,8 @@
 
 
 def project_kernel(
-    edges_hbm, mask_hbm, x_hbm, wq_hbm, c_hbm, wo_hbm, wk_hbm, wv_hbm, piece_ref,
-    q_ref, da_ref, bias_ref, pass_ref, wk_ref, wv_ref,
+    edges_hbm, mask_hbm, x_hbm, wq_hbm, c_hbm, wo_hbm, wk_hbm, wv_hbm,
+    q_ref, da_ref, bias_ref, wk_ref, wv_ref,
     edges_scr, mask_scr, x_scr, wq_scr, c_scr, wo_scr, sem,
 ):
     pairs = (
@@ -112,7 +112,6 @@
     copies = [pltpu.make_async_copy(a, b, sem.at[i]) for i, (a, b) in enumerate(pairs)]
     for copy in copies:
         copy.start()
-    pass_ref[...] = piece_ref[...]
     copies[0].wait()
     copies[1].wait()
     make_bias(edges_scr, mask_scr, bias_ref)
@@ -467,10 +466,7 @@
     return copies
 
 
-def layer_out_kernel(
-    x_ref, first, near, far, last, wo_ref, piece_ref, out_hbm, pass_ref, out_scr, sem
-):
-    pass_ref[...] = piece_ref[...]
+def layer_out_kernel(x_ref, first, near, far, last, wo_ref, out_hbm, out_scr, sem):
     for copy in emit(x_ref, (first, near, far, last), wo_ref, NN, out_hbm, out_scr, sem):
         copy.wait()
 
@@ -535,17 +531,17 @@
         (pltpu.SemaphoreType.DMA((2,)),), hbm=(0,),
     )
     got_a = lax.ppermute(send_a, "lat", lat_a)
-    q, da, bias, late_b, wk, wv = call(
+    got_b = lax.ppermute(send_b, "lat", lat_b)
+    q, da, bias, wk, wv = call(
         project_kernel,
-        (edges, edge_mask, x, w_query, c, w_out, w_key, w_value, send_b),
-        [tiled, tiled, ((TILES, NODES, POINTS), F32), piece, square, square],
+        (edges, edge_mask, x, w_query, c, w_out, w_key, w_value),
+        [tiled, tiled, ((TILES, NODES, POINTS), F32), square, square],
         2 * points * product,
         (pltpu.VMEM(edges.shape, jnp.int32),) * 2
         + (pltpu.VMEM((points, width), BF), pltpu.VMEM((width, width), BF)) * 2
         + (pltpu.SemaphoreType.DMA((8,)),),
         hbm=tuple(range(8)),
     )
-    got_b = lax.ppermute(late_b, "lat", lat_b)
     common = (wk, wv, q, da, bias)
     rows = ((POINTS, width), BF)
     half, half_grad = ((NODES, width), BF), ((NODES, width), F32)
@@ -578,12 +574,12 @@
     send_a, send_b = call(merge_kernel, (part, edge_a, edge_b), [piece, piece], 10**8)
     got_a = lax.ppermute(send_a, "lat", lat_a)
     out_scratch = (pltpu.VMEM((points, width), BF), pltpu.SemaphoreType.DMA((4,)))
-    layer_out, late_b = call(
-        layer_out_kernel, (x, att_first, att_near, att_far, att_last, w_out, send_b),
-        [((points, width), BF), piece],
+    got_b = lax.ppermute(send_b, "lat", lat_b)
+    (layer_out,) = call(
+        layer_out_kernel, (x, att_first, att_near, att_far, att_last, w_out),
+        [((points, width), BF)],
         points * product, out_scratch, hbm_out=(0,),
     )
-    got_b = lax.ppermute(late_b, "lat", lat_b)
     grid_grad, kept = call(
         grid_grad_kernel,
         (c, dq_first, dq_near, dq_far, dq_last, w_query, dk_own, dv_own, wkt, wvt, edge_a, edge_b),

time: 46.2 us -> 43.6 us (0.944)
  starting transfers between devices: 19.8 us -> 18.2 us
  waiting for transfers between devices: 1.11 us -> 0.02 us
    ppermute x2, starting transfers between devices: 4.8 us -> 3.69 us  [local(): got_a = lax.ppermute(send_a, 'lat', lat_a)]
    ppermute x2, starting transfers between devices: 2.15 us -> 1.14 us  [local(): got_b = lax.ppermute(send_b, 'lat', lat_b)]
    ppermute x2, waiting for transfers between devices: 0.59 us -> 0.01 us  [local(): got_b = lax.ppermute(send_b, 'lat', lat_b)]
    ppermute x2, starting transfers between devices: 12.6 us -> 13.2 us  [local(): edge_b = lax.ppermute(edge_b, 'lon', lon_b)]
    ppermute x2, waiting for transfers between devices: 0.51 us -> 0.01 us  [local(): got_a = lax.ppermute(send_a, 'lat', lat_a)]
  transfers between devices with their start and end apart: 8 -> 8, of which waited for: 2 -> 0; matrix products, arithmetic and copies ran while one was open for 0% -> 0% of each run, Pallas kernels for 36% -> 43%
where the time goes in v8:
time: 43.6 us; the launch traced here: 43.5 us
  Pallas kernels  24.2 us (56%)
  starting transfers between devices  18.2 us (42%)
  between operations  0.99 us (2%)
    pallas_call x11, Pallas kernels, call(): pl.pallas_call(kernel, in_specs=[placed(i) for i in range(len(inputs))],...  24.2 us
    ppermute x2, starting transfers between devices, local(): edge_b = lax.ppermute(edge_b, 'lon', lon_b)  13.2 us
    ppermute x2, starting transfers between devices, local(): got_a = lax.ppermute(send_a, 'lat', lat_a)  3.69 us
    ppermute x2, starting transfers between devices, local(): got_b = lax.ppermute(send_b, 'lat', lat_b)  1.14 us
  transfers between devices with their start and end apart: 8, of which 0 were waited for; matrix products, arithmetic and copies ran while one was open for 0% of the time, Pallas kernels for 43%

profile of v8, /device:TPU:8, one launch (start us, length us, event | category | flops | bytes accessed | tf_op | source)
XLA Modules:
  0.0 43.5 jit_solution(18338074485832953337)
XLA Ops:
  0.6 1.0 %shard_map.112 = (bf16[64,1024]{1,0:T(8,128)(2,1)S(1)}, bf16[64,1024]{1,0:T(8,128)(2,1)S(1)}) custom-call(bf16[128,1024]{1,0:T(8,128)(2,1)} %bitcast.11), custom_call_target="tpu_custom_call" | custom-call | flops 100000 | bytes 262144 | tf_op jit(solution)/shard_map/pallas_call | solution.py:46
  1.6 2.2 %collective-permute-start = (bf16[64,1024]{1,0:T(8,128)(2,1)S(1)}, bf16[64,1024]{1,0:T(8,128)(2,1)S(1)}, u32[]{:S(2)}, u32[]{:S(2)}) collective-permute-start(bf16[64,1024]{1,0:T(8,128)(2,1)S(1)} %get-tuple-element.45.own_a), channel_id=1, source_target_pairs={{0,64},{128,192},{64,0},{192,128},{1,65},{129,193},{65,1},{193,129... | collective-permute-start | bytes 393224 | tf_op jit(solution)/shard_map/ppermute | solution.py:533
  3.9 0.7 %collective-permute-start.1 = (bf16[64,1024]{1,0:T(8,128)(2,1)S(1)}, bf16[64,1024]{1,0:T(8,128)(2,1)S(1)}, u32[]{:S(2)}, u32[]{:S(2)}) collective-permute-start(bf16[64,1024]{1,0:T(8,128)(2,1)S(1)} %get-tuple-element.46.own_b), channel_id=1, source_target_pairs={{64,128},{192,0},{128,64},{0,192},{65,129},{193,1},{129,65},{1,193... | collective-permute-start | bytes 393224 | tf_op jit(solution)/shard_map/ppermute | solution.py:534
  4.6 4.6 %shard_map.113 = (bf16[4,128,1024]{2,1,0:T(8,128)(2,1)S(1)}, bf16[4,128,1024]{2,1,0:T(8,128)(2,1)S(1)}, f32[4,192,128]{2,1,0:T(8,128)S(1)}, bf16[1024,1024]{1,0:T(8,128)(2,1)S(1)}, bf16[1024,1024]{1,0:T(8,128)(2,1)S(1)}) custom-call(s32[12,16,32]{2,1,0:T(8,128)} %edges_hbm.1, s32[12,16,32]{2,1,0:T(8,128)} %mask_hbm.1, bf16[512,1024]{1,0:T(8,128)(2,1)} %bitcast.6, ...), custom_call_target="tpu_custom_call" | custom-call | flops 2147483648 | bytes 10534912 | tf_op jit(solution)/shard_map/pallas_call | solution.py:46
  9.2 0.0 collective-permute-done.got_a
  9.2 3.7 %shard_map.114 = (bf16[192,1024]{1,0:T(8,128)(2,1)S(1)}, bf16[192,1024]{1,0:T(8,128)(2,1)S(1)}, bf16[192,1024]{1,0:T(8,128)(2,1)S(1)}, bf16[128,1024]{1,0:T(8,12...) custom-call(bf16[64,1024]{1,0:T(8,128)(2,1)S(1)} %collective-permute, ...), custom_call_target="tpu_custom_call" | custom-call | flops 4000000000 | bytes 7077888 | tf_op jit(solution)/shard_map/pallas_call | solution.py:46
  12.9 0.0 collective-permute-done.1.got_b
  12.9 0.2 shard_map.115
  13.1 0.1 collective-permute-start.2
  13.2 8.2 %collective-permute-start.3 = (bf16[64,1024]{1,0:T(8,128)(2,1)S(1)}, bf16[64,1024]{1,0:T(8,128)(2,1)S(1)}, u32[]{:S(2)}, u32[]{:S(2)}) collective-permute-start(bf16[64,1024]{1,0:T(8,128)(2,1)S(1)} %get-tuple-element.59), channel_id=1, source_target_pairs={{1,2},{3,4},{5,6},{7,8},{9,10},{11,12},{13,14},{15,16},{17,18},{19... | collective-permute-start | bytes 393224 | tf_op jit(solution)/shard_map/ppermute | solution.py:556
  21.3 0.0 collective-permute-done.2.got_a
  21.4 2.7 %shard_map.116 = (bf16[256,1024]{1,0:T(8,128)(2,1)S(1)}, bf16[256,1024]{1,0:T(8,128)(2,1)S(1)}, bf16[128,1024]{1,0:T(8,128)(2,1)S(1)}, bf16[128,1024]{1,0:T(8,12...) custom-call(bf16[64,1024]{1,0:T(8,128)(2,1)S(1)} %collective-permute, ...), custom_call_target="tpu_custom_call" | custom-call | flops 4000000000 | bytes 7733248 | tf_op jit(solution)/shard_map/pallas_call | solution.py:46
  24.1 0.0 collective-permute-done.3.got_b
  24.1 3.4 %shard_map.117 = (bf16[128,1024]{1,0:T(8,128)(2,1)S(1)}, bf16[128,1024]{1,0:T(8,128)(2,1)S(1)}, f32[128,1024]{1,0:T(8,128)S(1)}, f32[128,1024]{1,0:T(8,128)S(1)}...) custom-call(bf16[64,1024]{1,0:T(8,128)(2,1)S(1)} %collective-permute-done.3.got_b, ...), custom_call_target="tpu_custom_call" | custom-call | flops 4000000000 | bytes 12320768 | tf_op jit(solution)/shard_map/pallas_call | solution.py:46
  27.5 0.1 collective-permute-start.4
  27.6 5.0 %collective-permute-start.5 = (bf16[64,1024]{1,0:T(8,128)(2,1)S(1)}, bf16[64,1024]{1,0:T(8,128)(2,1)S(1)}, u32[]{:S(2)}, u32[]{:S(2)}) collective-permute-start(bf16[64,1024]{1,0:T(8,128)(2,1)S(1)} %get-tuple-element.81), channel_id=1, source_target_pairs={{1,2},{3,4},{5,6},{7,8},{9,10},{11,12},{13,14},{15,16},{17,18},{19... | collective-permute-start | bytes 393224 | tf_op jit(solution)/shard_map/ppermute | solution.py:568
  32.6 0.0 copy-start
  32.7 0.0 copy-start.2
  32.7 3.1 %shard_map.118 = (bf16[128,1024]{1,0:T(8,128)(2,1)S(1)}, bf16[128,1024]{1,0:T(8,128)(2,1)S(1)}, f32[128,1024]{1,0:T(8,128)S(1)}, bf16[128,1024]{1,0:T(8,128)(2,1)S(1)}, bf16[128,1024]{1,0:T(8,128)(2,1)S(1)}) custom-call(bf16[256,1024]{1,0:T(8,128)(2,1)S(1)} %get-tuple-element.60.k_ref, bf16[256,1024]{1,0:T(8,128)(2,1)S(1)} %get-tuple-element.61.v_ref, ...), custom_call_target="tpu_custom_call" | custom-call | flops 4000000000 | bytes 11403264 | tf_op jit(solution)/shard_map/pallas_call | solution.py:46
  35.8 0.0 collective-permute-done.4.got_a
  35.8 0.0 collective-permute-done.5.got_b
  35.8 0.1 shard_map.121
  35.9 1.4 %collective-permute-start.6 = (bf16[64,1024]{1,0:T(8,128)(2,1)S(1)}, bf16[64,1024]{1,0:T(8,128)(2,1)S(1)}, u32[]{:S(2)}, u32[]{:S(2)}) collective-permute-start(bf16[64,1024]{1,0:T(8,128)(2,1)S(1)} %get-tuple-element.85), channel_id=1, source_target_pairs={{0,64},{128,192},{64,0},{192,128},{1,65},{129,193},{65,1},{193,129... | collective-permute-start | bytes 393224 | tf_op jit(solution)/shard_map/ppermute | solution.py:575
  37.3 0.4 %collective-permute-start.7 = (bf16[64,1024]{1,0:T(8,128)(2,1)S(1)}, bf16[64,1024]{1,0:T(8,128)(2,1)S(1)}, u32[]{:S(2)}, u32[]{:S(2)}) collective-permute-start(bf16[64,1024]{1,0:T(8,128)(2,1)S(1)} %get-tuple-element.86), channel_id=1, source_target_pairs={{64,128},{192,0},{128,64},{0,192},{65,129},{193,1},{129,65},{1,193... | collective-permute-start | bytes 393224 | tf_op jit(solution)/shard_map/ppermute | solution.py:577
  37.7 0.0 copy-done
  37.7 0.0 copy-done.2
  37.7 0.0 copy-start.1
  37.7 0.0 copy-start.3
  37.8 2.1 %shard_map.119 = bf16[512,1024]{1,0:T(8,128)(2,1)} custom-call(bf16[512,1024]{1,0:T(8,128)(2,1)S(1)} %bitcast.7, bf16[128,1024]{1,0:T(8,128)(2,1)S(1)} %get-tuple-element.52.first, bf16[128,1024]{1,0:T(8,128)(2,1)S(1)} %get-tuple-element.58.near, bf16[128,1024]{1,0:T(8,128)(2,1)S(1)} %get-tuple-element.66.far, bf16[128,1024]{1,0:T(8,128)(2,1)S(1)} %get-tuple-element.73.last, ...), custom_call_target="tpu_custom_call" | custom-call | flops 1073741824 | bytes 4194304 | tf_op jit(solution)/shard_map/pallas_call | solution.py:46
  39.9 0.0 copy-done.1
  39.9 0.0 copy-done.3
  39.9 2.4 %shard_map.120 = (bf16[512,1024]{1,0:T(8,128)(2,1)}, f32[128,1024]{1,0:T(8,128)S(1)}) custom-call(bf16[512,1024]{1,0:T(8,128)(2,1)S(1)} %bitcast.9, bf16[128,1024]{1,0:T(8,128)(2,1)S(1)} %get-tuple-element.74.first, bf16[128,1024]{1,0:T(8,128)(2,1)S(1)} %get-tuple-element.75.near, bf16[128,1024]{1,0:T(8,128)(2,1)S(1)} %get-tuple-element.76.far, ...), custom_call_target="tpu_custom_call" | custom-call | flops 1073741824 | bytes 9175040 | tf_op jit(solution)/shard_map/pallas_call | solution.py:46
  42.3 0.0 collective-permute-done.6.got_a
  42.3 0.0 collective-permute-done.7.got_b
  42.4 0.9 %shard_map.122 = bf16[128,1024]{1,0:T(8,128)(2,1)} custom-call(f32[128,1024]{1,0:T(8,128)S(1)} %get-tuple-element.83.own_ref, bf16[64,1024]{1,0:T(8,128)(2,1)S(1)} %collective-permute-done.6.got_a, bf16[64,1024]{1,0:T(8,128)(2,1)S(1)} %collective-permute-done.7.got_b), custom_call_target="tpu_custom_call" | custom-call | flops 1000000 | bytes 786432 | tf_op jit(solution)/shard_map/pallas_call | solution.py:46
Async XLA Ops:
  1.6 7.6 %collective-permute-start = (bf16[64,1024]{1,0:T(8,128)(2,1)S(1)}, bf16[64,1024]{1,0:T(8,128)(2,1)S(1)}, u32[]{:S(2)}, u32[]{:S(2)}) collective-permute-start(bf16[64,1024]{1,0:T(8,128)(2,1)S(1)} %get-tuple-element.45.own_a), channel_id=1, source_target_pairs={{0,64},{128,192},{64,0},{192,128},{1,65},{129,193},{65,1},{193,129... | collective-permute-start | bytes 393224 | tf_op jit(solution)/shard_map/ppermute | solution.py:533
  3.9 9.0 %collective-permute-start.1 = (bf16[64,1024]{1,0:T(8,128)(2,1)S(1)}, bf16[64,1024]{1,0:T(8,128)(2,1)S(1)}, u32[]{:S(2)}, u32[]{:S(2)}) collective-permute-start(bf16[64,1024]{1,0:T(8,128)(2,1)S(1)} %get-tuple-element.46.own_b), channel_id=1, source_target_pairs={{64,128},{192,0},{128,64},{0,192},{65,129},{193,1},{129,65},{1,193... | collective-permute-start | bytes 393224 | tf_op jit(solution)/shard_map/ppermute | solution.py:534
  13.1 8.3 %collective-permute-start.2 = (bf16[64,1024]{1,0:T(8,128)(2,1)S(1)}, bf16[64,1024]{1,0:T(8,128)(2,1)S(1)}, u32[]{:S(2)}, u32[]{:S(2)}) collective-permute-start(bf16[64,1024]{1,0:T(8,128)(2,1)S(1)} %get-tuple-element.54), channel_id=1, source_target_pairs={{0,1},{2,3},{4,5},{6,7},{8,9},{10,11},{12,13},{14,15},{16,17},{18,... | collective-permute-start | bytes 393224 | tf_op jit(solution)/shard_map/ppermute | solution.py:555
  13.2 10.9 %collective-permute-start.3 = (bf16[64,1024]{1,0:T(8,128)(2,1)S(1)}, bf16[64,1024]{1,0:T(8,128)(2,1)S(1)}, u32[]{:S(2)}, u32[]{:S(2)}) collective-permute-start(bf16[64,1024]{1,0:T(8,128)(2,1)S(1)} %get-tuple-element.59), channel_id=1, source_target_pairs={{1,2},{3,4},{5,6},{7,8},{9,10},{11,12},{13,14},{15,16},{17,18},{19... | collective-permute-start | bytes 393224 | tf_op jit(solution)/shard_map/ppermute | solution.py:556
  27.5 8.3 %collective-permute-start.4 = (bf16[64,1024]{1,0:T(8,128)(2,1)S(1)}, bf16[64,1024]{1,0:T(8,128)(2,1)S(1)}, u32[]{:S(2)}, u32[]{:S(2)}) collective-permute-start(bf16[64,1024]{1,0:T(8,128)(2,1)S(1)} %get-tuple-element.80), channel_id=1, source_target_pairs={{0,1},{2,3},{4,5},{6,7},{8,9},{10,11},{12,13},{14,15},{16,17},{18,... | collective-permute-start | bytes 393224 | tf_op jit(solution)/shard_map/ppermute | solution.py:567
  27.6 8.2 %collective-permute-start.5 = (bf16[64,1024]{1,0:T(8,128)(2,1)S(1)}, bf16[64,1024]{1,0:T(8,128)(2,1)S(1)}, u32[]{:S(2)}, u32[]{:S(2)}) collective-permute-start(bf16[64,1024]{1,0:T(8,128)(2,1)S(1)} %get-tuple-element.81), channel_id=1, source_target_pairs={{1,2},{3,4},{5,6},{7,8},{9,10},{11,12},{13,14},{15,16},{17,18},{19... | collective-permute-start | bytes 393224 | tf_op jit(solution)/shard_map/ppermute | solution.py:568
  32.6 5.1 %copy-start = (bf16[1024,1024]{1,0:T(8,128)(2,1)S(1)}, bf16[1024,1024]{1,0:T(8,128)(2,1)}, u32[]{:S(2)}) copy-start(bf16[1024,1024]{1,0:T(8,128)(2,1)} %wo_ref.1) | copy-start | bytes 6291460
  32.7 5.1 %copy-start.2 = (bf16[16,32,1024]{2,1,0:T(8,128)(2,1)S(1)}, bf16[16,32,1024]{2,1,0:T(8,128)(2,1)}, u32[]{:S(2)}) copy-start(bf16[16,32,1024]{2,1,0:T(8,128)(2,1)} %param.9) | copy-start | bytes 3145732
  35.9 6.5 %collective-permute-start.6 = (bf16[64,1024]{1,0:T(8,128)(2,1)S(1)}, bf16[64,1024]{1,0:T(8,128)(2,1)S(1)}, u32[]{:S(2)}, u32[]{:S(2)}) collective-permute-start(bf16[64,1024]{1,0:T(8,128)(2,1)S(1)} %get-tuple-element.85), channel_id=1, source_target_pairs={{0,64},{128,192},{64,0},{192,128},{1,65},{129,193},{65,1},{193,129... | collective-permute-start | bytes 393224 | tf_op jit(solution)/shard_map/ppermute | solution.py:575
  37.3 5.1 %collective-permute-start.7 = (bf16[64,1024]{1,0:T(8,128)(2,1)S(1)}, bf16[64,1024]{1,0:T(8,128)(2,1)S(1)}, u32[]{:S(2)}, u32[]{:S(2)}) collective-permute-start(bf16[64,1024]{1,0:T(8,128)(2,1)S(1)} %get-tuple-element.86), channel_id=1, source_target_pairs={{64,128},{192,0},{128,64},{0,192},{65,129},{193,1},{129,65},{1,193... | collective-permute-start | bytes 393224 | tf_op jit(solution)/shard_map/ppermute | solution.py:577
  37.7 2.2 %copy-start.1 = (bf16[1024,1024]{1,0:T(8,128)(2,1)S(1)}, bf16[1024,1024]{1,0:T(8,128)(2,1)}, u32[]{:S(2)}) copy-start(bf16[1024,1024]{1,0:T(8,128)(2,1)} %wq_ref.1) | copy-start | bytes 6291460
  37.7 2.2 %copy-start.3 = (bf16[16,32,1024]{2,1,0:T(8,128)(2,1)S(1)}, bf16[16,32,1024]{2,1,0:T(8,128)(2,1)}, u32[]{:S(2)}) copy-start(bf16[16,32,1024]{2,1,0:T(8,128)(2,1)} %param.17) | copy-start | bytes 3145732

commit v9 on v8

--- a/solution.py
+++ b/solution.py
@@ -178,16 +178,21 @@
     return jnp.where(odd, a, b), jnp.where(odd, b, a)
 
 
-def assemble_kernel(half_ref, got_b, rest_ref, send_a, send_b):
-    pick = select(BLOCK, to_blocks(4))
+def assemble_kernel(got_a, got_b, own_a, own_b, half_ref, rest_ref, send_a, send_b):
     first = is_odd("lat")
+    top = jnp.where(first, got_a[...], own_b[...])
+    bottom = jnp.where(first, own_b[...], got_a[...])
+    rows = jnp.concatenate([top, own_a[...], bottom], axis=0)
+    pick_most, pick_few = select(NODES, to_blocks(12)), select(BLOCK, to_blocks(4))
     for j in range(0, rest_ref.shape[-1], WIDE):
         lanes = slice(j, j + WIDE)
-        rest = mm(pick, got_b[:, lanes], NN).astype(BF)
+        half = mm(pick_most, rows[:, lanes], NN).astype(BF)
+        rest = mm(pick_few, got_b[:, lanes], NN).astype(BF)
+        half_ref[:, lanes] = half
         rest_ref[:, lanes] = rest
 
         def column(i):
-            most = half_ref[i * HALF : (i + 1) * HALF, lanes]
+            most = half[i * HALF : (i + 1) * HALF]
             few = rest[i * HALO : (i + 1) * HALO]
             return jnp.where(
                 first, jnp.concatenate([most, few], axis=0), jnp.concatenate([few, most], axis=0)
@@ -299,17 +304,9 @@
 
 
 def first_kernel(
-    got_a, own_a, own_b, wk_ref, wv_ref, q_ref, da_ref, bias_ref,
-    half_ref, k_ref, v_ref, att_ref, dq_ref, dk_ref, dv_ref, wkt_ref, wvt_ref, *scratch,
+    half_ref, wk_ref, wv_ref, q_ref, da_ref, bias_ref,
+    k_ref, v_ref, att_ref, dq_ref, dk_ref, dv_ref, wkt_ref, wvt_ref, *scratch,
 ):
-    upper = is_odd("lat")
-    top = jnp.where(upper, got_a[...], own_b[...])
-    bottom = jnp.where(upper, own_b[...], got_a[...])
-    rows = jnp.concatenate([top, own_a[...], bottom], axis=0)
-    pick = select(NODES, to_blocks(12))
-    for j in range(0, half_ref.shape[-1], WIDE):
-        lanes = slice(j, j + WIDE)
-        half_ref[:, lanes] = mm(pick, rows[:, lanes], NN).astype(BF)
     for j in range(0, half_ref.shape[-1], WIDE):
         lanes = slice(j, j + WIDE)
         k_ref[:, lanes] = mm(half_ref[...], wk_ref[:, lanes], NN).astype(BF)
@@ -322,7 +319,7 @@
     def load(lanes):
         return k_ref[:, lanes], v_ref[:, lanes]
 
-    tile = jnp.where(upper, 1, 2)
+    tile = jnp.where(is_odd("lat"), 1, 2)
     store = store_all(att_ref, dq_ref, dk_ref, dv_ref)
     attend(tile, load, store, q_ref, da_ref, bias_ref, scratch)
 
@@ -546,14 +543,16 @@
     rows = ((POINTS, width), BF)
     half, half_grad = ((NODES, width), BF), ((NODES, width), F32)
     mid, mid_grad = ((MIDDLE, width), BF), ((2 * BLOCK, width), F32)
-    half_rows, kh, vh, att_first, dq_first, dkh, dvh, wkt, wvt = call(
-        first_kernel, (got_a, send_a, send_b, *common),
-        [half] * 3 + [rows] * 2 + [half_grad] * 2 + [square] * 2,
-        4 * 10**9, PAIR_SCRATCH,
-    )
-    rest, edge_a, edge_b = call(assemble_kernel, (half_rows, got_b), [piece] * 3, 10**8)
+    half_rows, rest, edge_a, edge_b = call(
+        assemble_kernel, (got_a, got_b, send_a, send_b), [half] + [piece] * 3, 10**8
+    )
     edge_a = lax.ppermute(edge_a, "lon", lon_a)
     edge_b = lax.ppermute(edge_b, "lon", lon_b)
+    kh, vh, att_first, dq_first, dkh, dvh, wkt, wvt = call(
+        first_kernel, (half_rows, *common),
+        [half] * 2 + [rows] * 2 + [half_grad] * 2 + [square] * 2,
+        4 * 10**9, PAIR_SCRATCH,
+    )
     k, v, att_near, dq_near, dkn, dvn, rim_dk, rim_dv = call(
         near_kernel, (edge_a, rest, kh, vh, *common),
         [mid] * 2 + [rows] * 2 + [mid_grad] * 2 + [piece] * 2,

time: 43.6 us -> 43.9 us (level)
  waiting for transfers between devices: 0.02 us -> 3.17 us
  starting transfers between devices: 18.2 us -> 15.4 us
    ppermute x2, starting transfers between devices: 13.2 us -> 9.91 us  [local(): edge_b = lax.ppermute(edge_b, 'lon', lon_b)]
    ppermute x2, waiting for transfers between devices: 0.01 us -> 3.15 us  [local(): edge_b = lax.ppermute(edge_b, 'lon', lon_b)]
    ppermute x2, starting transfers between devices: 1.14 us -> 1.6 us  [local(): got_b = lax.ppermute(send_b, 'lat', lat_b)]
  transfers between devices with their start and end apart: 8 -> 8, of which waited for: 0 -> 1; matrix products, arithmetic and copies ran while one was open for 0% -> 0% of each run, Pallas kernels for 43% -> 42%
where the time goes in v9:
time: 43.9 us; the launch traced here: 43.8 us
  Pallas kernels  24.2 us (55%)
  starting transfers between devices  15.4 us (35%)
  waiting for transfers between devices  3.17 us (7%)
  between operations  0.98 us (2%)
    pallas_call x11, Pallas kernels, call(): pl.pallas_call(kernel, in_specs=[placed(i) for i in range(len(inputs))],...  24.2 us
    ppermute x2, starting transfers between devices, local(): edge_b = lax.ppermute(edge_b, 'lon', lon_b)  9.91 us
    ppermute x2, starting transfers between devices, local(): got_a = lax.ppermute(send_a, 'lat', lat_a)  3.67 us
    ppermute x2, waiting for transfers between devices, local(): edge_b = lax.ppermute(edge_b, 'lon', lon_b)  3.15 us
    ppermute x2, starting transfers between devices, local(): got_b = lax.ppermute(send_b, 'lat', lat_b)  1.6 us
  transfers between devices with their start and end apart: 8, of which 1 were waited for; matrix products, arithmetic and copies ran while one was open for 0% of the time, Pallas kernels for 42%

profile of v9, /device:TPU:8, one launch (start us, length us, event | category | flops | bytes accessed | tf_op | source)
XLA Modules:
  0.0 43.8 jit_solution(11290962017833552736)
XLA Ops:
  0.6 1.0 %shard_map.112 = (bf16[64,1024]{1,0:T(8,128)(2,1)S(1)}, bf16[64,1024]{1,0:T(8,128)(2,1)S(1)}) custom-call(bf16[128,1024]{1,0:T(8,128)(2,1)} %bitcast.11), custom_call_target="tpu_custom_call" | custom-call | flops 100000 | bytes 262144 | tf_op jit(solution)/shard_map/pallas_call | solution.py:46
  1.6 2.2 %collective-permute-start = (bf16[64,1024]{1,0:T(8,128)(2,1)S(1)}, bf16[64,1024]{1,0:T(8,128)(2,1)S(1)}, u32[]{:S(2)}, u32[]{:S(2)}) collective-permute-start(bf16[64,1024]{1,0:T(8,128)(2,1)S(1)} %get-tuple-element.45.own_a), channel_id=1, source_target_pairs={{0,64},{128,192},{64,0},{192,128},{1,65},{129,193},{65,1},{193,129... | collective-permute-start | bytes 393224 | tf_op jit(solution)/shard_map/ppermute | solution.py:530
  3.9 0.7 %collective-permute-start.1 = (bf16[64,1024]{1,0:T(8,128)(2,1)S(1)}, bf16[64,1024]{1,0:T(8,128)(2,1)S(1)}, u32[]{:S(2)}, u32[]{:S(2)}) collective-permute-start(bf16[64,1024]{1,0:T(8,128)(2,1)S(1)} %get-tuple-element.46.own_b), channel_id=1, source_target_pairs={{64,128},{192,0},{128,64},{0,192},{65,129},{193,1},{129,65},{1,193... | collective-permute-start | bytes 393224 | tf_op jit(solution)/shard_map/ppermute | solution.py:531
  4.6 4.6 %shard_map.114 = (bf16[4,128,1024]{2,1,0:T(8,128)(2,1)S(1)}, bf16[4,128,1024]{2,1,0:T(8,128)(2,1)S(1)}, f32[4,192,128]{2,1,0:T(8,128)S(1)}, bf16[1024,1024]{1,0:T(8,128)(2,1)S(1)}, bf16[1024,1024]{1,0:T(8,128)(2,1)S(1)}) custom-call(s32[12,16,32]{2,1,0:T(8,128)} %edges_hbm.1, s32[12,16,32]{2,1,0:T(8,128)} %mask_hbm.1, bf16[512,1024]{1,0:T(8,128)(2,1)} %bitcast.6, ...), custom_call_target="tpu_custom_call" | custom-call | flops 2147483648 | bytes 10534912 | tf_op jit(solution)/shard_map/pallas_call | solution.py:46
  9.2 0.0 collective-permute-done.got_a
  9.2 0.0 collective-permute-done.1.got_b
  9.3 0.3 shard_map.113
  9.6 0.1 collective-permute-start.2
  9.7 8.2 %collective-permute-start.3 = (bf16[64,1024]{1,0:T(8,128)(2,1)S(1)}, bf16[64,1024]{1,0:T(8,128)(2,1)S(1)}, u32[]{:S(2)}, u32[]{:S(2)}) collective-permute-start(bf16[64,1024]{1,0:T(8,128)(2,1)S(1)} %get-tuple-element.59), channel_id=1, source_target_pairs={{1,2},{3,4},{5,6},{7,8},{9,10},{11,12},{13,14},{15,16},{17,18},{19... | collective-permute-start | bytes 393224 | tf_op jit(solution)/shard_map/ppermute | solution.py:550
  17.8 3.5 %shard_map.115 = (bf16[192,1024]{1,0:T(8,128)(2,1)S(1)}, bf16[192,1024]{1,0:T(8,128)(2,1)S(1)}, bf16[128,1024]{1,0:T(8,128)(2,1)S(1)}, bf16[128,1024]{1,0:T(8,12...) custom-call(bf16[192,1024]{1,0:T(8,128)(2,1)S(1)} %get-tuple-element, ...), custom_call_target="tpu_custom_call" | custom-call | flops 4000000000 | bytes 7077888 | tf_op jit(solution)/shard_map/pallas_call | solution.py:46
  21.3 0.0 collective-permute-done.2.got_a
  21.4 2.7 %shard_map.116 = (bf16[256,1024]{1,0:T(8,128)(2,1)S(1)}, bf16[256,1024]{1,0:T(8,128)(2,1)S(1)}, bf16[128,1024]{1,0:T(8,128)(2,1)S(1)}, bf16[128,1024]{1,0:T(8,12...) custom-call(bf16[64,1024]{1,0:T(8,128)(2,1)S(1)} %collective-permute, ...), custom_call_target="tpu_custom_call" | custom-call | flops 4000000000 | bytes 7733248 | tf_op jit(solution)/shard_map/pallas_call | solution.py:46
  24.1 0.0 collective-permute-done.3.got_b
  24.1 3.4 %shard_map.117 = (bf16[128,1024]{1,0:T(8,128)(2,1)S(1)}, bf16[128,1024]{1,0:T(8,128)(2,1)S(1)}, f32[128,1024]{1,0:T(8,128)S(1)}, f32[128,1024]{1,0:T(8,128)S(1)}...) custom-call(bf16[64,1024]{1,0:T(8,128)(2,1)S(1)} %collective-permute-done.3.got_b, ...), custom_call_target="tpu_custom_call" | custom-call | flops 4000000000 | bytes 12320768 | tf_op jit(solution)/shard_map/pallas_call | solution.py:46
  27.5 0.1 collective-permute-start.4
  27.6 1.8 %collective-permute-start.5 = (bf16[64,1024]{1,0:T(8,128)(2,1)S(1)}, bf16[64,1024]{1,0:T(8,128)(2,1)S(1)}, u32[]{:S(2)}, u32[]{:S(2)}) collective-permute-start(bf16[64,1024]{1,0:T(8,128)(2,1)S(1)} %get-tuple-element.81), channel_id=1, source_target_pairs={{1,2},{3,4},{5,6},{7,8},{9,10},{11,12},{13,14},{15,16},{17,18},{19... | collective-permute-start | bytes 393224 | tf_op jit(solution)/shard_map/ppermute | solution.py:567
  29.4 0.0 copy-start
  29.4 0.0 copy-start.2
  29.4 3.1 %shard_map.118 = (bf16[128,1024]{1,0:T(8,128)(2,1)S(1)}, bf16[128,1024]{1,0:T(8,128)(2,1)S(1)}, f32[128,1024]{1,0:T(8,128)S(1)}, bf16[128,1024]{1,0:T(8,128)(2,1)S(1)}, bf16[128,1024]{1,0:T(8,128)(2,1)S(1)}) custom-call(bf16[256,1024]{1,0:T(8,128)(2,1)S(1)} %get-tuple-element.60.k_ref, bf16[256,1024]{1,0:T(8,128)(2,1)S(1)} %get-tuple-element.61.v_ref, ...), custom_call_target="tpu_custom_call" | custom-call | flops 4000000000 | bytes 11403264 | tf_op jit(solution)/shard_map/pallas_call | solution.py:46
  32.5 0.0 collective-permute-done.4.got_a
  32.5 3.1 %collective-permute-done.5.got_b = bf16[64,1024]{1,0:T(8,128)(2,1)S(1)} collective-permute-done((bf16[64,1024]{1,0:T(8,128)(2,1)S(1)}, bf16[64,1024]{1,0:T(8,128)(2,1)S(1)}, u32[]{:S(2)}, u32[]{:S(2)}) %collective-permute-start.5) | collective-permute-done | bytes 131104 | tf_op jit(solution)/shard_map/ppermute | solution.py:567
  35.6 0.1 shard_map.121
  35.7 1.4 %collective-permute-start.6 = (bf16[64,1024]{1,0:T(8,128)(2,1)S(1)}, bf16[64,1024]{1,0:T(8,128)(2,1)S(1)}, u32[]{:S(2)}, u32[]{:S(2)}) collective-permute-start(bf16[64,1024]{1,0:T(8,128)(2,1)S(1)} %get-tuple-element.85), channel_id=1, source_target_pairs={{0,64},{128,192},{64,0},{192,128},{1,65},{129,193},{65,1},{193,129... | collective-permute-start | bytes 393224 | tf_op jit(solution)/shard_map/ppermute | solution.py:574
  37.1 0.9 %collective-permute-start.7 = (bf16[64,1024]{1,0:T(8,128)(2,1)S(1)}, bf16[64,1024]{1,0:T(8,128)(2,1)S(1)}, u32[]{:S(2)}, u32[]{:S(2)}) collective-permute-start(bf16[64,1024]{1,0:T(8,128)(2,1)S(1)} %get-tuple-element.86), channel_id=1, source_target_pairs={{64,128},{192,0},{128,64},{0,192},{65,129},{193,1},{129,65},{1,193... | collective-permute-start | bytes 393224 | tf_op jit(solution)/shard_map/ppermute | solution.py:576
  38.0 0.0 copy-done
  38.0 0.0 copy-done.2
  38.0 0.0 copy-start.1
  38.0 0.0 copy-start.3
  38.0 2.1 %shard_map.119 = bf16[512,1024]{1,0:T(8,128)(2,1)} custom-call(bf16[512,1024]{1,0:T(8,128)(2,1)S(1)} %bitcast.7, bf16[128,1024]{1,0:T(8,128)(2,1)S(1)} %get-tuple-element.53.first, bf16[128,1024]{1,0:T(8,128)(2,1)S(1)} %get-tuple-element.58.near, bf16[128,1024]{1,0:T(8,128)(2,1)S(1)} %get-tuple-element.66.far, bf16[128,1024]{1,0:T(8,128)(2,1)S(1)} %get-tuple-element.73.last, ...), custom_call_target="tpu_custom_call" | custom-call | flops 1073741824 | bytes 4194304 | tf_op jit(solution)/shard_map/pallas_call | solution.py:46
  40.2 0.0 copy-done.1
  40.2 0.0 copy-done.3
  40.2 2.4 %shard_map.120 = (bf16[512,1024]{1,0:T(8,128)(2,1)}, f32[128,1024]{1,0:T(8,128)S(1)}) custom-call(bf16[512,1024]{1,0:T(8,128)(2,1)S(1)} %bitcast.9, bf16[128,1024]{1,0:T(8,128)(2,1)S(1)} %get-tuple-element.74.first, bf16[128,1024]{1,0:T(8,128)(2,1)S(1)} %get-tuple-element.75.near, bf16[128,1024]{1,0:T(8,128)(2,1)S(1)} %get-tuple-element.76.far, ...), custom_call_target="tpu_custom_call" | custom-call | flops 1073741824 | bytes 9175040 | tf_op jit(solution)/shard_map/pallas_call | solution.py:46
  42.6 0.0 collective-permute-done.6.got_a
  42.6 0.0 collective-permute-done.7.got_b
  42.6 0.9 %shard_map.122 = bf16[128,1024]{1,0:T(8,128)(2,1)} custom-call(f32[128,1024]{1,0:T(8,128)S(1)} %get-tuple-element.83.own_ref, bf16[64,1024]{1,0:T(8,128)(2,1)S(1)} %collective-permute-done.6.got_a, bf16[64,1024]{1,0:T(8,128)(2,1)S(1)} %collective-permute-done.7.got_b), custom_call_target="tpu_custom_call" | custom-call | flops 1000000 | bytes 786432 | tf_op jit(solution)/shard_map/pallas_call | solution.py:46
Async XLA Ops:
  1.6 7.6 %collective-permute-start = (bf16[64,1024]{1,0:T(8,128)(2,1)S(1)}, bf16[64,1024]{1,0:T(8,128)(2,1)S(1)}, u32[]{:S(2)}, u32[]{:S(2)}) collective-permute-start(bf16[64,1024]{1,0:T(8,128)(2,1)S(1)} %get-tuple-element.45.own_a), channel_id=1, source_target_pairs={{0,64},{128,192},{64,0},{192,128},{1,65},{129,193},{65,1},{193,129... | collective-permute-start | bytes 393224 | tf_op jit(solution)/shard_map/ppermute | solution.py:530
  3.9 5.4 %collective-permute-start.1 = (bf16[64,1024]{1,0:T(8,128)(2,1)S(1)}, bf16[64,1024]{1,0:T(8,128)(2,1)S(1)}, u32[]{:S(2)}, u32[]{:S(2)}) collective-permute-start(bf16[64,1024]{1,0:T(8,128)(2,1)S(1)} %get-tuple-element.46.own_b), channel_id=1, source_target_pairs={{64,128},{192,0},{128,64},{0,192},{65,129},{193,1},{129,65},{1,193... | collective-permute-start | bytes 393224 | tf_op jit(solution)/shard_map/ppermute | solution.py:531
  9.6 11.8 %collective-permute-start.2 = (bf16[64,1024]{1,0:T(8,128)(2,1)S(1)}, bf16[64,1024]{1,0:T(8,128)(2,1)S(1)}, u32[]{:S(2)}, u32[]{:S(2)}) collective-permute-start(bf16[64,1024]{1,0:T(8,128)(2,1)S(1)} %get-tuple-element.54), channel_id=1, source_target_pairs={{0,1},{2,3},{4,5},{6,7},{8,9},{10,11},{12,13},{14,15},{16,17},{18,... | collective-permute-start | bytes 393224 | tf_op jit(solution)/shard_map/ppermute | solution.py:549
  9.7 14.4 %collective-permute-start.3 = (bf16[64,1024]{1,0:T(8,128)(2,1)S(1)}, bf16[64,1024]{1,0:T(8,128)(2,1)S(1)}, u32[]{:S(2)}, u32[]{:S(2)}) collective-permute-start(bf16[64,1024]{1,0:T(8,128)(2,1)S(1)} %get-tuple-element.59), channel_id=1, source_target_pairs={{1,2},{3,4},{5,6},{7,8},{9,10},{11,12},{13,14},{15,16},{17,18},{19... | collective-permute-start | bytes 393224 | tf_op jit(solution)/shard_map/ppermute | solution.py:550
  27.5 5.0 %collective-permute-start.4 = (bf16[64,1024]{1,0:T(8,128)(2,1)S(1)}, bf16[64,1024]{1,0:T(8,128)(2,1)S(1)}, u32[]{:S(2)}, u32[]{:S(2)}) collective-permute-start(bf16[64,1024]{1,0:T(8,128)(2,1)S(1)} %get-tuple-element.80), channel_id=1, source_target_pairs={{0,1},{2,3},{4,5},{6,7},{8,9},{10,11},{12,13},{14,15},{16,17},{18,... | collective-permute-start | bytes 393224 | tf_op jit(solution)/shard_map/ppermute | solution.py:566
  27.6 8.0 %collective-permute-start.5 = (bf16[64,1024]{1,0:T(8,128)(2,1)S(1)}, bf16[64,1024]{1,0:T(8,128)(2,1)S(1)}, u32[]{:S(2)}, u32[]{:S(2)}) collective-permute-start(bf16[64,1024]{1,0:T(8,128)(2,1)S(1)} %get-tuple-element.81), channel_id=1, source_target_pairs={{1,2},{3,4},{5,6},{7,8},{9,10},{11,12},{13,14},{15,16},{17,18},{19... | collective-permute-start | bytes 393224 | tf_op jit(solution)/shard_map/ppermute | solution.py:567
  29.4 8.7 %copy-start = (bf16[1024,1024]{1,0:T(8,128)(2,1)S(1)}, bf16[1024,1024]{1,0:T(8,128)(2,1)}, u32[]{:S(2)}) copy-start(bf16[1024,1024]{1,0:T(8,128)(2,1)} %wo_ref.1) | copy-start | bytes 6291460
  29.4 8.7 %copy-start.2 = (bf16[16,32,1024]{2,1,0:T(8,128)(2,1)S(1)}, bf16[16,32,1024]{2,1,0:T(8,128)(2,1)}, u32[]{:S(2)}) copy-start(bf16[16,32,1024]{2,1,0:T(8,128)(2,1)} %param.9) | copy-start | bytes 3145732
  35.7 6.9 %collective-permute-start.6 = (bf16[64,1024]{1,0:T(8,128)(2,1)S(1)}, bf16[64,1024]{1,0:T(8,128)(2,1)S(1)}, u32[]{:S(2)}, u32[]{:S(2)}) collective-permute-start(bf16[64,1024]{1,0:T(8,128)(2,1)S(1)} %get-tuple-element.85), channel_id=1, source_target_pairs={{0,64},{128,192},{64,0},{192,128},{1,65},{129,193},{65,1},{193,129... | collective-permute-start | bytes 393224 | tf_op jit(solution)/shard_map/ppermute | solution.py:574
  37.1 5.5 %collective-permute-start.7 = (bf16[64,1024]{1,0:T(8,128)(2,1)S(1)}, bf16[64,1024]{1,0:T(8,128)(2,1)S(1)}, u32[]{:S(2)}, u32[]{:S(2)}) collective-permute-start(bf16[64,1024]{1,0:T(8,128)(2,1)S(1)} %get-tuple-element.86), channel_id=1, source_target_pairs={{64,128},{192,0},{128,64},{0,192},{65,129},{193,1},{129,65},{1,193... | collective-permute-start | bytes 393224 | tf_op jit(solution)/shard_map/ppermute | solution.py:576
  38.0 2.2 %copy-start.1 = (bf16[1024,1024]{1,0:T(8,128)(2,1)S(1)}, bf16[1024,1024]{1,0:T(8,128)(2,1)}, u32[]{:S(2)}) copy-start(bf16[1024,1024]{1,0:T(8,128)(2,1)} %wq_ref.1) | copy-start | bytes 6291460
  38.0 2.2 %copy-start.3 = (bf16[16,32,1024]{2,1,0:T(8,128)(2,1)S(1)}, bf16[16,32,1024]{2,1,0:T(8,128)(2,1)}, u32[]{:S(2)}) copy-start(bf16[16,32,1024]{2,1,0:T(8,128)(2,1)} %param.17) | copy-start | bytes 3145732

commit v10 on v9

--- a/solution.py
+++ b/solution.py
@@ -252,10 +252,14 @@
         st[tall, :] = ds
 
 
-def gather_grads(keys, values, bufs):
+def point_side(keys, values, pt, st):
+    att = mm(pt[...], spread_group(values), TN).astype(BF)
+    return att, mm(st[...], spread_group(keys), TN).astype(BF)
+
+
+def gather_grads(keys, values, bufs, late):
     _, _, qs_ref, gs_ref, pw, sw, pt, st = bufs
-    att = mm(pt[...], spread_group(values), TN).astype(BF)
-    dq = mm(st[...], spread_group(keys), TN).astype(BF)
+    att, dq = (None, None) if late else point_side(keys, values, pt, st)
     dk, dv = [], []
     for i in range(GROUP // 2):
         _, at = pair_lanes(i)
@@ -273,23 +277,28 @@
 PAIR_SCRATCH = ITEM_SCRATCH * 2
 
 
-def attend(tile, load, store, q_ref, da_ref, bias_ref, scratch):
+def attend(tile, load, store, q_ref, da_ref, bias_ref, scratch, late=None):
     n = len(ITEM_SCRATCH)
-    bufs = (scratch[:n], scratch[n:])
+    halves = (scratch[:n], scratch[n:])
+
+    def bufs(k):
+        half = halves[k % 2]
+        return half if late is None else (*half[:-2], late[0].at[k], late[1].at[k])
+
     items = [slice(j, j + WIDE) for j in range(0, HEADS * HEAD, WIDE)]
 
     def do_score(k):
         lanes = items[k]
-        score(*load(lanes), q_ref[tile, :, lanes], da_ref[tile, :, lanes], bufs[k % 2])
+        score(*load(lanes), q_ref[tile, :, lanes], da_ref[tile, :, lanes], bufs(k))
 
     def do_grads(k):
-        store(items[k], *gather_grads(*load(items[k]), bufs[k % 2]))
+        store(items[k], *gather_grads(*load(items[k]), bufs(k), late is not None))
 
     do_score(0)
     for k in range(len(items)):
         if k > 0:
             do_grads(k - 1)
-        soften(bias_ref[tile], bufs[k % 2])
+        soften(bias_ref[tile], bufs(k))
         if k + 1 < len(items):
             do_score(k + 1)
     do_grads(len(items) - 1)
@@ -324,8 +333,7 @@
     attend(tile, load, store, q_ref, da_ref, bias_ref, scratch)
 
 
-def edge_tile(left, k_ref, v_ref, kr, vr, outs, q_ref, da_ref, bias_ref, scratch):
-    att_ref, dq_ref, dk_ref, dv_ref, dkr, dvr = outs
+def edge_load(left, k_ref, v_ref, kr, vr):
     start = pl.multiple_of(jnp.where(left, 0, 2 * BLOCK), 2 * BLOCK)
 
     def load(lanes):
@@ -334,14 +342,22 @@
 
         return one(kr, k_ref), one(vr, v_ref)
 
+    return load
+
+
+def edge_tile(left, k_ref, v_ref, kr, vr, outs, q_ref, da_ref, bias_ref, scratch, late=None):
+    att_ref, dq_ref, dk_ref, dv_ref, dkr, dvr = outs
+    load = edge_load(left, k_ref, v_ref, kr, vr)
+
     def store(lanes, att, dq, dk, dv):
-        att_ref[:, lanes] = att
-        dq_ref[:, lanes] = dq
+        if late is None:
+            att_ref[:, lanes] = att
+            dq_ref[:, lanes] = dq
         for grad, rim, out in ((dk, dkr, dk_ref), (dv, dvr, dv_ref)):
             rim[:, lanes] = (grad[:BLOCK] * (1.0 / SCALE)).astype(BF)
             out[:, lanes] = grad[BLOCK:]
 
-    attend(jnp.where(left, 0, 3), load, store, q_ref, da_ref, bias_ref, scratch)
+    attend(jnp.where(left, 0, 3), load, store, q_ref, da_ref, bias_ref, scratch, late)
 
 
 def near_kernel(
@@ -371,16 +387,17 @@
 def far_kernel(
     got_b, k_ref, v_ref, wk_ref, wv_ref, q_ref, da_ref, bias_ref, near_dkr, near_dvr,
     wkt_ref, wvt_ref,
-    att_ref, dq_ref, dk_ref, dv_ref, send_a, send_b,
-    kr, vr, dkr, dvr, *scratch,
+    pt_ref, st_ref, kr, vr, dk_ref, dv_ref, send_a, send_b,
+    dkr, dvr, *scratch,
 ):
     for j in range(0, kr.shape[-1], WIDE):
         lanes = slice(j, j + WIDE)
         kr[:, lanes] = mm(got_b[...], wk_ref[:, lanes], NN).astype(BF)
         vr[:, lanes] = mm(got_b[...], wv_ref[:, lanes], NN).astype(BF)
-    outs = (att_ref, dq_ref, dk_ref, dv_ref, dkr, dvr)
+    outs = (None, None, dk_ref, dv_ref, dkr, dvr)
     left = lax.axis_index("lon") % 2 == 0
-    edge_tile(left, k_ref, v_ref, kr, vr, outs, q_ref, da_ref, bias_ref, scratch)
+    late = (pt_ref, st_ref)
+    edge_tile(left, k_ref, v_ref, kr, vr, outs, q_ref, da_ref, bias_ref, scratch, late)
     dk = jnp.concatenate([near_dkr[...], dkr[...]], axis=0)
     dv = jnp.concatenate([near_dvr[...], dvr[...]], axis=0)
     for j in range(0, kr.shape[-1], WIDE):
@@ -392,10 +409,14 @@
 
 def last_kernel(
     k_ref, v_ref, wkt_ref, wvt_ref, q_ref, da_ref, bias_ref,
-    dkh_ref, dvh_ref, dkn_ref, dvn_ref, dkf_ref, dvf_ref,
-    att_ref, dq_ref, part_ref, dko_ref, dvo_ref,
+    dkh_ref, dvh_ref, dkn_ref, dvn_ref, dkf_ref, dvf_ref, pt_ref, st_ref, kr, vr,
+    att_ref, dq_ref, att_far, dq_far, part_ref, dko_ref, dvo_ref,
     dkr, dvr, *scratch,
 ):
+    far = edge_load(lax.axis_index("lon") % 2 == 0, k_ref, v_ref, kr, vr)
+    for g in range(HEADS // GROUP):
+        lanes = slice(g * WIDE, (g + 1) * WIDE)
+        att_far[:, lanes], dq_far[:, lanes] = point_side(*far(lanes), pt_ref.at[g], st_ref.at[g])
     upper_done = is_odd("lat")
     offset = jnp.where(upper_done, HALO, 0)
 
@@ -558,16 +579,17 @@
         [mid] * 2 + [rows] * 2 + [mid_grad] * 2 + [piece] * 2,
         4 * 10**9, (pltpu.VMEM((BLOCK, width), BF),) * 2 + PAIR_SCRATCH,
     )
-    att_far, dq_far, dkf, dvf, edge_a, edge_b = call(
+    kept = ((HEADS // GROUP, GROUP * NODES, POINTS), BF)
+    pt, st, kr, vr, dkf, dvf, edge_a, edge_b = call(
         far_kernel, (edge_b, k, v, *common, rim_dk, rim_dv, wkt, wvt),
-        [rows] * 2 + [mid_grad] * 2 + [piece] * 2,
-        4 * 10**9, (pltpu.VMEM((BLOCK, width), BF),) * 4 + PAIR_SCRATCH,
+        [kept] * 2 + [piece] * 2 + [mid_grad] * 2 + [piece] * 2,
+        4 * 10**9, (pltpu.VMEM((BLOCK, width), BF),) * 2 + PAIR_SCRATCH,
     )
     edge_a = lax.ppermute(edge_a, "lon", lon_a)
     edge_b = lax.ppermute(edge_b, "lon", lon_b)
-    att_last, dq_last, part, dk_own, dv_own = call(
-        last_kernel, (k, v, wkt, wvt, q, da, bias, dkh, dvh, dkn, dvn, dkf, dvf),
-        [rows] * 2 + [mid_grad] + [((2 * BLOCK, width), BF)] * 2,
+    att_last, dq_last, att_far, dq_far, part, dk_own, dv_own = call(
+        last_kernel, (k, v, wkt, wvt, q, da, bias, dkh, dvh, dkn, dvn, dkf, dvf, pt, st, kr, vr),
+        [rows] * 4 + [mid_grad] + [((2 * BLOCK, width), BF)] * 2,
         4 * 10**9, (pltpu.VMEM((2 * BLOCK, width), BF),) * 2 + PAIR_SCRATCH,
     )
     send_a, send_b = call(merge_kernel, (part, edge_a, edge_b), [piece, piece], 10**8)

time: 43.9 us -> 43.4 us (0.989)
  transfers between devices with their start and end apart: 8 -> 8, of which waited for: 1 -> 1; matrix products, arithmetic and copies ran while one was open for 0% -> 0% of each run, Pallas kernels for 42% -> 44%
where the time goes in v10:
time: 43.4 us; the launch traced here: 43.3 us
  Pallas kernels  24.2 us (56%)
  starting transfers between devices  15.4 us (35%)
  waiting for transfers between devices  2.75 us (6%)
  between operations  0.98 us (2%)
    pallas_call x11, Pallas kernels, call(): pl.pallas_call(kernel, in_specs=[placed(i) for i in range(len(inputs))],...  24.2 us
    ppermute x2, starting transfers between devices, local(): edge_b = lax.ppermute(edge_b, 'lon', lon_b)  9.9 us
    ppermute x2, starting transfers between devices, local(): got_a = lax.ppermute(send_a, 'lat', lat_a)  3.68 us
    ppermute x2, waiting for transfers between devices, local(): edge_b = lax.ppermute(edge_b, 'lon', lon_b)  2.74 us
    ppermute x2, starting transfers between devices, local(): got_b = lax.ppermute(send_b, 'lat', lat_b)  1.6 us
  transfers between devices with their start and end apart: 8, of which 1 were waited for; matrix products, arithmetic and copies ran while one was open for 0% of the time, Pallas kernels for 44%

profile of v10, /device:TPU:8, one launch (start us, length us, event | category | flops | bytes accessed | tf_op | source)
XLA Modules:
  0.0 43.3 jit_solution(4177767797440795024)
XLA Ops:
  0.6 1.0 %shard_map.112 = (bf16[64,1024]{1,0:T(8,128)(2,1)S(1)}, bf16[64,1024]{1,0:T(8,128)(2,1)S(1)}) custom-call(bf16[128,1024]{1,0:T(8,128)(2,1)} %bitcast.11), custom_call_target="tpu_custom_call" | custom-call | flops 100000 | bytes 262144 | tf_op jit(solution)/shard_map/pallas_call | solution.py:46
  1.6 2.2 %collective-permute-start = (bf16[64,1024]{1,0:T(8,128)(2,1)S(1)}, bf16[64,1024]{1,0:T(8,128)(2,1)S(1)}, u32[]{:S(2)}, u32[]{:S(2)}) collective-permute-start(bf16[64,1024]{1,0:T(8,128)(2,1)S(1)} %get-tuple-element.49.own_a), channel_id=1, source_target_pairs={{0,64},{128,192},{64,0},{192,128},{1,65},{129,193},{65,1},{193,129... | collective-permute-start | bytes 393224 | tf_op jit(solution)/shard_map/ppermute | solution.py:551
  3.9 0.7 %collective-permute-start.1 = (bf16[64,1024]{1,0:T(8,128)(2,1)S(1)}, bf16[64,1024]{1,0:T(8,128)(2,1)S(1)}, u32[]{:S(2)}, u32[]{:S(2)}) collective-permute-start(bf16[64,1024]{1,0:T(8,128)(2,1)S(1)} %get-tuple-element.50.own_b), channel_id=1, source_target_pairs={{64,128},{192,0},{128,64},{0,192},{65,129},{193,1},{129,65},{1,193... | collective-permute-start | bytes 393224 | tf_op jit(solution)/shard_map/ppermute | solution.py:552
  4.6 4.6 %shard_map.114 = (bf16[4,128,1024]{2,1,0:T(8,128)(2,1)S(1)}, bf16[4,128,1024]{2,1,0:T(8,128)(2,1)S(1)}, f32[4,192,128]{2,1,0:T(8,128)S(1)}, bf16[1024,1024]{1,0:T(8,128)(2,1)S(1)}, bf16[1024,1024]{1,0:T(8,128)(2,1)S(1)}) custom-call(s32[12,16,32]{2,1,0:T(8,128)} %edges_hbm.1, s32[12,16,32]{2,1,0:T(8,128)} %mask_hbm.1, bf16[512,1024]{1,0:T(8,128)(2,1)} %bitcast.6, ...), custom_call_target="tpu_custom_call" | custom-call | flops 2147483648 | bytes 10534912 | tf_op jit(solution)/shard_map/pallas_call | solution.py:46
  9.2 0.0 collective-permute-done.got_a
  9.2 0.0 collective-permute-done.1.got_b
  9.3 0.3 shard_map.113
  9.6 0.1 collective-permute-start.2
  9.7 8.2 %collective-permute-start.3 = (bf16[64,1024]{1,0:T(8,128)(2,1)S(1)}, bf16[64,1024]{1,0:T(8,128)(2,1)S(1)}, u32[]{:S(2)}, u32[]{:S(2)}) collective-permute-start(bf16[64,1024]{1,0:T(8,128)(2,1)S(1)} %get-tuple-element.71), channel_id=1, source_target_pairs={{1,2},{3,4},{5,6},{7,8},{9,10},{11,12},{13,14},{15,16},{17,18},{19... | collective-permute-start | bytes 393224 | tf_op jit(solution)/shard_map/ppermute | solution.py:571
  17.8 3.5 %shard_map.115 = (bf16[192,1024]{1,0:T(8,128)(2,1)S(1)}, bf16[192,1024]{1,0:T(8,128)(2,1)S(1)}, bf16[128,1024]{1,0:T(8,128)(2,1)S(1)}, bf16[128,1024]{1,0:T(8,12...) custom-call(bf16[192,1024]{1,0:T(8,128)(2,1)S(1)} %get-tuple-element, ...), custom_call_target="tpu_custom_call" | custom-call | flops 4000000000 | bytes 7077888 | tf_op jit(solution)/shard_map/pallas_call | solution.py:46
  21.3 0.0 collective-permute-done.2.got_a
  21.4 2.7 %shard_map.116 = (bf16[256,1024]{1,0:T(8,128)(2,1)S(1)}, bf16[256,1024]{1,0:T(8,128)(2,1)S(1)}, bf16[128,1024]{1,0:T(8,128)(2,1)S(1)}, bf16[128,1024]{1,0:T(8,12...) custom-call(bf16[64,1024]{1,0:T(8,128)(2,1)S(1)} %collective-permute, ...), custom_call_target="tpu_custom_call" | custom-call | flops 4000000000 | bytes 7733248 | tf_op jit(solution)/shard_map/pallas_call | solution.py:46
  24.1 0.0 collective-permute-done.3.got_b
  24.1 2.9 %shard_map.117 = (bf16[4,768,128]{2,1,0:T(8,128)(2,1)S(1)}, bf16[4,768,128]{2,1,0:T(8,128)(2,1)S(1)}, bf16[64,1024]{1,0:T(8,128)(2,1)S(1)}, bf16[64,1024]{1,0:T(...) custom-call(bf16[64,1024]{1,0:T(8,128)(2,1)S(1)} %collective-permute, ...), custom_call_target="tpu_custom_call" | custom-call | flops 4000000000 | bytes 12320768 | tf_op jit(solution)/shard_map/pallas_call | solution.py:46
  27.0 0.1 collective-permute-start.4
  27.1 1.7 %collective-permute-start.5 = (bf16[64,1024]{1,0:T(8,128)(2,1)S(1)}, bf16[64,1024]{1,0:T(8,128)(2,1)S(1)}, u32[]{:S(2)}, u32[]{:S(2)}) collective-permute-start(bf16[64,1024]{1,0:T(8,128)(2,1)S(1)} %get-tuple-element.89), channel_id=1, source_target_pairs={{1,2},{3,4},{5,6},{7,8},{9,10},{11,12},{13,14},{15,16},{17,18},{19... | collective-permute-start | bytes 393224 | tf_op jit(solution)/shard_map/ppermute | solution.py:589
  28.9 0.0 copy-start
  28.9 0.0 copy-start.2
  28.9 3.5 %shard_map.118 = (bf16[128,1024]{1,0:T(8,128)(2,1)S(1)}, bf16[128,1024]{1,0:T(8,128)(2,1)S(1)}, bf16[128,1024]{1,0:T(8,128)(2,1)S(1)}, bf16[128,1024]{1,0:T(8,12...) custom-call(bf16[256,1024]{1,0:T(8,128)(2,1)S(1)} %get-tuple-element.63.k_ref, ...), custom_call_target="tpu_custom_call" | custom-call | flops 4000000000 | bytes 13238272 | tf_op jit(solution)/shard_map/pallas_call | solution.py:46
  32.4 0.0 collective-permute-done.4.got_a
  32.4 2.7 %collective-permute-done.5.got_b = bf16[64,1024]{1,0:T(8,128)(2,1)S(1)} collective-permute-done((bf16[64,1024]{1,0:T(8,128)(2,1)S(1)}, bf16[64,1024]{1,0:T(8,128)(2,1)S(1)}, u32[]{:S(2)}, u32[]{:S(2)}) %collective-permute-start.5) | collective-permute-done | bytes 131104 | tf_op jit(solution)/shard_map/ppermute | solution.py:589
  35.2 0.1 shard_map.121
  35.2 1.4 %collective-permute-start.6 = (bf16[64,1024]{1,0:T(8,128)(2,1)S(1)}, bf16[64,1024]{1,0:T(8,128)(2,1)S(1)}, u32[]{:S(2)}, u32[]{:S(2)}) collective-permute-start(bf16[64,1024]{1,0:T(8,128)(2,1)S(1)} %get-tuple-element.93), channel_id=1, source_target_pairs={{0,64},{128,192},{64,0},{192,128},{1,65},{129,193},{65,1},{193,129... | collective-permute-start | bytes 393224 | tf_op jit(solution)/shard_map/ppermute | solution.py:596
  36.7 0.9 %collective-permute-start.7 = (bf16[64,1024]{1,0:T(8,128)(2,1)S(1)}, bf16[64,1024]{1,0:T(8,128)(2,1)S(1)}, u32[]{:S(2)}, u32[]{:S(2)}) collective-permute-start(bf16[64,1024]{1,0:T(8,128)(2,1)S(1)} %get-tuple-element.94), channel_id=1, source_target_pairs={{64,128},{192,0},{128,64},{0,192},{65,129},{193,1},{129,65},{1,193... | collective-permute-start | bytes 393224 | tf_op jit(solution)/shard_map/ppermute | solution.py:598
  37.6 0.0 copy-done
  37.6 0.0 copy-done.2
  37.6 0.0 copy-start.1
  37.6 0.0 copy-start.3
  37.6 2.1 %shard_map.119 = bf16[512,1024]{1,0:T(8,128)(2,1)} custom-call(bf16[512,1024]{1,0:T(8,128)(2,1)S(1)} %bitcast.7, bf16[128,1024]{1,0:T(8,128)(2,1)S(1)} %get-tuple-element.57.first, bf16[128,1024]{1,0:T(8,128)(2,1)S(1)} %get-tuple-element.62.near, bf16[128,1024]{1,0:T(8,128)(2,1)S(1)} %get-tuple-element.80.far, bf16[128,1024]{1,0:T(8,128)(2,1)S(1)} %get-tuple-element.81.last, ...), custom_call_target="tpu_custom_call" | custom-call | flops 1073741824 | bytes 4194304 | tf_op jit(solution)/shard_map/pallas_call | solution.py:46
  39.7 0.0 copy-done.1
  39.7 0.0 copy-done.3
  39.7 2.4 %shard_map.120 = (bf16[512,1024]{1,0:T(8,128)(2,1)}, f32[128,1024]{1,0:T(8,128)S(1)}) custom-call(bf16[512,1024]{1,0:T(8,128)(2,1)S(1)} %bitcast.9, bf16[128,1024]{1,0:T(8,128)(2,1)S(1)} %get-tuple-element.82.first, bf16[128,1024]{1,0:T(8,128)(2,1)S(1)} %get-tuple-element.83.near, bf16[128,1024]{1,0:T(8,128)(2,1)S(1)} %get-tuple-element.84.far, ...), custom_call_target="tpu_custom_call" | custom-call | flops 1073741824 | bytes 9175040 | tf_op jit(solution)/shard_map/pallas_call | solution.py:46
  42.2 0.0 collective-permute-done.6.got_a
  42.2 0.0 collective-permute-done.7.got_b
  42.2 0.9 %shard_map.122 = bf16[128,1024]{1,0:T(8,128)(2,1)} custom-call(f32[128,1024]{1,0:T(8,128)S(1)} %get-tuple-element.91.own_ref, bf16[64,1024]{1,0:T(8,128)(2,1)S(1)} %collective-permute-done.6.got_a, bf16[64,1024]{1,0:T(8,128)(2,1)S(1)} %collective-permute-done.7.got_b), custom_call_target="tpu_custom_call" | custom-call | flops 1000000 | bytes 786432 | tf_op jit(solution)/shard_map/pallas_call | solution.py:46
Async XLA Ops:
  1.6 7.6 %collective-permute-start = (bf16[64,1024]{1,0:T(8,128)(2,1)S(1)}, bf16[64,1024]{1,0:T(8,128)(2,1)S(1)}, u32[]{:S(2)}, u32[]{:S(2)}) collective-permute-start(bf16[64,1024]{1,0:T(8,128)(2,1)S(1)} %get-tuple-element.49.own_a), channel_id=1, source_target_pairs={{0,64},{128,192},{64,0},{192,128},{1,65},{129,193},{65,1},{193,129... | collective-permute-start | bytes 393224 | tf_op jit(solution)/shard_map/ppermute | solution.py:551
  3.9 5.4 %collective-permute-start.1 = (bf16[64,1024]{1,0:T(8,128)(2,1)S(1)}, bf16[64,1024]{1,0:T(8,128)(2,1)S(1)}, u32[]{:S(2)}, u32[]{:S(2)}) collective-permute-start(bf16[64,1024]{1,0:T(8,128)(2,1)S(1)} %get-tuple-element.50.own_b), channel_id=1, source_target_pairs={{64,128},{192,0},{128,64},{0,192},{65,129},{193,1},{129,65},{1,193... | collective-permute-start | bytes 393224 | tf_op jit(solution)/shard_map/ppermute | solution.py:552
  9.6 11.8 %collective-permute-start.2 = (bf16[64,1024]{1,0:T(8,128)(2,1)S(1)}, bf16[64,1024]{1,0:T(8,128)(2,1)S(1)}, u32[]{:S(2)}, u32[]{:S(2)}) collective-permute-start(bf16[64,1024]{1,0:T(8,128)(2,1)S(1)} %get-tuple-element.58), channel_id=1, source_target_pairs={{0,1},{2,3},{4,5},{6,7},{8,9},{10,11},{12,13},{14,15},{16,17},{18,... | collective-permute-start | bytes 393224 | tf_op jit(solution)/shard_map/ppermute | solution.py:570
  9.7 14.4 %collective-permute-start.3 = (bf16[64,1024]{1,0:T(8,128)(2,1)S(1)}, bf16[64,1024]{1,0:T(8,128)(2,1)S(1)}, u32[]{:S(2)}, u32[]{:S(2)}) collective-permute-start(bf16[64,1024]{1,0:T(8,128)(2,1)S(1)} %get-tuple-element.71), channel_id=1, source_target_pairs={{1,2},{3,4},{5,6},{7,8},{9,10},{11,12},{13,14},{15,16},{17,18},{19... | collective-permute-start | bytes 393224 | tf_op jit(solution)/shard_map/ppermute | solution.py:571
  27.0 5.4 %collective-permute-start.4 = (bf16[64,1024]{1,0:T(8,128)(2,1)S(1)}, bf16[64,1024]{1,0:T(8,128)(2,1)S(1)}, u32[]{:S(2)}, u32[]{:S(2)}) collective-permute-start(bf16[64,1024]{1,0:T(8,128)(2,1)S(1)} %get-tuple-element.88), channel_id=1, source_target_pairs={{0,1},{2,3},{4,5},{6,7},{8,9},{10,11},{12,13},{14,15},{16,17},{18,... | collective-permute-start | bytes 393224 | tf_op jit(solution)/shard_map/ppermute | solution.py:588
  27.1 8.0 %collective-permute-start.5 = (bf16[64,1024]{1,0:T(8,128)(2,1)S(1)}, bf16[64,1024]{1,0:T(8,128)(2,1)S(1)}, u32[]{:S(2)}, u32[]{:S(2)}) collective-permute-start(bf16[64,1024]{1,0:T(8,128)(2,1)S(1)} %get-tuple-element.89), channel_id=1, source_target_pairs={{1,2},{3,4},{5,6},{7,8},{9,10},{11,12},{13,14},{15,16},{17,18},{19... | collective-permute-start | bytes 393224 | tf_op jit(solution)/shard_map/ppermute | solution.py:589
  28.9 8.7 %copy-start = (bf16[1024,1024]{1,0:T(8,128)(2,1)S(1)}, bf16[1024,1024]{1,0:T(8,128)(2,1)}, u32[]{:S(2)}) copy-start(bf16[1024,1024]{1,0:T(8,128)(2,1)} %wo_ref.1) | copy-start | bytes 6291460
  28.9 8.7 %copy-start.2 = (bf16[16,32,1024]{2,1,0:T(8,128)(2,1)S(1)}, bf16[16,32,1024]{2,1,0:T(8,128)(2,1)}, u32[]{:S(2)}) copy-start(bf16[16,32,1024]{2,1,0:T(8,128)(2,1)} %param.9) | copy-start | bytes 3145732
  35.2 6.9 %collective-permute-start.6 = (bf16[64,1024]{1,0:T(8,128)(2,1)S(1)}, bf16[64,1024]{1,0:T(8,128)(2,1)S(1)}, u32[]{:S(2)}, u32[]{:S(2)}) collective-permute-start(bf16[64,1024]{1,0:T(8,128)(2,1)S(1)} %get-tuple-element.93), channel_id=1, source_target_pairs={{0,64},{128,192},{64,0},{192,128},{1,65},{129,193},{65,1},{193,129... | collective-permute-start | bytes 393224 | tf_op jit(solution)/shard_map/ppermute | solution.py:596
  36.7 5.5 %collective-permute-start.7 = (bf16[64,1024]{1,0:T(8,128)(2,1)S(1)}, bf16[64,1024]{1,0:T(8,128)(2,1)S(1)}, u32[]{:S(2)}, u32[]{:S(2)}) collective-permute-start(bf16[64,1024]{1,0:T(8,128)(2,1)S(1)} %get-tuple-element.94), channel_id=1, source_target_pairs={{64,128},{192,0},{128,64},{0,192},{65,129},{193,1},{129,65},{1,193... | collective-permute-start | bytes 393224 | tf_op jit(solution)/shard_map/ppermute | solution.py:598
  37.6 2.2 %copy-start.1 = (bf16[1024,1024]{1,0:T(8,128)(2,1)S(1)}, bf16[1024,1024]{1,0:T(8,128)(2,1)}, u32[]{:S(2)}) copy-start(bf16[1024,1024]{1,0:T(8,128)(2,1)} %wq_ref.1) | copy-start | bytes 6291460
  37.6 2.2 %copy-start.3 = (bf16[16,32,1024]{2,1,0:T(8,128)(2,1)S(1)}, bf16[16,32,1024]{2,1,0:T(8,128)(2,1)}, u32[]{:S(2)}) copy-start(bf16[16,32,1024]{2,1,0:T(8,128)(2,1)} %param.17) | copy-start | bytes 3145732
